TPU v7x, 256 devices: a whole 4x4x8 slice. The times are simulated.
256 devices in a mesh: row: 32 (over x, z), col: 8 (over y, core).
Axes of the slice: x: 4, y: 4, z: 8, core: 2. Of those that a mesh axis runs over, the one named last changes fastest.
Arguments:
- covariance: float32 [16384, 16384], P('row', 'col'), as said below
- first_jacobian: bfloat16 [32, 16384], P(None, ('row', 'col')), may hold values from -0.046875 to 0.046875
- second_jacobian: bfloat16 [32, 16384], P(None, ('row', 'col')), may hold values from -0.046875 to 0.046875
- first_residuals: float32 [32], replicated, may hold values from -96 to 96
- second_residuals: float32 [32], replicated, may hold values from -48 to 48
Outputs:
- covariance_out: float32 [16384, 16384], P('row', 'col')
- increment: float32 [16384], P(('row', 'col'))
Inputs may be any that keep to these rules, and one draw needn't show every extreme that they name: covariance is symmetric and positive definite, its diagonal between 3 and 6.
All inputs are finite; a program needn't handle non-finite values.
Results may differ from a plain program's by a relative error of at most 0.0003.
Values may be sent and summed in bfloat16 or wider, within the bound.
No kernel may reach another device: no remote copies, remote signals or barrier semaphores. Data moves between devices by JAX's collectives and lax.ppermute only.
A program may use at most 64 MiB of HBM per device.

v0:
```python
import jax
import jax.numpy as jnp
from jax import lax
from jax.sharding import PartitionSpec as P

lam_start = 0.98
forget_rate = 0.9987


def sent_to_all(array, axis):
    copies = jnp.broadcast_to(array, (lax.axis_size(axis), *array.shape))
    return lax.all_to_all(copies, axis, split_axis=0, concat_axis=0, tiled=True)


def joined_along(tiles, dim):
    tiles = jnp.moveaxis(tiles, 0, dim)
    dims = tiles.shape
    return tiles.reshape(*dims[:dim], dims[dim] * dims[dim + 1], *dims[dim + 2 :])


def collect(array, axis, dim):
    tiles = sent_to_all(array, axis)
    return joined_along(tiles, dim)


def cut_along(array, dim, size):
    before, after = (array.shape[:dim], array.shape[dim + 1 :])
    return jnp.moveaxis(array.reshape(*before, size, -1, *after), dim, 0)


def sum_at_owner(array, axis, dim):
    size = lax.axis_size(axis)
    tiles = lax.all_to_all(cut_along(array, dim, size), axis, 0, 0, tiled=True)
    return jnp.sum(tiles, axis=0)


def rows_for(lines, size):
    spare = -len(lines) % size
    return jnp.pad(lines, [(0, spare)] + [(0, 0)] * (lines.ndim - 1))


def total_of(array, axes):
    lines = array.reshape(-1, array.shape[-1])
    own = sum_at_owner(rows_for(lines, lax.axis_size(axes)), axes, 0)
    whole = collect(own, axes, 0)
    return whole[: len(lines)].reshape(array.shape)


def broadcast(array, axis, root):
    return lax.dynamic_index_in_dim(lax.all_gather(array, axis), root, 0, keepdims=False)


def taken_together(array, axis):
    return sent_to_all(array, axis).sum(axis=0)


def body(covariance, first_jacobian, second_jacobian, first_residuals, second_residuals):
    row_index = lax.axis_index("row")
    col_index = lax.axis_index("col")
    row_count = lax.axis_size("row")
    col_count = lax.axis_size("col")
    per_col = row_count // col_count
    tile_rows, tile_cols = covariance.shape
    shard_width = first_jacobian.shape[1]
    measures = first_jacobian.shape[0]
    high = lax.Precision.HIGHEST
    current = covariance
    current_lambda = lam_start
    accum_rows = jnp.zeros((tile_rows,), jnp.float32)
    previous_rows = jnp.zeros((tile_rows,), jnp.float32)
    for jacobian, errors in (
        (first_jacobian, first_residuals),
        (second_jacobian, second_residuals),
    ):
        jac_rows = collect(jacobian, "col", 1).astype(jnp.float32)
        left_part = jnp.dot(jac_rows, current, precision=high)
        prod_cols = total_of(left_part, "row")
        own_block = lax.dynamic_slice_in_dim(
            prod_cols, row_index % per_col * tile_rows, tile_rows, 1
        )
        prod_rows = broadcast(own_block, "col", row_index // per_col)
        inner_part = jnp.dot(jac_rows, prod_rows.T, precision=high)
        pred_part = jnp.dot(jac_rows, previous_rows, precision=high)
        innovation_matrix, predicted = (
            taken_together(inner_part, "row"),
            taken_together(pred_part, "row"),
        )
        innovation_matrix = innovation_matrix + current_lambda * jnp.eye(
            measures, dtype=jnp.float32
        )
        factor = jnp.linalg.cholesky(innovation_matrix)
        solved = jax.scipy.linalg.cho_solve((factor, True), (errors - predicted)[:, None])[:, 0]
        delta_rows = jnp.dot(prod_rows.T, solved, precision=high)
        gain_cols = jax.scipy.linalg.cho_solve((factor, True), prod_cols)
        current = (current - jnp.dot(prod_rows.T, gain_cols, precision=high)) / current_lambda
        accum_rows = accum_rows + delta_rows
        previous_rows = delta_rows
        current_lambda = forget_rate * current_lambda + (1.0 - forget_rate)
    increment = lax.dynamic_slice_in_dim(accum_rows, col_index * shard_width, shard_width, 0)
    return (current, increment)


def solution(mesh):
    return jax.shard_map(
        body,
        mesh=mesh,
        in_specs=(P("row", "col"), P(None, ("row", "col")), P(None, ("row", "col")), P(), P()),
        out_specs=(P("row", "col"), P(("row", "col"))),
        check_vma=False,
    )
```

profile of v0, /device:TPU:8, one launch (start us, length us, event | category | flops | bytes accessed | tf_op | source)
XLA Modules:
  0.0 207.5 jit_solution(11376787234627393570)
XLA Ops:
  1.5 8.7 %all_to_all.52 = bf16[8,2,1024]{2,1,0:T(2,128)(2,1)S(1)} all-to-all(bf16[8,2,1024]{2,1,0:T(2,128)(2,1)S(1)} %reshape.89), channel_id=1, replica_groups=mesh['row'=32,'col'=8] {'col'}, dimensions={0} | all-to-all | bytes 65536 | tf_op jit(solution)/shard_map/all_to_all | solution.py:12
  10.4 3.8 %convolution_bitcast_fusion.1 = f32[32,1,2048]{2,0,1:T(8,128)S(1)} fusion(bf16[32,512]{1,0:T(8,128)(2,1)S(1)} %reshape.62, f32[512,2048]{1,0:T(8,128)} %param.10), kind=kOutput, calls=%fused_computation.3 | convolution fusion | flops 402653184 | bytes 4489216 | tf_op jit(solution)/shard_map/dot_general | solution.py:76
  14.5 23.5 %all_to_all.53 = f32[32,1,2048]{2,1,0:T(1,128)S(1)} all-to-all(f32[32,1,2048]{2,1,0:T(1,128)S(1)} %copy.34), channel_id=1, replica_groups=mesh['row'=32,'col'=8] {'row'}, dimensions={0} | all-to-all | bytes 524288 | tf_op jit(solution)/shard_map/all_to_all | solution.py:33
  38.2 0.8 broadcast_in_dim.35
  39.0 4.4 %all-to-all-start.2 = ((f32[32,1,2048]{2,1,0:T(1,128)}), f32[32,1,2048]{2,1,0:T(1,128)S(1)}, u32[]{:S(2)}, u32[]{:S(2)}) async-start(f32[32,1,2048]{2,1,0:T(1,128)} %broadcast_in_dim.35), calls=%async_computation.2 | async-start | bytes 524288 | tf_op jit(solution)/shard_map/all_to_all | solution.py:12
  44.2 10.6 %all-to-all-done.2 = f32[32,1,2048]{2,1,0:T(1,128)S(1)} async-done(((f32[32,1,2048]{2,1,0:T(1,128)}), f32[32,1,2048]{2,1,0:T(1,128)S(1)}, u32[]{:S(2)}, u32[]{:S(2)}) %all-to-all-start.2) | async-done | bytes 262176 | tf_op jit(solution)/shard_map/all_to_all | solution.py:12
  54.8 4.7 %all-to-all-start.4 = ((bf16[8,2,1024]{2,1,0:T(2,128)(2,1)}), bf16[8,2,1024]{2,1,0:T(2,128)(2,1)S(1)}, u32[]{:S(2)}, u32[]{:S(2)}) async-start(bf16[8,2,1024]{2,1,0:T(2,128)(2,1)} %reshape.93), calls=%async_computation.4 | async-start | bytes 65536 | tf_op jit(solution)/shard_map/all_to_all | solution.py:12
  59.5 13.1 %all-gather = f32[256,1,512]{2,1,0:T(1,128)S(1)} all-gather(f32[32,1,512]{2,1,0:T(1,128)S(1)} %constant_dynamic-slice_fusion.1), channel_id=2, replica_groups=mesh['row'=32,'col'=8] {'col'}, dimensions={0}, use_global_device_ids=true | all-gather | bytes 589824 | tf_op jit(solution)/shard_map/all_gather | solution.py:50
  73.0 0.9 reshape.91
  73.9 4.5 %all-to-all-start.3 = ((f32[32,1,1024]{2,1,0:T(1,128)}), f32[32,1,1024]{2,1,0:T(1,128)S(1)}, u32[]{:S(2)}, u32[]{:S(2)}) async-start(f32[32,1,1024]{2,1,0:T(1,128)} %reshape.91), calls=%async_computation.3 | async-start | bytes 262144 | tf_op jit(solution)/shard_map/all_to_all | solution.py:12
  78.8 10.4 %all-to-all-done.3 = f32[32,1,1024]{2,1,0:T(1,128)S(1)} async-done(((f32[32,1,1024]{2,1,0:T(1,128)}), f32[32,1,1024]{2,1,0:T(1,128)S(1)}, u32[]{:S(2)}, u32[]{:S(2)}) %all-to-all-start.3) | async-done | bytes 131104 | tf_op jit(solution)/shard_map/all_to_all | solution.py:12
  89.8 3.8 %all-to-all-start.8 = ((f32[32,1,32]{2,1,0:T(1,128)}), f32[32,1,32]{2,1,0:T(1,128)S(1)}, u32[]{:S(2)}, u32[]{:S(2)}) async-start(f32[32,1,32]{2,1,0:T(1,128)} %broadcast_in_dim.41), calls=%async_computation.8 | async-start | bytes 32768 | tf_op jit(solution)/shard_map/all_to_all | solution.py:12
  94.2 0.9 reduce.8
  95.6 2.9 %cholesky.44 = f32[32,32]{1,0:T(8,128)S(1)} custom-call(f32[32,32]{1,0:T(8,128)S(1)} %fusion.33), custom_call_target="Cholesky" | custom-call | tf_op jit(solution)/shard_map/jit(cholesky)/cholesky | solution.py:91
  99.8 2.4 %custom-call.14 = f32[1,32,32]{1,2,0:T(8,128)S(1)} custom-call(f32[1,32,32]{2,1,0:T(8,128)S(1)} %fusion.20), custom_call_target="InvertDiagBlocksLowerTriangular" | custom-call | tf_op jit(solution)/shard_map/jit(_cho_solve)/triangular_solve | solution.py:94
  103.1 5.5 %subtract_multiply_fusion.1 = f32[512,2048]{1,0:T(8,128)S(1)} fusion(f32[512,2048]{1,0:T(8,128)} %param.10, f32[32,2048]{1,0:T(8,128)S(1)} %fusion.30, f32[8,32,512]{2,1,0:T(8,128)S(1)} %bitcast.124, s32[]{:T(128)S(6)} %select_n.32), kind=kOutput, calls=%fused_computation.1 | convolution fusion | flops 404750336 | bytes 8716292 | tf_op jit(solution)/shard_map/dot_general | solution.py:95
  108.6 2.0 copy-done
  110.6 1.7 convolution_bitcast_fusion
  112.3 1.0 copy.39
  113.3 9.8 %all-to-all-start.5 = ((f32[32,1,2048]{2,1,0:T(1,128)}), f32[32,1,2048]{2,1,0:T(1,128)S(1)}, u32[]{:S(2)}, u32[]{:S(2)}) async-start(f32[32,1,2048]{2,1,0:T(1,128)} %copy.39), calls=%async_computation.5 | async-start | bytes 524288 | tf_op jit(solution)/shard_map/all_to_all | solution.py:33
  123.2 11.1 %all-to-all-done.5 = f32[32,1,2048]{2,1,0:T(1,128)S(1)} async-done(((f32[32,1,2048]{2,1,0:T(1,128)}), f32[32,1,2048]{2,1,0:T(1,128)S(1)}, u32[]{:S(2)}, u32[]{:S(2)}) %all-to-all-start.5) | async-done | bytes 262176 | tf_op jit(solution)/shard_map/all_to_all | solution.py:33
  135.3 4.4 %all-to-all-start.6 = ((f32[32,1,2048]{2,1,0:T(1,128)}), f32[32,1,2048]{2,1,0:T(1,128)S(1)}, u32[]{:S(2)}, u32[]{:S(2)}) async-start(f32[32,1,2048]{2,1,0:T(1,128)} %broadcast_in_dim.38), calls=%async_computation.6 | async-start | bytes 524288 | tf_op jit(solution)/shard_map/all_to_all | solution.py:12
  140.2 10.6 %all-to-all-done.6 = f32[32,1,2048]{2,1,0:T(1,128)S(1)} async-done(((f32[32,1,2048]{2,1,0:T(1,128)}), f32[32,1,2048]{2,1,0:T(1,128)S(1)}, u32[]{:S(2)}, u32[]{:S(2)}) %all-to-all-start.6) | async-done | bytes 262176 | tf_op jit(solution)/shard_map/all_to_all | solution.py:12
  151.4 4.5 %all-to-all-start.9 = ((f32[32,1,32]{2,1,0:T(1,128)}), f32[32,1,32]{2,1,0:T(1,128)S(1)}, u32[]{:S(2)}, u32[]{:S(2)}) async-start(f32[32,1,32]{2,1,0:T(1,128)} %broadcast_in_dim.43), calls=%async_computation.9 | async-start | bytes 32768 | tf_op jit(solution)/shard_map/all_to_all | solution.py:12
  155.9 13.1 %all-gather.1 = f32[256,1,512]{2,1,0:T(1,128)S(1)} all-gather(f32[32,1,512]{2,1,0:T(1,128)S(1)} %constant_dynamic-slice_fusion), channel_id=3, replica_groups=mesh['row'=32,'col'=8] {'col'}, dimensions={0}, use_global_device_ids=true | all-gather | bytes 589824 | tf_op jit(solution)/shard_map/all_gather | solution.py:50
  169.3 0.9 reshape.95
  170.2 9.8 %all-to-all-start.7 = ((f32[32,1,1024]{2,1,0:T(1,128)}), f32[32,1,1024]{2,1,0:T(1,128)S(1)}, u32[]{:S(2)}, u32[]{:S(2)}) async-start(f32[32,1,1024]{2,1,0:T(1,128)} %reshape.95), calls=%async_computation.7 | async-start | bytes 262144 | tf_op jit(solution)/shard_map/all_to_all | solution.py:12
  180.1 10.8 %all-to-all-done.7 = f32[32,1,1024]{2,1,0:T(1,128)S(1)} async-done(((f32[32,1,1024]{2,1,0:T(1,128)}), f32[32,1,1024]{2,1,0:T(1,128)S(1)}, u32[]{:S(2)}, u32[]{:S(2)}) %all-to-all-start.7) | async-done | bytes 131104 | tf_op jit(solution)/shard_map/all_to_all | solution.py:12
  190.8 1.0 reduce.9
  192.2 2.9 %cholesky.55 = f32[32,32]{1,0:T(8,128)S(1)} custom-call(f32[32,32]{1,0:T(8,128)S(1)} %fusion.27), custom_call_target="Cholesky" | custom-call | tf_op jit(solution)/shard_map/jit(cholesky)/cholesky | solution.py:91
  196.5 2.4 %custom-call.15 = f32[1,32,32]{1,2,0:T(8,128)S(1)} custom-call(f32[1,32,32]{2,1,0:T(8,128)S(1)} %fusion.21), custom_call_target="InvertDiagBlocksLowerTriangular" | custom-call | tf_op jit(solution)/shard_map/jit(_cho_solve)/triangular_solve | solution.py:94
  200.0 6.8 %subtract_multiply_fusion = f32[512,2048]{1,0:T(8,128)} fusion(f32[512,2048]{1,0:T(8,128)} %copy-done, f32[32,2048]{1,0:T(8,128)S(1)} %fusion.24, f32[8,32,512]{2,1,0:T(8,128)S(1)} %bitcast.127, s32[]{:T(128)S(6)} %select_n.32), kind=kOutput, calls=%fused_computation | convolution fusion | flops 404750336 | bytes 8716292 | tf_op jit(solution)/shard_map/dot_general | solution.py:95
  (71 shorter events, 12.7 us)
Async XLA Ops:
  0.6 42.8 %copy-start.1 = (bf16[32,64]{1,0:T(8,128)(2,1)S(1)}, bf16[32,64]{1,0:T(8,128)(2,1)}, u32[]{:S(2)}) copy-start(bf16[32,64]{1,0:T(8,128)(2,1)} %param.12) | copy-start | bytes 12292
  39.0 15.8 %all-to-all-start.2 = ((f32[32,1,2048]{2,1,0:T(1,128)}), f32[32,1,2048]{2,1,0:T(1,128)S(1)}, u32[]{:S(2)}, u32[]{:S(2)}) async-start(f32[32,1,2048]{2,1,0:T(1,128)} %broadcast_in_dim.35), calls=%async_computation.2 | async-start | bytes 524288 | tf_op jit(solution)/shard_map/all_to_all | solution.py:12
  54.8 19.1 %all-to-all-start.4 = ((bf16[8,2,1024]{2,1,0:T(2,128)(2,1)}), bf16[8,2,1024]{2,1,0:T(2,128)(2,1)S(1)}, u32[]{:S(2)}, u32[]{:S(2)}) async-start(bf16[8,2,1024]{2,1,0:T(2,128)(2,1)} %reshape.93), calls=%async_computation.4 | async-start | bytes 65536 | tf_op jit(solution)/shard_map/all_to_all | solution.py:12
  73.9 15.3 %all-to-all-start.3 = ((f32[32,1,1024]{2,1,0:T(1,128)}), f32[32,1,1024]{2,1,0:T(1,128)S(1)}, u32[]{:S(2)}, u32[]{:S(2)}) async-start(f32[32,1,1024]{2,1,0:T(1,128)} %reshape.91), calls=%async_computation.3 | async-start | bytes 262144 | tf_op jit(solution)/shard_map/all_to_all | solution.py:12
  89.8 23.4 %all-to-all-start.8 = ((f32[32,1,32]{2,1,0:T(1,128)}), f32[32,1,32]{2,1,0:T(1,128)S(1)}, u32[]{:S(2)}, u32[]{:S(2)}) async-start(f32[32,1,32]{2,1,0:T(1,128)} %broadcast_in_dim.41), calls=%async_computation.8 | async-start | bytes 32768 | tf_op jit(solution)/shard_map/all_to_all | solution.py:12
  108.6 2.0 copy-start
  110.6 12.5 %copy-start.2 = (f32[32]{0:T(128)S(1)}, f32[32]{0:T(128)}, u32[]{:S(2)}) copy-start(f32[32]{0:T(128)} %param.13) | copy-start | bytes 388
  112.3 86.6 %copy-start.3 = (f32[32]{0:T(128)S(1)}, f32[32]{0:T(128)}, u32[]{:S(2)}) copy-start(f32[32]{0:T(128)} %param.14) | copy-start | bytes 388
  113.3 21.1 %all-to-all-start.5 = ((f32[32,1,2048]{2,1,0:T(1,128)}), f32[32,1,2048]{2,1,0:T(1,128)S(1)}, u32[]{:S(2)}, u32[]{:S(2)}) async-start(f32[32,1,2048]{2,1,0:T(1,128)} %copy.39), calls=%async_computation.5 | async-start | bytes 524288 | tf_op jit(solution)/shard_map/all_to_all | solution.py:33
  135.3 15.5 %all-to-all-start.6 = ((f32[32,1,2048]{2,1,0:T(1,128)}), f32[32,1,2048]{2,1,0:T(1,128)S(1)}, u32[]{:S(2)}, u32[]{:S(2)}) async-start(f32[32,1,2048]{2,1,0:T(1,128)} %broadcast_in_dim.38), calls=%async_computation.6 | async-start | bytes 524288 | tf_op jit(solution)/shard_map/all_to_all | solution.py:12
  151.4 18.8 %all-to-all-start.9 = ((f32[32,1,32]{2,1,0:T(1,128)}), f32[32,1,32]{2,1,0:T(1,128)S(1)}, u32[]{:S(2)}, u32[]{:S(2)}) async-start(f32[32,1,32]{2,1,0:T(1,128)} %broadcast_in_dim.43), calls=%async_computation.9 | async-start | bytes 32768 | tf_op jit(solution)/shard_map/all_to_all | solution.py:12
  170.2 20.6 %all-to-all-start.7 = ((f32[32,1,1024]{2,1,0:T(1,128)}), f32[32,1,1024]{2,1,0:T(1,128)S(1)}, u32[]{:S(2)}, u32[]{:S(2)}) async-start(f32[32,1,1024]{2,1,0:T(1,128)} %reshape.95), calls=%async_computation.7 | async-start | bytes 262144 | tf_op jit(solution)/shard_map/all_to_all | solution.py:12
where the time goes:
time: 208 us
  blocking collectives  58.4 us (28%)
  waiting for transfers between devices  53.5 us (26%)
  starting transfers between devices  45.9 us (22%)
  matrix products  20.8 us (10%)
  other arithmetic  15.8 us (8%)
  local copies, waits for them, and re-layouts  12.1 us (6%)
    all_to_all x7, waiting for transfers between devices, sent_to_all(): return lax.all_to_all(copies, axis, split_axis=0, concat_axis=0, tiled=True)  42.4 us
    all_to_all x7, starting transfers between devices, sent_to_all(): return lax.all_to_all(copies, axis, split_axis=0, concat_axis=0, tiled=True)  36.1 us
    all_gather x2, blocking collectives, broadcast(): lax.all_gather(array, axis)  26.2 us
    all_to_all x1, blocking collectives, sum_at_owner(): tiles = lax.all_to_all(cut_along(array, dim, size), axis, 0, 0, tiled=True)  23.5 us
    dot_general x2, matrix products, body(): jnp.dot(prod_rows.T, gain_cols, precision=high)  12.3 us
    all_to_all x1, waiting for transfers between devices, sum_at_owner(): tiles = lax.all_to_all(cut_along(array, dim, size), axis, 0, 0, tiled=True)  11.1 us
    all_to_all x1, starting transfers between devices, sum_at_owner(): tiles = lax.all_to_all(cut_along(array, dim, size), axis, 0, 0, tiled=True)  9.79 us
    all_to_all x1, blocking collectives, sent_to_all(): return lax.all_to_all(copies, axis, split_axis=0, concat_axis=0, tiled=True)  8.7 us
  transfers between devices with their start and end apart: 8, of which 5 were waited for; matrix products, arithmetic and copies ran while one was open for 10% of the time, Pallas kernels for 0%

commit v1 on v0

v1 whole, which is shorter than its diff:
```python
import jax
import jax.numpy as jnp
from jax import lax
from jax.experimental import pallas as pl
from jax.experimental.pallas import tpu as pltpu
from jax.sharding import PartitionSpec as P

lam_start = 0.98
forget_rate = 0.9987
lam_next = forget_rate * lam_start + (1.0 - forget_rate)

f32 = jnp.float32
bf16 = jnp.bfloat16


def device(x, y, z, k):
    return (x * 8 + z) * 8 + y * 2 + k


def to_row_block(swap):
    pairs = []
    for x in range(4):
        for y in range(4):
            for z in range(8):
                for k in range(2):
                    i = ((z + 2 + 4 * k) % 8) // 2
                    target = device(y, (x + 2) % 4, 4 * k + i, (z + swap) % 2)
                    pairs.append((device(x, y, z, k), target))
    return pairs


def reversed_pairs(pairs):
    return [(b, a) for a, b in pairs]


def piece_at(tile, h, core):
    x = (tile % 4 + 2) % 4
    z = lax.rem(2 * (tile // 4) + h + 6 + 4 * core, 8)
    return x * 8 + z


def halves(value):
    hi = value.astype(bf16)
    return hi, (value - hi.astype(f32)).astype(bf16)


def thirds(value):
    hi = value.astype(bf16)
    rest = value - hi.astype(f32)
    mid = rest.astype(bf16)
    return hi, mid, (rest - mid.astype(f32)).astype(bf16)


def dot(a, b, dims):
    return lax.dot_general(a, b, (dims, ((), ())), preferred_element_type=f32)


def paired(even, odd):
    even, odd = even.astype(f32), odd.astype(f32)
    low = lax.broadcasted_iota(jnp.int32, even.shape, 1) < 64
    top = jnp.where(low, even, pltpu.roll(odd, 64, 1))
    bottom = jnp.where(low, pltpu.roll(even, 64, 1), odd)
    return jnp.concatenate([top, bottom], axis=0).astype(bf16)


VMEM = pl.BlockSpec(memory_space=pltpu.VMEM)


def product_kernel(jac_ref, cov_ref, out_ref):
    step = pl.program_id(0)
    core = lax.rem(lax.axis_index("col"), 2)
    jac = jnp.concatenate(
        [paired(jac_ref[2 * q], jac_ref[2 * q + 1]) for q in range(4)], axis=1
    )
    hi, mid, low = thirds(cov_ref[...])
    dims = ((1,), (0,))
    part = dot(jac, low, dims) + dot(jac, mid, dims) + dot(jac, hi, dims)
    for tile in range(4):
        for h in range(2):
            place = ((tile + 2) % 4) * 8 + lax.rem(2 * step + h + 6 + 4 * core, 8)
            out_ref[place] = part[32 * h : 32 * h + 32, 128 * tile : 128 * tile + 128]


def product(jac, cov):
    return pl.pallas_call(
        product_kernel,
        grid=(4,),
        in_specs=[
            pl.BlockSpec((8, 32, 128), lambda g: (0, 0, 0)),
            pl.BlockSpec((512, 512), lambda g: (0, g)),
        ],
        out_specs=pl.BlockSpec((32, 32, 128), lambda g: (0, 0, 0)),
        out_shape=jax.ShapeDtypeStruct((32, 32, 128), f32),
        name="product",
    )(jac, cov)


def reduce_kernel(parts_ref, same_ref, other_ref, row_ref, own_ref, gram_ref):
    total = jnp.sum(parts_ref[...], axis=0)
    own_ref[...] = total
    row_ref[...] = jnp.broadcast_to(total[None], row_ref.shape)
    second = lax.rem(lax.axis_index("row"), 2) == 1
    same, other = same_ref[...].astype(f32), other_ref[...].astype(f32)
    jac = paired(jnp.where(second, other, same), jnp.where(second, same, other))
    dims = ((1,), (1,))
    hi, mid, low = thirds(total)
    gram = dot(jac, low, dims) + dot(jac, mid, dims) + dot(jac, hi, dims)
    packed = jnp.concatenate([gram[16 * q : 16 * q + 16] for q in range(4)], axis=1)
    gram_ref[...] = jnp.broadcast_to(packed[None], gram_ref.shape)


def reduce(parts, same, other):
    return pl.pallas_call(
        reduce_kernel,
        in_specs=[VMEM] * 3,
        out_specs=[VMEM] * 3,
        out_shape=[
            jax.ShapeDtypeStruct((32, 32, 128), f32),
            jax.ShapeDtypeStruct((32, 128), f32),
            jax.ShapeDtypeStruct((8, 16, 128), f32),
        ],
        name="reduce",
    )(parts, same, other)


def spread_kernel(parts_ref, out_ref):
    total = jnp.sum(parts_ref[...], axis=0)
    out_ref[...] = jnp.broadcast_to(total[None], out_ref.shape)


def spread(parts):
    return pl.pallas_call(
        spread_kernel,
        in_specs=[VMEM],
        out_specs=VMEM,
        out_shape=jax.ShapeDtypeStruct((32, 16, 128), f32),
        name="spread",
    )(parts)


def factor_kernel(gram_ref, out_ref):
    first = gram_ref[0]
    second = gram_ref[1]
    for t in range(1, 16):
        first = first + gram_ref[2 * t]
        second = second + gram_ref[2 * t + 1]
    left = jnp.concatenate([first[:, 32 * q : 32 * q + 32] for q in range(4)], axis=0)
    right = jnp.concatenate([second[:, 32 * q : 32 * q + 32] for q in range(4)], axis=0)
    gram = jnp.concatenate([left, right, jnp.zeros((64, 64), f32)], axis=1)
    rows = lax.broadcasted_iota(jnp.int32, (64, 128), 0)
    lanes = lax.broadcasted_iota(jnp.int32, (64, 128), 1)
    shift = jnp.where(rows < 32, lam_start, lam_start * lam_next).astype(f32)
    work = gram + jnp.where(rows == lanes, shift, 0.0) + jnp.where(rows + 64 == lanes, 1.0, 0.0)
    diag = jnp.ones((64, 128), f32)
    for k in range(64):
        base = k // 8 * 8
        pivot_row = work[k : k + 1, :]
        pivot = pivot_row[:, k : k + 1]
        diag = jnp.where(rows == k, pivot, diag)
        if k == 63:
            break
        part = work[base:, :]
        column = part[:, k : k + 1] * (1.0 / pivot)
        column = jnp.where(rows[base:, :] > k, column, 0.0)
        part = part - column * pivot_row
        work = jnp.concatenate([work[:base, :], part], axis=0) if base else part
    out_ref[...] = work[:, 64:] * lax.rsqrt(diag)[:, :64]


def factor(gram):
    return pl.pallas_call(
        factor_kernel,
        in_specs=[VMEM],
        out_specs=VMEM,
        out_shape=jax.ShapeDtypeStruct((64, 64), f32),
        name="factor",
    )(gram)


def update_kernel(cov_ref, cols_ref, rows_ref, inv_ref, errors_ref, out_ref, inc_ref, left_ref):
    step = pl.program_id(0)
    core = lax.rem(lax.axis_index("col"), 2)
    highest = lax.Precision.HIGHEST

    def whitened(block):
        return jnp.dot(inv_ref[...], block, precision=highest, preferred_element_type=f32)

    @pl.when(step == 0)
    def _():
        rows = jnp.concatenate(
            [
                jnp.concatenate([rows_ref[2 * t], rows_ref[2 * t + 1]], axis=0)
                for t in range(4)
            ],
            axis=1,
        )
        rows = whitened(rows)
        hi, low = halves(rows)
        left_ref[...] = jnp.concatenate([hi, hi, low, low], axis=0)
        weights = jnp.sum(inv_ref[...] * errors_ref[...], axis=1, keepdims=True)
        inc_ref[...] = jnp.sum(rows * weights, axis=0, keepdims=True)

    pieces = []
    for tile in range(4):
        place = ((tile + 2) % 4) * 8
        turn = 2 * step + 6 + 4 * core
        pieces.append(
            jnp.concatenate(
                [cols_ref[place + lax.rem(turn + h, 8)] for h in range(2)], axis=0
            )
        )
    cols = whitened(jnp.concatenate(pieces, axis=1))
    hi, low = halves(cols)
    right = jnp.concatenate([hi, low, hi, low], axis=0)
    change = dot(left_ref[...], right, ((0,), (0,)))
    out_ref[...] = (cov_ref[...] - change) * (1.0 / (lam_start * lam_next))


def update(cov, cols, rows, inv, errors):
    return pl.pallas_call(
        update_kernel,
        grid=(4,),
        in_specs=[
            pl.BlockSpec((512, 512), lambda g: (0, g)),
            pl.BlockSpec((32, 32, 128), lambda g: (0, 0, 0)),
            pl.BlockSpec((8, 32, 128), lambda g: (0, 0, 0)),
            pl.BlockSpec((64, 64), lambda g: (0, 0)),
            pl.BlockSpec((1, 64), lambda g: (0, 0)),
        ],
        out_specs=[
            pl.BlockSpec((512, 512), lambda g: (0, g)),
            pl.BlockSpec((1, 512), lambda g: (0, 0)),
        ],
        out_shape=[
            jax.ShapeDtypeStruct((512, 2048), f32),
            jax.ShapeDtypeStruct((1, 512), f32),
        ],
        scratch_shapes=[pltpu.VMEM((256, 512), bf16)],
        name="update",
    )(cov, cols, rows, inv, errors)


def exchange(array, axis):
    return lax.all_to_all(array, axis, 0, 0, tiled=True)


def body(covariance, first_jacobian, second_jacobian, first_residuals, second_residuals):
    both = ("row", "col")
    jac = jnp.concatenate([first_jacobian, second_jacobian], axis=1)
    errors = jnp.concatenate([first_residuals, second_residuals])[None]
    jac_rows = exchange(jnp.broadcast_to(jac[None], (8, 32, 128)), "col")
    same = lax.ppermute(jac, both, reversed_pairs(to_row_block(0)))
    other = lax.ppermute(jac, both, reversed_pairs(to_row_block(1)))
    parts = exchange(product(jac_rows, covariance), "row")
    for_row, own, gram = reduce(parts, same, other)
    gram = exchange(gram, "col")
    cols = exchange(for_row, "row")
    natural = lax.ppermute(own, both, to_row_block(0))
    gram = exchange(spread(gram), "row")
    rows = exchange(jnp.broadcast_to(natural[None], (8, 32, 128)), "col")
    out, increment = update(covariance, cols, rows, factor(gram), errors)
    start = lax.axis_index("col") * 64
    return out, lax.dynamic_slice_in_dim(increment[0], start, 64, 0)


def solution(mesh):
    return jax.shard_map(
        body,
        mesh=mesh,
        in_specs=(P("row", "col"), P(None, ("row", "col")), P(None, ("row", "col")), P(), P()),
        out_specs=(P("row", "col"), P(("row", "col"))),
        check_vma=False,
    )
```

time: 208 us -> 119 us (0.57)
  blocking collectives: 58.4 us -> 28.1 us
  waiting for transfers between devices: 53.5 us -> 26.1 us
  Pallas kernels: 0 us -> 21.7 us
  matrix products: 20.8 us -> 0 us
  other arithmetic: 15.8 us -> 1.38 us
  starting transfers between devices: 45.9 us -> 35.8 us
  local copies, waits for them, and re-layouts: 12.1 us -> 3.5 us
    all_to_all x8 -> x4, waiting for transfers between devices: 53.5 us -> 14.1 us  [exchange(): return lax.all_to_all(array, axis, 0, 0, tiled=True)]
    all_gather x2 -> x0, blocking collectives: 26.2 us -> none  [broadcast(): lax.all_gather(array, axis)]
    pallas_call x0 -> x5, Pallas kernels: none -> 21.7 us  [the longest x1 7.04 us: factor(): pl.pallas_call(factor_kernel, in_specs=[VMEM], out_specs=VMEM, out_shape=...]
    all_to_all x8 -> x4, starting transfers between devices: 45.9 us -> 24.7 us  [exchange(): return lax.all_to_all(array, axis, 0, 0, tiled=True)]
    dot_general x10 -> x0, matrix products: 18.6 us -> none  [the longest x2 12.3 us: body(): jnp.dot(prod_rows.T, gain_cols, precision=high)]
    another operation x10 -> x0, other arithmetic: 13.4 us -> none  [the longest x6 7.18 us: body(): factor = jnp.linalg.cholesky(innovation_matrix)]
    ppermute x0 -> x3, waiting for transfers between devices: none -> 12 us  [the longest x1 7.03 us: body(): same = lax.ppermute(jac, both, reversed_pairs(to_row_block(0)))]
    ppermute x0 -> x3, starting transfers between devices: none -> 11.2 us  [the longest x1 7.08 us: body(): same = lax.ppermute(jac, both, reversed_pairs(to_row_block(0)))]
  transfers between devices with their start and end apart: 8 -> 7, of which waited for: 5 -> 5; matrix products, arithmetic and copies ran while one was open for 10% -> 0% of each run, Pallas kernels for 0% -> 7%
where the time goes in v1:
time: 119 us; the launch traced here: 117 us
  starting transfers between devices  35.8 us (30%)
  blocking collectives  28.1 us (24%)
  waiting for transfers between devices  26.1 us (22%)
  Pallas kernels  21.7 us (18%)
  local copies, waits for them, and re-layouts  3.5 us (3%)
  other arithmetic  1.38 us (1%)
    all_to_all x2, blocking collectives, exchange(): return lax.all_to_all(array, axis, 0, 0, tiled=True)  28.1 us
    all_to_all x4, starting transfers between devices, exchange(): return lax.all_to_all(array, axis, 0, 0, tiled=True)  24.7 us
    all_to_all x4, waiting for transfers between devices, exchange(): return lax.all_to_all(array, axis, 0, 0, tiled=True)  14.1 us
    ppermute x1, starting transfers between devices, body(): same = lax.ppermute(jac, both, reversed_pairs(to_row_block(0)))  7.08 us
    pallas_call x1, Pallas kernels, factor(): pl.pallas_call(factor_kernel, in_specs=[VMEM], out_specs=VMEM, out_shape=...  7.04 us
    ppermute x1, waiting for transfers between devices, body(): same = lax.ppermute(jac, both, reversed_pairs(to_row_block(0)))  7.03 us
    pallas_call x1, Pallas kernels, update(): pl.pallas_call(update_kernel, grid=(4,), in_specs=[pl.BlockSpec((512, 512...  6.29 us
    ppermute x1, waiting for transfers between devices, body(): natural = lax.ppermute(own, both, to_row_block(0))  4.98 us
  transfers between devices with their start and end apart: 7, of which 5 were waited for; matrix products, arithmetic and copies ran while one was open for 0% of the time, Pallas kernels for 7%

profile of v1, /device:TPU:8, one launch (start us, length us, event | category | flops | bytes accessed | tf_op | source)
XLA Modules:
  0.0 117.3 jit_solution(1052190685179777248)
XLA Ops:
  0.6 0.8 pad_maximum_fusion
  1.4 9.4 %all_to_all.30.jac_ref = bf16[8,32,128]{2,1,0:T(8,128)(2,1)} all-to-all(bf16[8,32,128]{2,1,0:T(8,128)(2,1)S(1)} %broadcast_in_dim.6), channel_id=1, replica_groups=mesh['row'=32,'col'=8] {'col'}, dimensions={0} | all-to-all | bytes 131072 | tf_op jit(solution)/shard_map/all_to_all | solution.py:244
  10.8 4.8 %product.1 = f32[32,32,128]{2,1,0:T(8,128)} custom-call(bf16[8,32,128]{2,1,0:T(8,128)(2,1)} %all_to_all.30.jac_ref, f32[512,2048]{1,0:T(8,128)} %cov_ref.3), custom_call_target="tpu_custom_call" | custom-call | tf_op jit(solution)/shard_map/product/pallas_call | solution.py:85
  15.6 10.9 %all-to-all-start.1 = ((f32[32,32,128]{2,1,0:T(8,128)}), f32[32,32,128]{2,1,0:T(8,128)S(1)}, u32[]{:S(2)}, u32[]{:S(2)}) async-start(f32[32,32,128]{2,1,0:T(8,128)} %product.1), calls=%async_computation.1 | async-start | bytes 1048576 | tf_op jit(solution)/shard_map/all_to_all | solution.py:244
  26.5 7.1 %collective-permute-start = (bf16[32,128]{1,0:T(8,128)(2,1)S(1)}, bf16[32,128]{1,0:T(8,128)(2,1)S(1)}, u32[]{:S(2)}, u32[]{:S(2)}) collective-permute-start(bf16[32,128]{1,0:T(8,128)(2,1)S(1)} %pad_maximum_fusion), channel_id=1, source_target_pairs={{12,0},{60,1},{13,8},{61,9},{20,16},{36,17},{21,24},{37,25},{28,32... | collective-permute-start | bytes 24584 | tf_op jit(solution)/shard_map/ppermute | solution.py:252
  33.6 0.0 collective-permute-start.1
  33.6 7.0 %collective-permute-done.same_ref = bf16[32,128]{1,0:T(8,128)(2,1)S(1)} collective-permute-done((bf16[32,128]{1,0:T(8,128)(2,1)S(1)}, bf16[32,128]{1,0:T(8,128)(2,1)S(1)}, u32[]{:S(2)}, u32[]{:S(2)}) %collective-permute-start) | collective-permute-done | bytes 8224 | tf_op jit(solution)/shard_map/ppermute | solution.py:252
  40.7 0.0 collective-permute-done.1.other_ref
  40.7 2.4 %all-to-all-done.1.parts_ref = f32[32,32,128]{2,1,0:T(8,128)S(1)} async-done(((f32[32,32,128]{2,1,0:T(8,128)}), f32[32,32,128]{2,1,0:T(8,128)S(1)}, u32[]{:S(2)}, u32[]{:S(2)}) %all-to-all-start.1) | async-done | bytes 524320 | tf_op jit(solution)/shard_map/all_to_all | solution.py:244
  43.0 0.0 copy-done.4
  43.1 0.0 copy-done.5
  43.1 0.8 copy-done.1
  43.8 2.0 %reduce.1 = (f32[32,32,128]{2,1,0:T(8,128)}, f32[32,128]{1,0:T(8,128)}, f32[8,16,128]{2,1,0:T(8,128)}) custom-call(f32[32,32,128]{2,1,0:T(8,128)} %copy-done.1, bf16[32,128]{1,0:T(8,128)(2,1)} %copy-done.4, bf16[32,128]{1,0:T(8,128)(2,1)} %copy-done.5), custom_call_target="tpu_custom_call" | custom-call | tf_op jit(solution)/shard_map/reduce/pallas_call | solution.py:113
  45.8 4.7 %all-to-all-start.4 = ((f32[8,16,128]{2,1,0:T(8,128)}), f32[8,16,128]{2,1,0:T(8,128)S(1)}, u32[]{:S(2)}, u32[]{:S(2)}) async-start(f32[8,16,128]{2,1,0:T(8,128)} %get-tuple-element.9), calls=%async_computation.4 | async-start | bytes 131072 | tf_op jit(solution)/shard_map/all_to_all | solution.py:244
  50.6 4.1 %collective-permute-start.2 = (f32[32,128]{1,0:T(8,128)}, f32[32,128]{1,0:T(8,128)S(1)}, u32[]{:S(2)}, u32[]{:S(2)}) collective-permute-start(f32[32,128]{1,0:T(8,128)} %get-tuple-element.8), channel_id=1, source_target_pairs={{0,12},{1,60},{8,13},{9,61},{16,20},{17,36},{24,21},{25,37},{32,28... | collective-permute-start | bytes 49160 | tf_op jit(solution)/shard_map/ppermute | solution.py:258
  54.6 5.0 %collective-permute-done.2 = f32[32,128]{1,0:T(8,128)S(1)} collective-permute-done((f32[32,128]{1,0:T(8,128)}, f32[32,128]{1,0:T(8,128)S(1)}, u32[]{:S(2)}, u32[]{:S(2)}) %collective-permute-start.2) | collective-permute-done | bytes 16416 | tf_op jit(solution)/shard_map/ppermute | solution.py:258
  59.6 0.0 all-to-all-done.4.parts_ref
  59.6 0.7 broadcast_in_dim.7
  60.3 4.5 %all-to-all-start.3 = ((f32[8,32,128]{2,1,0:T(8,128)}), f32[8,32,128]{2,1,0:T(8,128)S(1)}, u32[]{:S(2)}, u32[]{:S(2)}) async-start(f32[8,32,128]{2,1,0:T(8,128)} %broadcast_in_dim.7), calls=%async_computation.3 | async-start | bytes 262144 | tf_op jit(solution)/shard_map/all_to_all | solution.py:244
  64.8 0.0 copy-done.3
  64.8 1.6 %spread.1 = f32[32,16,128]{2,1,0:T(8,128)} custom-call(f32[8,16,128]{2,1,0:T(8,128)} %copy-done.3), custom_call_target="tpu_custom_call" | custom-call | tf_op jit(solution)/shard_map/spread/pallas_call | solution.py:132
  66.4 3.1 %all-to-all-done.3.rows_ref = f32[8,32,128]{2,1,0:T(8,128)S(1)} async-done(((f32[8,32,128]{2,1,0:T(8,128)}), f32[8,32,128]{2,1,0:T(8,128)S(1)}, u32[]{:S(2)}, u32[]{:S(2)}) %all-to-all-start.3) | async-done | bytes 131104 | tf_op jit(solution)/shard_map/all_to_all | solution.py:244
  69.5 18.8 %all_to_all.31.gram_ref = f32[32,16,128]{2,1,0:T(8,128)} all-to-all(f32[32,16,128]{2,1,0:T(8,128)} %spread.1), channel_id=1, replica_groups=mesh['row'=32,'col'=8] {'row'}, dimensions={0} | all-to-all | bytes 524288 | tf_op jit(solution)/shard_map/all_to_all | solution.py:244
  88.3 4.5 %all-to-all-start.2 = ((f32[32,32,128]{2,1,0:T(8,128)}), f32[32,32,128]{2,1,0:T(8,128)S(1)}, u32[]{:S(2)}, u32[]{:S(2)}) async-start(f32[32,32,128]{2,1,0:T(8,128)} %get-tuple-element.7), calls=%async_computation.2 | async-start | bytes 1048576 | tf_op jit(solution)/shard_map/all_to_all | solution.py:244
  92.7 0.0 copy-done.6
  92.8 0.0 copy-done.7
  92.8 0.6 maximum_bitcast_fusion.errors_ref
  93.4 7.0 %factor.1.inv_ref = f32[64,64]{1,0:T(8,128)} custom-call(f32[32,16,128]{2,1,0:T(8,128)} %all_to_all.31.gram_ref), custom_call_target="tpu_custom_call" | custom-call | tf_op jit(solution)/shard_map/factor/pallas_call | solution.py:171
  100.4 8.6 %all-to-all-done.2.cols_ref = f32[32,32,128]{2,1,0:T(8,128)S(1)} async-done(((f32[32,32,128]{2,1,0:T(8,128)}), f32[32,32,128]{2,1,0:T(8,128)S(1)}, u32[]{:S(2)}, u32[]{:S(2)}) %all-to-all-start.2) | async-done | bytes 524320 | tf_op jit(solution)/shard_map/all_to_all | solution.py:244
  109.0 0.8 copy-done
  109.8 6.3 %update.1 = (f32[512,2048]{1,0:T(8,128)}, f32[1,512]{1,0:T(1,128)}) custom-call(f32[512,2048]{1,0:T(8,128)} %cov_ref.3, f32[32,32,128]{2,1,0:T(8,128)} %copy-done, f32[8,32,128]{2,1,0:T(8,128)} %copy-done.2, f32[64,64]{1,0:T(8,128)} %factor.1.inv_ref, f32[1,64]{1,0:T(1,128)} %maximum_bitcast_fusion.errors_ref), custom_call_target="tpu_custom_call" | custom-call | tf_op jit(solution)/shard_map/update/pallas_call | solution.py:220
  116.1 1.2 %dynamic-slice_bitcast_fusion = f32[64]{0:T(128)} fusion(f32[1,512]{1,0:T(1,128)} %get-tuple-element.11, s32[]{:T(128)S(6)} %select_n.3), kind=kLoop, calls=%fused_computation.2 | loop fusion | bytes 516 | tf_op jit(solution)/shard_map/dynamic_slice | solution.py:263
  (10 shorter events, 0.0 us)
Async XLA Ops:
  10.8 81.9 %copy-start.6 = (f32[32]{0:T(128)S(1)}, f32[32]{0:T(128)}, u32[]{:S(2)}) copy-start(f32[32]{0:T(128)} %param.9) | copy-start | bytes 388
  10.8 81.9 %copy-start.7 = (f32[32]{0:T(128)S(1)}, f32[32]{0:T(128)}, u32[]{:S(2)}) copy-start(f32[32]{0:T(128)} %param.8) | copy-start | bytes 388
  15.6 27.4 %all-to-all-start.1 = ((f32[32,32,128]{2,1,0:T(8,128)}), f32[32,32,128]{2,1,0:T(8,128)S(1)}, u32[]{:S(2)}, u32[]{:S(2)}) async-start(f32[32,32,128]{2,1,0:T(8,128)} %product.1), calls=%async_computation.1 | async-start | bytes 1048576 | tf_op jit(solution)/shard_map/all_to_all | solution.py:244
  26.5 14.1 %collective-permute-start = (bf16[32,128]{1,0:T(8,128)(2,1)S(1)}, bf16[32,128]{1,0:T(8,128)(2,1)S(1)}, u32[]{:S(2)}, u32[]{:S(2)}) collective-permute-start(bf16[32,128]{1,0:T(8,128)(2,1)S(1)} %pad_maximum_fusion), channel_id=1, source_target_pairs={{12,0},{60,1},{13,8},{61,9},{20,16},{36,17},{21,24},{37,25},{28,32... | collective-permute-start | bytes 24584 | tf_op jit(solution)/shard_map/ppermute | solution.py:252
  33.6 7.0 %collective-permute-start.1 = (bf16[32,128]{1,0:T(8,128)(2,1)S(1)}, bf16[32,128]{1,0:T(8,128)(2,1)S(1)}, u32[]{:S(2)}, u32[]{:S(2)}) collective-permute-start(bf16[32,128]{1,0:T(8,128)(2,1)S(1)} %pad_maximum_fusion), channel_id=1, source_target_pairs={{13,0},{61,1},{12,8},{60,9},{21,16},{37,17},{20,24},{36,25},{29,32... | collective-permute-start | bytes 24584 | tf_op jit(solution)/shard_map/ppermute | solution.py:253
  40.7 2.4 %copy-start.4 = (bf16[32,128]{1,0:T(8,128)(2,1)}, bf16[32,128]{1,0:T(8,128)(2,1)S(1)}, u32[]{:S(2)}) copy-start(bf16[32,128]{1,0:T(8,128)(2,1)S(1)} %collective-permute-done.same_ref) | copy-start | bytes 24580
  40.7 2.4 %copy-start.5 = (bf16[32,128]{1,0:T(8,128)(2,1)}, bf16[32,128]{1,0:T(8,128)(2,1)S(1)}, u32[]{:S(2)}) copy-start(bf16[32,128]{1,0:T(8,128)(2,1)S(1)} %collective-permute-done.1.other_ref) | copy-start | bytes 24580
  43.1 0.8 copy-start.1
  45.8 13.8 %all-to-all-start.4 = ((f32[8,16,128]{2,1,0:T(8,128)}), f32[8,16,128]{2,1,0:T(8,128)S(1)}, u32[]{:S(2)}, u32[]{:S(2)}) async-start(f32[8,16,128]{2,1,0:T(8,128)} %get-tuple-element.9), calls=%async_computation.4 | async-start | bytes 131072 | tf_op jit(solution)/shard_map/all_to_all | solution.py:244
  50.6 9.1 %collective-permute-start.2 = (f32[32,128]{1,0:T(8,128)}, f32[32,128]{1,0:T(8,128)S(1)}, u32[]{:S(2)}, u32[]{:S(2)}) collective-permute-start(f32[32,128]{1,0:T(8,128)} %get-tuple-element.8), channel_id=1, source_target_pairs={{0,12},{1,60},{8,13},{9,61},{16,20},{17,36},{24,21},{25,37},{32,28... | collective-permute-start | bytes 49160 | tf_op jit(solution)/shard_map/ppermute | solution.py:258
  59.6 5.2 %copy-start.3 = (f32[8,16,128]{2,1,0:T(8,128)}, f32[8,16,128]{2,1,0:T(8,128)S(1)}, u32[]{:S(2)}) copy-start(f32[8,16,128]{2,1,0:T(8,128)S(1)} %all-to-all-done.4.parts_ref) | copy-start | bytes 196612
  60.3 9.2 %all-to-all-start.3 = ((f32[8,32,128]{2,1,0:T(8,128)}), f32[8,32,128]{2,1,0:T(8,128)S(1)}, u32[]{:S(2)}, u32[]{:S(2)}) async-start(f32[8,32,128]{2,1,0:T(8,128)} %broadcast_in_dim.7), calls=%async_computation.3 | async-start | bytes 262144 | tf_op jit(solution)/shard_map/all_to_all | solution.py:244
  69.5 39.5 %copy-start.2 = (f32[8,32,128]{2,1,0:T(8,128)}, f32[8,32,128]{2,1,0:T(8,128)S(1)}, u32[]{:S(2)}) copy-start(f32[8,32,128]{2,1,0:T(8,128)S(1)} %all-to-all-done.3.rows_ref) | copy-start | bytes 393220
  88.3 20.7 %all-to-all-start.2 = ((f32[32,32,128]{2,1,0:T(8,128)}), f32[32,32,128]{2,1,0:T(8,128)S(1)}, u32[]{:S(2)}, u32[]{:S(2)}) async-start(f32[32,32,128]{2,1,0:T(8,128)} %get-tuple-element.7), calls=%async_computation.2 | async-start | bytes 1048576 | tf_op jit(solution)/shard_map/all_to_all | solution.py:244
  109.0 0.8 copy-start

commit v2 on v1

v2 whole, which is shorter than its diff:
```python
import jax
import jax.numpy as jnp
from jax import lax
from jax.experimental import pallas as pl
from jax.experimental.pallas import tpu as pltpu
from jax.sharding import PartitionSpec as P

lam_start = 0.98
forget_rate = 0.9987
lam_next = forget_rate * lam_start + (1.0 - forget_rate)

f32 = jnp.float32
bf16 = jnp.bfloat16


def device(x, y, z, k):
    return (x * 8 + z) * 8 + y * 2 + k


def to_row_block(swap):
    pairs = []
    for x in range(4):
        for y in range(4):
            for z in range(8):
                for k in range(2):
                    i = ((z + 2 + 4 * k) % 8) // 2
                    target = device(y, (x + 2) % 4, 4 * k + i, (z + swap) % 2)
                    pairs.append((device(x, y, z, k), target))
    return pairs


def reversed_pairs(pairs):
    return [(b, a) for a, b in pairs]


def piece_at(tile, h, core):
    x = (tile % 4 + 2) % 4
    z = lax.rem(2 * (tile // 4) + h + 6 + 4 * core, 8)
    return x * 8 + z


def halves(value):
    hi = value.astype(bf16)
    return hi, (value - hi.astype(f32)).astype(bf16)


def thirds(value):
    hi = value.astype(bf16)
    rest = value - hi.astype(f32)
    mid = rest.astype(bf16)
    return hi, mid, (rest - mid.astype(f32)).astype(bf16)


def dot(a, b, dims):
    return lax.dot_general(a, b, (dims, ((), ())), preferred_element_type=f32)


def paired(even, odd):
    even, odd = even.astype(f32), odd.astype(f32)
    low = lax.broadcasted_iota(jnp.int32, even.shape, 1) < 64
    top = jnp.where(low, even, pltpu.roll(odd, 64, 1))
    bottom = jnp.where(low, pltpu.roll(even, 64, 1), odd)
    return jnp.concatenate([top, bottom], axis=0).astype(bf16)


VMEM = pl.BlockSpec(memory_space=pltpu.VMEM)
HBM = pl.BlockSpec(memory_space=pltpu.HBM)
GROUP = 256
GROUPS = 8


def group_of(ref, group):
    return ref.at[:, pl.ds(GROUP * group, GROUP)]


def start_loading(cov_ref, held_ref, sems):
    copies = [
        pltpu.make_async_copy(group_of(cov_ref, g), held_ref.at[g], sems.at[g])
        for g in range(GROUPS)
    ]
    for copy in copies:
        copy.start()
    return copies


def params(mib):
    return pltpu.CompilerParams(vmem_limit_bytes=int(mib * 1048576))


def product_kernel(jac_ref, cov_ref, out_ref, held_ref, sems):
    copies = start_loading(cov_ref, held_ref, sems)
    core = lax.rem(lax.axis_index("col"), 2)
    jac = jnp.concatenate(
        [paired(jac_ref[2 * q], jac_ref[2 * q + 1]) for q in range(4)], axis=1
    )
    dims = ((1,), (0,))
    for group in range(GROUPS):
        copies[group].wait()
        hi, mid, low = thirds(held_ref[group])
        part = dot(jac, low, dims) + dot(jac, mid, dims) + dot(jac, hi, dims)
        for half in range(2):
            tile = 2 * group + half
            for h in range(2):
                out_ref[piece_at(tile, h, core)] = part[
                    32 * h : 32 * h + 32, 128 * half : 128 * half + 128
                ]


def product(jac, cov):
    return pl.pallas_call(
        product_kernel,
        in_specs=[VMEM, HBM],
        out_specs=VMEM,
        out_shape=jax.ShapeDtypeStruct((32, 32, 128), f32),
        scratch_shapes=[
            pltpu.VMEM((GROUPS, 512, GROUP), f32),
            pltpu.SemaphoreType.DMA((GROUPS,)),
        ],
        compiler_params=params(60.25),
        name="product",
    )(jac, cov)


def reduce_kernel(parts_ref, same_ref, other_ref, row_ref, own_ref):
    total = jnp.sum(parts_ref[...], axis=0)
    own_ref[...] = total
    second = lax.rem(lax.axis_index("row"), 2) == 1
    same, other = same_ref[...].astype(f32), other_ref[...].astype(f32)
    jac = paired(jnp.where(second, other, same), jnp.where(second, same, other))
    dims = ((1,), (1,))
    hi, mid, low = thirds(total)
    gram = dot(jac, low, dims) + dot(jac, mid, dims) + dot(jac, hi, dims)
    packed = jnp.concatenate([gram[16 * q : 16 * q + 16] for q in range(4)], axis=1)
    row_ref[:, :32] = jnp.broadcast_to(total[None], (32, 32, 128))
    row_ref[:, 32:] = jnp.broadcast_to(packed[None], (32, 16, 128))


def reduce(parts, same, other):
    return pl.pallas_call(
        reduce_kernel,
        in_specs=[VMEM] * 3,
        out_specs=[VMEM] * 2,
        out_shape=[
            jax.ShapeDtypeStruct((32, 48, 128), f32),
            jax.ShapeDtypeStruct((32, 128), f32),
        ],
        compiler_params=params(8),
        name="reduce",
    )(parts, same, other)


def spread_kernel(parts_ref, natural_ref, out_ref):
    out_ref[:, :32] = jnp.broadcast_to(natural_ref[...][None], (8, 32, 128))
    for h in range(2):
        total = parts_ref[h, 32:]
        for t in range(1, 16):
            total = total + parts_ref[2 * t + h, 32:]
        out_ref[:, 32 + 16 * h : 48 + 16 * h] = jnp.broadcast_to(total[None], (8, 16, 128))


def spread(parts, natural):
    return pl.pallas_call(
        spread_kernel,
        in_specs=[VMEM] * 2,
        out_specs=VMEM,
        out_shape=jax.ShapeDtypeStruct((8, 64, 128), f32),
        compiler_params=params(4),
        name="spread",
    )(parts, natural)


PANEL = 4


def inverse_factor(total):
    first, second = total[:16], total[16:]
    left = jnp.concatenate([first[:, 32 * q : 32 * q + 32] for q in range(4)], axis=0)
    right = jnp.concatenate([second[:, 32 * q : 32 * q + 32] for q in range(4)], axis=0)
    gram = jnp.concatenate([left, right, jnp.zeros((64, 64), f32)], axis=1)
    rows = lax.broadcasted_iota(jnp.int32, (64, 128), 0)
    lanes = lax.broadcasted_iota(jnp.int32, (64, 128), 1)
    shift = jnp.where(rows < 32, lam_start, lam_start * lam_next).astype(f32)
    work = gram + jnp.where(rows == lanes, shift, 0.0) + jnp.where(rows + 64 == lanes, 1.0, 0.0)
    done = []
    for start in range(0, 64, PANEL):
        pivots = [work[j : j + 1, :] for j in range(PANEL)]
        rest = work[PANEL:, :]
        low = rest.shape[0]
        spots = range(start, start + PANEL)
        entry = {
            (i, j): jnp.broadcast_to(pivots[i][:, start + j : start + j + 1], (1, 128))
            for i in range(PANEL)
            for j in range(i + 1)
        }
        columns = [jnp.broadcast_to(rest[:, j : j + 1], (low, 128)) for j in spots] if low else []
        for j in range(PANEL):
            inverse = 1.0 / entry[j, j]
            factors = {i: entry[i, j] * inverse for i in range(j + 1, PANEL)}
            for i in range(j + 1, PANEL):
                pivots[i] = pivots[i] - factors[i] * pivots[j]
                for m in range(j + 1, i + 1):
                    entry[i, m] = entry[i, m] - factors[m] * entry[i, j]
                if low:
                    columns[i] = columns[i] - factors[i] * columns[j]
            done.append(pivots[j] * lax.rsqrt(entry[j, j]))
            if low:
                rest = rest - columns[j] * (pivots[j] * inverse)
        work = rest
    return jnp.concatenate(done, axis=0)[:, 64:]


def update_kernel(
    cov_ref, cols_ref, rows_ref, first_ref, second_ref, out_ref, inc_ref, held_ref, in_sems, out_sems
):
    loads = start_loading(cov_ref, held_ref, in_sems)
    col = lax.axis_index("col")
    core = lax.rem(col, 2)
    total = rows_ref[0, 32:]
    for c in range(1, 8):
        total = total + rows_ref[c, 32:]
    inverse = inverse_factor(total)
    hi, mid, low = thirds(inverse)
    inverse_parts = jnp.concatenate([hi, hi, hi, mid, mid, low], axis=1)

    def whitened(block):
        hi, mid, low = thirds(block)
        parts = jnp.concatenate([hi, mid, low, hi, mid, hi], axis=0)
        return dot(inverse_parts, parts, ((1,), (0,)))

    rows = whitened(
        jnp.concatenate(
            [
                jnp.concatenate([rows_ref[2 * t, :32], rows_ref[2 * t + 1, :32]], axis=0)
                for t in range(4)
            ],
            axis=1,
        )
    )
    hi, low = halves(rows.T)
    left = jnp.concatenate([hi, hi, low, low], axis=1)
    errors = jnp.concatenate([first_ref[...], second_ref[...]], axis=1)
    weights = jnp.sum(inverse * errors, axis=1, keepdims=True)
    inc = jnp.sum(rows * weights, axis=0, keepdims=True)
    own = jnp.zeros((1, 128), f32)
    for tile in range(4):
        own = own + jnp.where(col // 2 == tile, inc[:, 128 * tile : 128 * tile + 128], 0.0)
    inc_ref[...] = jnp.where(core == 1, own[:, 64:], own[:, :64])

    stores = []
    for group in range(GROUPS):
        pieces = [
            jnp.concatenate([cols_ref[piece_at(tile, h, core), :32] for h in range(2)], axis=0)
            for tile in (2 * group, 2 * group + 1)
        ]
        hi, low = halves(whitened(jnp.concatenate(pieces, axis=1)))
        change = dot(left, jnp.concatenate([hi, low, hi, low], axis=0), ((1,), (0,)))
        loads[group].wait()
        held_ref[group] = (held_ref[group] - change) * (1.0 / (lam_start * lam_next))
        store = pltpu.make_async_copy(
            held_ref.at[group], group_of(out_ref, group), out_sems.at[group]
        )
        store.start()
        stores.append(store)
    for store in stores:
        store.wait()


def update(cov, cols, rows, first, second):
    return pl.pallas_call(
        update_kernel,
        in_specs=[HBM] + [VMEM] * 4,
        out_specs=[HBM, VMEM],
        out_shape=[
            jax.ShapeDtypeStruct((512, 2048), f32),
            jax.ShapeDtypeStruct((1, 64), f32),
        ],
        scratch_shapes=[
            pltpu.VMEM((GROUPS, 512, GROUP), f32),
            pltpu.SemaphoreType.DMA((GROUPS,)),
            pltpu.SemaphoreType.DMA((GROUPS,)),
        ],
        compiler_params=params(60.25),
        name="update",
    )(cov, cols, rows, first, second)


def exchange(array, axis):
    return lax.all_to_all(array, axis, 0, 0, tiled=True)


def body(covariance, first_jacobian, second_jacobian, first_residuals, second_residuals):
    both = ("row", "col")
    jac = jnp.concatenate([first_jacobian, second_jacobian], axis=1)
    jac_rows = exchange(jnp.broadcast_to(jac[None], (8, 32, 128)), "col")
    same = lax.ppermute(jac, both, reversed_pairs(to_row_block(0)))
    other = lax.ppermute(jac, both, reversed_pairs(to_row_block(1)))
    parts = product(jac_rows, covariance)
    parts = exchange(parts, "row")
    for_row, own = reduce(parts, same, other)
    cols = exchange(for_row, "row")
    natural = lax.ppermute(own, both, to_row_block(0))
    rows = exchange(spread(cols, natural), "col")
    out, increment = update(covariance, cols, rows, first_residuals[None], second_residuals[None])
    return out, increment[0]


def solution(mesh):
    return jax.shard_map(
        body,
        mesh=mesh,
        in_specs=(P("row", "col"), P(None, ("row", "col")), P(None, ("row", "col")), P(), P()),
        out_specs=(P("row", "col"), P(("row", "col"))),
        check_vma=False,
    )
```

time: 119 us -> 97.5 us (0.82)
  blocking collectives: 28.1 us -> 20.5 us
  starting transfers between devices: 35.8 us -> 28.3 us
  Pallas kernels: 21.7 us -> 16.4 us
  local copies, waits for them, and re-layouts: 3.5 us -> 0.02 us
  waiting for transfers between devices: 26.1 us -> 28.9 us
    ppermute x1, waiting for transfers between devices: 4.98 us -> 19.6 us  [body(): natural = lax.ppermute(own, both, to_row_block(0))]
    all_to_all x4 -> x2, waiting for transfers between devices: 14.1 us -> 2.49 us  [exchange(): return lax.all_to_all(array, axis, 0, 0, tiled=True)]
    all_to_all x2, blocking collectives: 28.1 us -> 20.5 us  [exchange(): return lax.all_to_all(array, axis, 0, 0, tiled=True)]
    all_to_all x4 -> x2, starting transfers between devices: 24.7 us -> 17.4 us  [exchange(): return lax.all_to_all(array, axis, 0, 0, tiled=True)]
    ppermute x1, starting transfers between devices: 0.01 us -> 6.19 us  [body(): other = lax.ppermute(jac, both, reversed_pairs(to_row_block(1)))]
    ppermute x1, starting transfers between devices: 7.08 us -> 1.08 us  [body(): same = lax.ppermute(jac, both, reversed_pairs(to_row_block(0)))]
    ppermute x1, waiting for transfers between devices: 7.03 us -> 1.72 us  [body(): same = lax.ppermute(jac, both, reversed_pairs(to_row_block(0)))]
    pallas_call x5 -> x4, Pallas kernels: 21.7 us -> 16.4 us  [the longest x1 9.62 us: update(): pl.pallas_call(update_kernel, in_specs=[HBM] + [VMEM] * 4, out_specs=[HBM...]
  transfers between devices with their start and end apart: 7 -> 5, of which waited for: 5 -> 4; matrix products, arithmetic and copies ran while one was open for 0% -> 0% of each run, Pallas kernels for 7% -> 0%
where the time goes in v2:
time: 97.5 us; the launch traced here: 95.6 us
  waiting for transfers between devices  28.9 us (30%)
  starting transfers between devices  28.3 us (29%)
  blocking collectives  20.5 us (21%)
  Pallas kernels  16.4 us (17%)
    all_to_all x2, blocking collectives, exchange(): return lax.all_to_all(array, axis, 0, 0, tiled=True)  20.5 us
    ppermute x1, waiting for transfers between devices, body(): natural = lax.ppermute(own, both, to_row_block(0))  19.6 us
    all_to_all x2, starting transfers between devices, exchange(): return lax.all_to_all(array, axis, 0, 0, tiled=True)  17.4 us
    pallas_call x1, Pallas kernels, update(): pl.pallas_call(update_kernel, in_specs=[HBM] + [VMEM] * 4, out_specs=[HBM...  9.62 us
    ppermute x1, starting transfers between devices, body(): other = lax.ppermute(jac, both, reversed_pairs(to_row_block(1)))  6.19 us
    pallas_call x1, Pallas kernels, product(): pl.pallas_call(product_kernel, in_specs=[VMEM, HBM], out_specs=VMEM, out_...  5.6 us
    ppermute x1, waiting for transfers between devices, body(): other = lax.ppermute(jac, both, reversed_pairs(to_row_block(1)))  5.13 us
    ppermute x1, starting transfers between devices, body(): natural = lax.ppermute(own, both, to_row_block(0))  3.65 us
  transfers between devices with their start and end apart: 5, of which 4 were waited for; matrix products, arithmetic and copies ran while one was open for 0% of the time, Pallas kernels for 0%

profile of v2, /device:TPU:8, one launch (start us, length us, event | category | flops | bytes accessed | tf_op | source)
XLA Modules:
  0.0 95.6 jit_solution(14746743109493516664)
XLA Ops:
  0.6 0.8 pad_maximum_fusion
  1.4 9.4 %all_to_all.20.jac_ref = bf16[8,32,128]{2,1,0:T(8,128)(2,1)} all-to-all(bf16[8,32,128]{2,1,0:T(8,128)(2,1)S(1)} %broadcast_in_dim.12), channel_id=1, replica_groups=mesh['row'=32,'col'=8] {'col'}, dimensions={0} | all-to-all | bytes 131072 | tf_op jit(solution)/shard_map/all_to_all | solution.py:288
  10.8 5.6 %product.1 = f32[32,32,128]{2,1,0:T(8,128)} custom-call(bf16[8,32,128]{2,1,0:T(8,128)(2,1)} %all_to_all.20.jac_ref, f32[512,2048]{1,0:T(8,128)} %cov_ref.3), custom_call_target="tpu_custom_call" | custom-call | tf_op jit(solution)/shard_map/product/pallas_call | solution.py:110
  16.4 10.9 %all-to-all-start.1 = ((f32[32,32,128]{2,1,0:T(8,128)}), f32[32,32,128]{2,1,0:T(8,128)S(1)}, u32[]{:S(2)}, u32[]{:S(2)}) async-start(f32[32,32,128]{2,1,0:T(8,128)} %product.1), calls=%async_computation.1 | async-start | bytes 1048576 | tf_op jit(solution)/shard_map/all_to_all | solution.py:288
  27.4 6.2 %collective-permute-start.1 = (bf16[32,128]{1,0:T(8,128)(2,1)S(1)}, bf16[32,128]{1,0:T(8,128)(2,1)S(1)}, u32[]{:S(2)}, u32[]{:S(2)}) collective-permute-start(bf16[32,128]{1,0:T(8,128)(2,1)S(1)} %pad_maximum_fusion), channel_id=1, source_target_pairs={{13,0},{61,1},{12,8},{60,9},{21,16},{37,17},{20,24},{36,25},{29,32... | collective-permute-start | bytes 24584 | tf_op jit(solution)/shard_map/ppermute | solution.py:296
  33.6 1.1 %collective-permute-start = (bf16[32,128]{1,0:T(8,128)(2,1)S(1)}, bf16[32,128]{1,0:T(8,128)(2,1)S(1)}, u32[]{:S(2)}, u32[]{:S(2)}) collective-permute-start(bf16[32,128]{1,0:T(8,128)(2,1)S(1)} %pad_maximum_fusion), channel_id=1, source_target_pairs={{12,0},{60,1},{13,8},{61,9},{20,16},{36,17},{21,24},{37,25},{28,32... | collective-permute-start | bytes 24584 | tf_op jit(solution)/shard_map/ppermute | solution.py:295
  34.6 5.1 %collective-permute-done.1.other_ref = bf16[32,128]{1,0:T(8,128)(2,1)S(1)} collective-permute-done((bf16[32,128]{1,0:T(8,128)(2,1)S(1)}, bf16[32,128]{1,0:T(8,128)(2,1)S(1)}, u32[]{:S(2)}, u32[]{:S(2)}) %collective-permute-start.1) | collective-permute-done | bytes 8224 | tf_op jit(solution)/shard_map/ppermute | solution.py:296
  39.8 1.7 %collective-permute-done.same_ref = bf16[32,128]{1,0:T(8,128)(2,1)S(1)} collective-permute-done((bf16[32,128]{1,0:T(8,128)(2,1)S(1)}, bf16[32,128]{1,0:T(8,128)(2,1)S(1)}, u32[]{:S(2)}, u32[]{:S(2)}) %collective-permute-start) | collective-permute-done | bytes 8224 | tf_op jit(solution)/shard_map/ppermute | solution.py:295
  41.5 2.5 %all-to-all-done.1.parts_ref = f32[32,32,128]{2,1,0:T(8,128)S(1)} async-done(((f32[32,32,128]{2,1,0:T(8,128)}), f32[32,32,128]{2,1,0:T(8,128)S(1)}, u32[]{:S(2)}, u32[]{:S(2)}) %all-to-all-start.1) | async-done | bytes 524320 | tf_op jit(solution)/shard_map/all_to_all | solution.py:288
  44.0 1.2 %reduce.1 = (f32[32,48,128]{2,1,0:T(8,128)}, f32[32,128]{1,0:T(8,128)S(1)}) custom-call(f32[32,32,128]{2,1,0:T(8,128)S(1)} %all-to-all-done.1.parts_ref, bf16[32,128]{1,0:T(8,128)(2,1)S(1)} %collective-permute-done.same_ref, bf16[32,128]{1,0:T(8,128)(2,1)S(1)} %collective-permute-done.1.other_ref), custom_call_target="tpu_custom_call" | custom-call | tf_op jit(solution)/shard_map/reduce/pallas_call | solution.py:139
  45.1 6.4 %all-to-all-start.2 = ((f32[32,48,128]{2,1,0:T(8,128)}), f32[32,48,128]{2,1,0:T(8,128)S(1)}, u32[]{:S(2)}, u32[]{:S(2)}) async-start(f32[32,48,128]{2,1,0:T(8,128)} %get-tuple-element.6), calls=%async_computation.2 | async-start | bytes 1572864 | tf_op jit(solution)/shard_map/all_to_all | solution.py:288
  51.6 3.7 %collective-permute-start.2 = (f32[32,128]{1,0:T(8,128)S(1)}, f32[32,128]{1,0:T(8,128)S(1)}, u32[]{:S(2)}, u32[]{:S(2)}) collective-permute-start(f32[32,128]{1,0:T(8,128)S(1)} %get-tuple-element.7), channel_id=1, source_target_pairs={{0,12},{1,60},{8,13},{9,61},{16,20},{17,36},{24,21},{25,37},{32,28... | collective-permute-start | bytes 49160 | tf_op jit(solution)/shard_map/ppermute | solution.py:301
  55.2 19.6 %collective-permute-done.2.natural_ref = f32[32,128]{1,0:T(8,128)S(1)} collective-permute-done((f32[32,128]{1,0:T(8,128)S(1)}, f32[32,128]{1,0:T(8,128)S(1)}, u32[]{:S(2)}, u32[]{:S(2)}) %collective-permute-start.2) | collective-permute-done | bytes 16416 | tf_op jit(solution)/shard_map/ppermute | solution.py:301
  74.8 0.0 all-to-all-done.2.parts_ref.cols_ref
  74.9 0.0 copy-start
  74.9 11.1 %all_to_all.21.rows_ref = f32[8,64,128]{2,1,0:T(8,128)} all-to-all(f32[8,64,128]{2,1,0:T(8,128)S(1)} %spread.1), channel_id=1, replica_groups=mesh['row'=32,'col'=8] {'col'}, dimensions={0} | all-to-all | bytes 524288 | tf_op jit(solution)/shard_map/all_to_all | solution.py:288
  86.0 0.0 copy-done
  86.0 9.6 %update.1 = (f32[512,2048]{1,0:T(8,128)}, f32[1,64]{1,0:T(1,128)}) custom-call(f32[512,2048]{1,0:T(8,128)} %cov_ref.3, f32[32,48,128]{2,1,0:T(8,128)} %copy-done, f32[8,64,128]{2,1,0:T(8,128)} %all_to_all.21.rows_ref, f32[1,32]{1,0:T(1,128)} %bitcast.3, f32[1,32]{1,0:T(1,128)} %bitcast.4), custom_call_target="tpu_custom_call" | custom-call | tf_op jit(solution)/shard_map/update/pallas_call | solution.py:269
  (2 shorter events, 0.0 us)
Async XLA Ops:
  16.4 27.5 %all-to-all-start.1 = ((f32[32,32,128]{2,1,0:T(8,128)}), f32[32,32,128]{2,1,0:T(8,128)S(1)}, u32[]{:S(2)}, u32[]{:S(2)}) async-start(f32[32,32,128]{2,1,0:T(8,128)} %product.1), calls=%async_computation.1 | async-start | bytes 1048576 | tf_op jit(solution)/shard_map/all_to_all | solution.py:288
  27.4 12.4 %collective-permute-start.1 = (bf16[32,128]{1,0:T(8,128)(2,1)S(1)}, bf16[32,128]{1,0:T(8,128)(2,1)S(1)}, u32[]{:S(2)}, u32[]{:S(2)}) collective-permute-start(bf16[32,128]{1,0:T(8,128)(2,1)S(1)} %pad_maximum_fusion), channel_id=1, source_target_pairs={{13,0},{61,1},{12,8},{60,9},{21,16},{37,17},{20,24},{36,25},{29,32... | collective-permute-start | bytes 24584 | tf_op jit(solution)/shard_map/ppermute | solution.py:296
  33.6 7.9 %collective-permute-start = (bf16[32,128]{1,0:T(8,128)(2,1)S(1)}, bf16[32,128]{1,0:T(8,128)(2,1)S(1)}, u32[]{:S(2)}, u32[]{:S(2)}) collective-permute-start(bf16[32,128]{1,0:T(8,128)(2,1)S(1)} %pad_maximum_fusion), channel_id=1, source_target_pairs={{12,0},{60,1},{13,8},{61,9},{20,16},{36,17},{21,24},{37,25},{28,32... | collective-permute-start | bytes 24584 | tf_op jit(solution)/shard_map/ppermute | solution.py:295
  45.1 29.7 %all-to-all-start.2 = ((f32[32,48,128]{2,1,0:T(8,128)}), f32[32,48,128]{2,1,0:T(8,128)S(1)}, u32[]{:S(2)}, u32[]{:S(2)}) async-start(f32[32,48,128]{2,1,0:T(8,128)} %get-tuple-element.6), calls=%async_computation.2 | async-start | bytes 1572864 | tf_op jit(solution)/shard_map/all_to_all | solution.py:288
  51.6 23.3 %collective-permute-start.2 = (f32[32,128]{1,0:T(8,128)S(1)}, f32[32,128]{1,0:T(8,128)S(1)}, u32[]{:S(2)}, u32[]{:S(2)}) collective-permute-start(f32[32,128]{1,0:T(8,128)S(1)} %get-tuple-element.7), channel_id=1, source_target_pairs={{0,12},{1,60},{8,13},{9,61},{16,20},{17,36},{24,21},{25,37},{32,28... | collective-permute-start | bytes 49160 | tf_op jit(solution)/shard_map/ppermute | solution.py:301
  74.9 11.1 %copy-start = (f32[32,48,128]{2,1,0:T(8,128)}, f32[32,48,128]{2,1,0:T(8,128)S(1)}, u32[]{:S(2)}) copy-start(f32[32,48,128]{2,1,0:T(8,128)S(1)} %all-to-all-done.2.parts_ref.cols_ref) | copy-start | bytes 2359300

commit v3 on v2

--- a/solution.py
+++ b/solution.py
@@ -4,6 +4,7 @@
 from jax.experimental import pallas as pl
 from jax.experimental.pallas import tpu as pltpu
 from jax.sharding import PartitionSpec as P
+
 
 lam_start = 0.98
 forget_rate = 0.9987
@@ -65,8 +66,8 @@
 
 VMEM = pl.BlockSpec(memory_space=pltpu.VMEM)
 HBM = pl.BlockSpec(memory_space=pltpu.HBM)
-GROUP = 256
-GROUPS = 8
+GROUP = 512
+GROUPS = 4
 
 
 def group_of(ref, group):
@@ -96,14 +97,12 @@
     dims = ((1,), (0,))
     for group in range(GROUPS):
         copies[group].wait()
-        hi, mid, low = thirds(held_ref[group])
-        part = dot(jac, low, dims) + dot(jac, mid, dims) + dot(jac, hi, dims)
-        for half in range(2):
-            tile = 2 * group + half
+        hi, low = halves(held_ref[group])
+        part = dot(jac, low, dims) + dot(jac, hi, dims)
+        for step in range(GROUP // 128):
             for h in range(2):
-                out_ref[piece_at(tile, h, core)] = part[
-                    32 * h : 32 * h + 32, 128 * half : 128 * half + 128
-                ]
+                place = piece_at(GROUP // 128 * group + step, h, core)
+                out_ref[place] = part[32 * h : 32 * h + 32, 128 * step : 128 * step + 128]
 
 
 def product(jac, cov):
@@ -169,7 +168,7 @@
     )(parts, natural)
 
 
-PANEL = 4
+PANEL = 8
 
 
 def inverse_factor(total):
@@ -246,15 +245,22 @@
         own = own + jnp.where(col // 2 == tile, inc[:, 128 * tile : 128 * tile + 128], 0.0)
     inc_ref[...] = jnp.where(core == 1, own[:, 64:], own[:, :64])
 
+    cols = whitened(
+        jnp.concatenate(
+            [
+                jnp.concatenate([cols_ref[piece_at(tile, h, core), :32] for h in range(2)], axis=0)
+                for tile in range(16)
+            ],
+            axis=1,
+        )
+    )
+    hi, low = halves(cols)
+    right = jnp.concatenate([hi, low, hi, low], axis=0)
+    for load in loads:
+        load.wait()
     stores = []
     for group in range(GROUPS):
-        pieces = [
-            jnp.concatenate([cols_ref[piece_at(tile, h, core), :32] for h in range(2)], axis=0)
-            for tile in (2 * group, 2 * group + 1)
-        ]
-        hi, low = halves(whitened(jnp.concatenate(pieces, axis=1)))
-        change = dot(left, jnp.concatenate([hi, low, hi, low], axis=0), ((1,), (0,)))
-        loads[group].wait()
+        change = dot(left, right[:, GROUP * group : GROUP * group + GROUP], ((1,), (0,)))
         held_ref[group] = (held_ref[group] - change) * (1.0 / (lam_start * lam_next))
         store = pltpu.make_async_copy(
             held_ref.at[group], group_of(out_ref, group), out_sems.at[group]

time: 97.5 us -> 94.6 us (0.970)
  the two profiles are of different devices: /device:TPU:8 before, /device:TPU:1 now
where the time goes in v3:
time: 94.6 us; the launch traced here: 94.1 us
  starting transfers between devices  31.3 us (33%)
  blocking collectives  25.2 us (27%)
  waiting for transfers between devices  22.6 us (24%)
  Pallas kernels  13.5 us (14%)
    all_to_all x2, blocking collectives, exchange(): return lax.all_to_all(array, axis, 0, 0, tiled=True)  25.2 us
    all_to_all x2, starting transfers between devices, exchange(): return lax.all_to_all(array, axis, 0, 0, tiled=True)  18.4 us
    ppermute x1, waiting for transfers between devices, body(): natural = lax.ppermute(own, both, to_row_block(0))  15 us
    pallas_call x1, Pallas kernels, update(): pl.pallas_call(update_kernel, in_specs=[HBM] + [VMEM] * 4, out_specs=[HBM...  8.15 us
    ppermute x1, starting transfers between devices, body(): other = lax.ppermute(jac, both, reversed_pairs(to_row_block(1)))  7.07 us
    ppermute x1, starting transfers between devices, body(): natural = lax.ppermute(own, both, to_row_block(0))  5.83 us
    pallas_call x1, Pallas kernels, product(): pl.pallas_call(product_kernel, in_specs=[VMEM, HBM], out_specs=VMEM, out_...  4.16 us
    ppermute x1, waiting for transfers between devices, body(): same = lax.ppermute(jac, both, reversed_pairs(to_row_block(0)))  3.87 us
  transfers between devices with their start and end apart: 5, of which 4 were waited for; matrix products, arithmetic and copies ran while one was open for 0% of the time, Pallas kernels for 0%

profile of v3, /device:TPU:1, one launch (start us, length us, event | category | flops | bytes accessed | tf_op | source)
XLA Modules:
  0.0 94.1 jit_solution(6469762208068500789)
XLA Ops:
  0.6 0.8 pad_maximum_fusion
  1.4 11.1 %all_to_all.20.jac_ref = bf16[8,32,128]{2,1,0:T(8,128)(2,1)} all-to-all(bf16[8,32,128]{2,1,0:T(8,128)(2,1)S(1)} %broadcast_in_dim.12), channel_id=1, replica_groups=mesh['row'=32,'col'=8] {'col'}, dimensions={0} | all-to-all | bytes 131072 | tf_op jit(solution)/shard_map/all_to_all | solution.py:294
  12.5 4.2 %product.1 = f32[32,32,128]{2,1,0:T(8,128)} custom-call(bf16[8,32,128]{2,1,0:T(8,128)(2,1)} %all_to_all.20.jac_ref, f32[512,2048]{1,0:T(8,128)} %cov_ref.3), custom_call_target="tpu_custom_call" | custom-call | tf_op jit(solution)/shard_map/product/pallas_call | solution.py:109
  16.7 10.7 %all-to-all-start.1 = ((f32[32,32,128]{2,1,0:T(8,128)}), f32[32,32,128]{2,1,0:T(8,128)S(1)}, u32[]{:S(2)}, u32[]{:S(2)}) async-start(f32[32,32,128]{2,1,0:T(8,128)} %product.1), calls=%async_computation.1 | async-start | bytes 1048576 | tf_op jit(solution)/shard_map/all_to_all | solution.py:294
  27.4 7.1 %collective-permute-start.1 = (bf16[32,128]{1,0:T(8,128)(2,1)S(1)}, bf16[32,128]{1,0:T(8,128)(2,1)S(1)}, u32[]{:S(2)}, u32[]{:S(2)}) collective-permute-start(bf16[32,128]{1,0:T(8,128)(2,1)S(1)} %pad_maximum_fusion), channel_id=1, source_target_pairs={{13,0},{61,1},{12,8},{60,9},{21,16},{37,17},{20,24},{36,25},{29,32... | collective-permute-start | bytes 24584 | tf_op jit(solution)/shard_map/ppermute | solution.py:302
  34.4 0.0 collective-permute-start
  34.5 3.3 %collective-permute-done.1.other_ref = bf16[32,128]{1,0:T(8,128)(2,1)S(1)} collective-permute-done((bf16[32,128]{1,0:T(8,128)(2,1)S(1)}, bf16[32,128]{1,0:T(8,128)(2,1)S(1)}, u32[]{:S(2)}, u32[]{:S(2)}) %collective-permute-start.1) | collective-permute-done | bytes 8224 | tf_op jit(solution)/shard_map/ppermute | solution.py:302
  37.7 3.9 %collective-permute-done.same_ref = bf16[32,128]{1,0:T(8,128)(2,1)S(1)} collective-permute-done((bf16[32,128]{1,0:T(8,128)(2,1)S(1)}, bf16[32,128]{1,0:T(8,128)(2,1)S(1)}, u32[]{:S(2)}, u32[]{:S(2)}) %collective-permute-start) | collective-permute-done | bytes 8224 | tf_op jit(solution)/shard_map/ppermute | solution.py:301
  41.6 0.4 all-to-all-done.1.parts_ref
  42.0 1.2 %reduce.1 = (f32[32,48,128]{2,1,0:T(8,128)}, f32[32,128]{1,0:T(8,128)S(1)}) custom-call(f32[32,32,128]{2,1,0:T(8,128)S(1)} %all-to-all-done.1.parts_ref, bf16[32,128]{1,0:T(8,128)(2,1)S(1)} %collective-permute-done.same_ref, bf16[32,128]{1,0:T(8,128)(2,1)S(1)} %collective-permute-done.1.other_ref), custom_call_target="tpu_custom_call" | custom-call | tf_op jit(solution)/shard_map/reduce/pallas_call | solution.py:138
  43.2 7.8 %all-to-all-start.2 = ((f32[32,48,128]{2,1,0:T(8,128)}), f32[32,48,128]{2,1,0:T(8,128)S(1)}, u32[]{:S(2)}, u32[]{:S(2)}) async-start(f32[32,48,128]{2,1,0:T(8,128)} %get-tuple-element.6), calls=%async_computation.2 | async-start | bytes 1572864 | tf_op jit(solution)/shard_map/all_to_all | solution.py:294
  51.0 5.8 %collective-permute-start.2 = (f32[32,128]{1,0:T(8,128)S(1)}, f32[32,128]{1,0:T(8,128)S(1)}, u32[]{:S(2)}, u32[]{:S(2)}) collective-permute-start(f32[32,128]{1,0:T(8,128)S(1)} %get-tuple-element.7), channel_id=1, source_target_pairs={{0,12},{1,60},{8,13},{9,61},{16,20},{17,36},{24,21},{25,37},{32,28... | collective-permute-start | bytes 49160 | tf_op jit(solution)/shard_map/ppermute | solution.py:307
  56.8 15.0 %collective-permute-done.2.natural_ref = f32[32,128]{1,0:T(8,128)S(1)} collective-permute-done((f32[32,128]{1,0:T(8,128)S(1)}, f32[32,128]{1,0:T(8,128)S(1)}, u32[]{:S(2)}, u32[]{:S(2)}) %collective-permute-start.2) | collective-permute-done | bytes 16416 | tf_op jit(solution)/shard_map/ppermute | solution.py:307
  71.8 0.0 all-to-all-done.2.parts_ref.cols_ref
  71.8 0.0 copy-start
  71.9 14.1 %all_to_all.21.rows_ref = f32[8,64,128]{2,1,0:T(8,128)} all-to-all(f32[8,64,128]{2,1,0:T(8,128)S(1)} %spread.1), channel_id=1, replica_groups=mesh['row'=32,'col'=8] {'col'}, dimensions={0} | all-to-all | bytes 524288 | tf_op jit(solution)/shard_map/all_to_all | solution.py:294
  86.0 0.0 copy-done
  86.0 8.1 %update.1 = (f32[512,2048]{1,0:T(8,128)}, f32[1,64]{1,0:T(1,128)}) custom-call(f32[512,2048]{1,0:T(8,128)} %cov_ref.3, f32[32,48,128]{2,1,0:T(8,128)} %copy-done, f32[8,64,128]{2,1,0:T(8,128)} %all_to_all.21.rows_ref, f32[1,32]{1,0:T(1,128)} %bitcast.3, f32[1,32]{1,0:T(1,128)} %bitcast.4), custom_call_target="tpu_custom_call" | custom-call | tf_op jit(solution)/shard_map/update/pallas_call | solution.py:275
  (2 shorter events, 0.0 us)
Async XLA Ops:
  16.7 25.3 %all-to-all-start.1 = ((f32[32,32,128]{2,1,0:T(8,128)}), f32[32,32,128]{2,1,0:T(8,128)S(1)}, u32[]{:S(2)}, u32[]{:S(2)}) async-start(f32[32,32,128]{2,1,0:T(8,128)} %product.1), calls=%async_computation.1 | async-start | bytes 1048576 | tf_op jit(solution)/shard_map/all_to_all | solution.py:294
  27.4 10.4 %collective-permute-start.1 = (bf16[32,128]{1,0:T(8,128)(2,1)S(1)}, bf16[32,128]{1,0:T(8,128)(2,1)S(1)}, u32[]{:S(2)}, u32[]{:S(2)}) collective-permute-start(bf16[32,128]{1,0:T(8,128)(2,1)S(1)} %pad_maximum_fusion), channel_id=1, source_target_pairs={{13,0},{61,1},{12,8},{60,9},{21,16},{37,17},{20,24},{36,25},{29,32... | collective-permute-start | bytes 24584 | tf_op jit(solution)/shard_map/ppermute | solution.py:302
  34.4 7.2 %collective-permute-start = (bf16[32,128]{1,0:T(8,128)(2,1)S(1)}, bf16[32,128]{1,0:T(8,128)(2,1)S(1)}, u32[]{:S(2)}, u32[]{:S(2)}) collective-permute-start(bf16[32,128]{1,0:T(8,128)(2,1)S(1)} %pad_maximum_fusion), channel_id=1, source_target_pairs={{12,0},{60,1},{13,8},{61,9},{20,16},{36,17},{21,24},{37,25},{28,32... | collective-permute-start | bytes 24584 | tf_op jit(solution)/shard_map/ppermute | solution.py:301
  43.2 28.6 %all-to-all-start.2 = ((f32[32,48,128]{2,1,0:T(8,128)}), f32[32,48,128]{2,1,0:T(8,128)S(1)}, u32[]{:S(2)}, u32[]{:S(2)}) async-start(f32[32,48,128]{2,1,0:T(8,128)} %get-tuple-element.6), calls=%async_computation.2 | async-start | bytes 1572864 | tf_op jit(solution)/shard_map/all_to_all | solution.py:294
  51.0 20.9 %collective-permute-start.2 = (f32[32,128]{1,0:T(8,128)S(1)}, f32[32,128]{1,0:T(8,128)S(1)}, u32[]{:S(2)}, u32[]{:S(2)}) collective-permute-start(f32[32,128]{1,0:T(8,128)S(1)} %get-tuple-element.7), channel_id=1, source_target_pairs={{0,12},{1,60},{8,13},{9,61},{16,20},{17,36},{24,21},{25,37},{32,28... | collective-permute-start | bytes 49160 | tf_op jit(solution)/shard_map/ppermute | solution.py:307
  71.8 14.1 %copy-start = (f32[32,48,128]{2,1,0:T(8,128)}, f32[32,48,128]{2,1,0:T(8,128)S(1)}, u32[]{:S(2)}) copy-start(f32[32,48,128]{2,1,0:T(8,128)S(1)} %all-to-all-done.2.parts_ref.cols_ref) | copy-start | bytes 2359300

commit v4 on v3

--- a/solution.py
+++ b/solution.py
@@ -18,14 +18,14 @@
     return (x * 8 + z) * 8 + y * 2 + k
 
 
-def to_row_block(swap):
+def to_row_block():
     pairs = []
     for x in range(4):
         for y in range(4):
             for z in range(8):
                 for k in range(2):
                     i = ((z + 2 + 4 * k) % 8) // 2
-                    target = device(y, (x + 2) % 4, 4 * k + i, (z + swap) % 2)
+                    target = device(y, (x + 2) % 4, 4 * k + i, z % 2)
                     pairs.append((device(x, y, z, k), target))
     return pairs
 
@@ -88,16 +88,52 @@
     return pltpu.CompilerParams(vmem_limit_bytes=int(mib * 1048576))
 
 
-def product_kernel(jac_ref, cov_ref, out_ref, held_ref, sems):
-    copies = start_loading(cov_ref, held_ref, sems)
-    core = lax.rem(lax.axis_index("col"), 2)
-    jac = jnp.concatenate(
-        [paired(jac_ref[2 * q], jac_ref[2 * q + 1]) for q in range(4)], axis=1
-    )
+EARLY = 3
+
+
+def load_kernel(cov_ref, out_ref, sems):
+    copies = [
+        pltpu.make_async_copy(group_of(cov_ref, g), out_ref.at[g], sems.at[g])
+        for g in range(EARLY)
+    ]
+    for copy in copies:
+        copy.start()
+    for copy in copies:
+        copy.wait()
+
+
+def load(cov):
+    return pl.pallas_call(
+        load_kernel,
+        in_specs=[HBM],
+        out_specs=VMEM,
+        out_shape=jax.ShapeDtypeStruct((EARLY, 512, GROUP), f32),
+        scratch_shapes=[pltpu.SemaphoreType.DMA((EARLY,))],
+        compiler_params=params(16),
+        name="load",
+    )(cov)
+
+
+def product_kernel(jac_ref, early_ref, cov_ref, out_ref, own_ref, late_ref, sems):
+    copies = [
+        pltpu.make_async_copy(group_of(cov_ref, g), late_ref.at[g - EARLY], sems.at[g - EARLY])
+        for g in range(EARLY, GROUPS)
+    ]
+    for copy in copies:
+        copy.start()
+    col = lax.axis_index("col")
+    core = lax.rem(col, 2)
+    blocks = [paired(jac_ref[2 * q], jac_ref[2 * q + 1]) for q in range(4)]
+    own = blocks[0]
+    for q in range(1, 4):
+        own = jnp.where(col // 2 == q, blocks[q], own)
+    own_ref[...] = own
+    jac = jnp.concatenate(blocks, axis=1)
     dims = ((1,), (0,))
     for group in range(GROUPS):
-        copies[group].wait()
-        hi, low = halves(held_ref[group])
+        if group >= EARLY:
+            copies[group - EARLY].wait()
+        hi, low = halves(early_ref[group] if group < EARLY else late_ref[group - EARLY])
         part = dot(jac, low, dims) + dot(jac, hi, dims)
         for step in range(GROUP // 128):
             for h in range(2):
@@ -105,47 +141,67 @@
                 out_ref[place] = part[32 * h : 32 * h + 32, 128 * step : 128 * step + 128]
 
 
-def product(jac, cov):
+def product(jac, early, cov):
     return pl.pallas_call(
         product_kernel,
-        in_specs=[VMEM, HBM],
-        out_specs=VMEM,
-        out_shape=jax.ShapeDtypeStruct((32, 32, 128), f32),
+        in_specs=[VMEM, VMEM, HBM],
+        out_specs=[VMEM] * 2,
+        out_shape=[
+            jax.ShapeDtypeStruct((32, 32, 128), f32),
+            jax.ShapeDtypeStruct((64, 128), bf16),
+        ],
         scratch_shapes=[
-            pltpu.VMEM((GROUPS, 512, GROUP), f32),
-            pltpu.SemaphoreType.DMA((GROUPS,)),
-        ],
-        compiler_params=params(60.25),
+            pltpu.VMEM((GROUPS - EARLY, 512, GROUP), f32),
+            pltpu.SemaphoreType.DMA((GROUPS - EARLY,)),
+        ],
+        compiler_params=params(16),
         name="product",
-    )(jac, cov)
-
-
-def reduce_kernel(parts_ref, same_ref, other_ref, row_ref, own_ref):
+    )(jac, early, cov)
+
+
+def reduce_kernel(parts_ref, jac_ref, own_ref, kept_ref, sent_ref):
     total = jnp.sum(parts_ref[...], axis=0)
     own_ref[...] = total
-    second = lax.rem(lax.axis_index("row"), 2) == 1
-    same, other = same_ref[...].astype(f32), other_ref[...].astype(f32)
-    jac = paired(jnp.where(second, other, same), jnp.where(second, same, other))
     dims = ((1,), (1,))
     hi, mid, low = thirds(total)
+    jac = jac_ref[...]
     gram = dot(jac, low, dims) + dot(jac, mid, dims) + dot(jac, hi, dims)
     packed = jnp.concatenate([gram[16 * q : 16 * q + 16] for q in range(4)], axis=1)
-    row_ref[:, :32] = jnp.broadcast_to(total[None], (32, 32, 128))
-    row_ref[:, 32:] = jnp.broadcast_to(packed[None], (32, 16, 128))
-
-
-def reduce(parts, same, other):
+    first = lax.rem(lax.axis_index("col"), 2) == 0
+    kept_ref[...] = jnp.where(first, packed[:8], packed[8:])
+    sent_ref[...] = jnp.where(first, packed[8:], packed[:8])
+
+
+def reduce(parts, jac):
     return pl.pallas_call(
         reduce_kernel,
-        in_specs=[VMEM] * 3,
-        out_specs=[VMEM] * 2,
+        in_specs=[VMEM] * 2,
+        out_specs=[VMEM] * 3,
         out_shape=[
-            jax.ShapeDtypeStruct((32, 48, 128), f32),
             jax.ShapeDtypeStruct((32, 128), f32),
+            jax.ShapeDtypeStruct((8, 128), f32),
+            jax.ShapeDtypeStruct((8, 128), f32),
         ],
         compiler_params=params(8),
         name="reduce",
-    )(parts, same, other)
+    )(parts, jac)
+
+
+def fill_kernel(own_ref, kept_ref, got_ref, out_ref):
+    out_ref[:, :32] = jnp.broadcast_to(own_ref[...][None], (32, 32, 128))
+    gram = kept_ref[...] + got_ref[...]
+    out_ref[:, 32:] = jnp.broadcast_to(gram[None], (32, 8, 128))
+
+
+def fill(own, kept, got):
+    return pl.pallas_call(
+        fill_kernel,
+        in_specs=[VMEM] * 3,
+        out_specs=VMEM,
+        out_shape=jax.ShapeDtypeStruct((32, 40, 128), f32),
+        compiler_params=params(8),
+        name="fill",
+    )(own, kept, got)
 
 
 def spread_kernel(parts_ref, natural_ref, out_ref):
@@ -154,7 +210,7 @@
         total = parts_ref[h, 32:]
         for t in range(1, 16):
             total = total + parts_ref[2 * t + h, 32:]
-        out_ref[:, 32 + 16 * h : 48 + 16 * h] = jnp.broadcast_to(total[None], (8, 16, 128))
+        out_ref[:, 32 + 8 * h : 40 + 8 * h] = jnp.broadcast_to(total[None], (8, 8, 128))
 
 
 def spread(parts, natural):
@@ -162,7 +218,7 @@
         spread_kernel,
         in_specs=[VMEM] * 2,
         out_specs=VMEM,
-        out_shape=jax.ShapeDtypeStruct((8, 64, 128), f32),
+        out_shape=jax.ShapeDtypeStruct((8, 48, 128), f32),
         compiler_params=params(4),
         name="spread",
     )(parts, natural)
@@ -171,8 +227,7 @@
 PANEL = 8
 
 
-def inverse_factor(total):
-    first, second = total[:16], total[16:]
+def inverse_factor(first, second):
     left = jnp.concatenate([first[:, 32 * q : 32 * q + 32] for q in range(4)], axis=0)
     right = jnp.concatenate([second[:, 32 * q : 32 * q + 32] for q in range(4)], axis=0)
     gram = jnp.concatenate([left, right, jnp.zeros((64, 64), f32)], axis=1)
@@ -214,10 +269,18 @@
     loads = start_loading(cov_ref, held_ref, in_sems)
     col = lax.axis_index("col")
     core = lax.rem(col, 2)
-    total = rows_ref[0, 32:]
-    for c in range(1, 8):
-        total = total + rows_ref[c, 32:]
-    inverse = inverse_factor(total)
+    first, second = [
+        jnp.concatenate(
+            [
+                sum(rows_ref[2 * y + k, 32 + 8 * h : 40 + 8 * h] for y in range(1, 4))
+                + rows_ref[k, 32 + 8 * h : 40 + 8 * h]
+                for k in range(2)
+            ],
+            axis=0,
+        )
+        for h in range(2)
+    ]
+    inverse = inverse_factor(first, second)
     hi, mid, low = thirds(inverse)
     inverse_parts = jnp.concatenate([hi, hi, hi, mid, mid, low], axis=1)
 
@@ -285,7 +348,7 @@
             pltpu.SemaphoreType.DMA((GROUPS,)),
             pltpu.SemaphoreType.DMA((GROUPS,)),
         ],
-        compiler_params=params(60.25),
+        compiler_params=params(16),
         name="update",
     )(cov, cols, rows, first, second)
 
@@ -298,13 +361,15 @@
     both = ("row", "col")
     jac = jnp.concatenate([first_jacobian, second_jacobian], axis=1)
     jac_rows = exchange(jnp.broadcast_to(jac[None], (8, 32, 128)), "col")
-    same = lax.ppermute(jac, both, reversed_pairs(to_row_block(0)))
-    other = lax.ppermute(jac, both, reversed_pairs(to_row_block(1)))
-    parts = product(jac_rows, covariance)
+    covariance = pltpu.with_memory_space_constraint(covariance, pltpu.HBM)
+    held = load(covariance)
+    parts, jac_own = product(jac_rows, held, covariance)
     parts = exchange(parts, "row")
-    for_row, own = reduce(parts, same, other)
-    cols = exchange(for_row, "row")
-    natural = lax.ppermute(own, both, to_row_block(0))
+    jac_piece = lax.ppermute(jac_own, both, reversed_pairs(to_row_block()))
+    own, kept, sent = reduce(parts, jac_piece)
+    got = lax.ppermute(sent, "col", [(c, c ^ 1) for c in range(8)])
+    cols = exchange(fill(own, kept, got), "row")
+    natural = lax.ppermute(own, both, to_row_block())
     rows = exchange(spread(cols, natural), "col")
     out, increment = update(covariance, cols, rows, first_residuals[None], second_residuals[None])
     return out, increment[0]

time: 94.6 us -> 90 us (0.951)
  blocking collectives: 25.2 us -> 12.3 us
  starting transfers between devices: 31.3 us -> 37.4 us
  waiting for transfers between devices: 22.6 us -> 24.9 us
  Pallas kernels: 13.5 us -> 12 us
  local copies, waits for them, and re-layouts: 0.02 us -> 1.44 us
    all_to_all x2 -> x1, blocking collectives: 25.2 us -> 12.3 us  [exchange(): return lax.all_to_all(array, axis, 0, 0, tiled=True)]
    all_to_all x2 -> x3, starting transfers between devices: 18.4 us -> 22.7 us  [exchange(): return lax.all_to_all(array, axis, 0, 0, tiled=True)]
    all_to_all x2 -> x3, waiting for transfers between devices: 0.43 us -> 3.4 us  [exchange(): return lax.all_to_all(array, axis, 0, 0, tiled=True)]
    ppermute x3, starting transfers between devices: 12.9 us -> 14.7 us  [the longest x1 6.18 us: body(): jac_piece = lax.ppermute(jac_own, both, reversed_pairs(to_row_block()))]
    pallas_call x1, Pallas kernels: 8.15 us -> 6.86 us  [update(): pl.pallas_call(update_kernel, in_specs=[HBM] + [VMEM] * 4, out_specs=[HBM...]
    pallas_call x2 -> x4, Pallas kernels: 5.34 us -> 5.15 us  [the longest x1 2.15 us: product(): pl.pallas_call(product_kernel, in_specs=[VMEM, VMEM, HBM], out_specs=[VME...]
  transfers between devices with their start and end apart: 5 -> 6, of which waited for: 4 -> 5; matrix products, arithmetic and copies ran while one was open for 0% -> 0% of each run, Pallas kernels for 0% -> 2%
where the time goes in v4:
time: 90 us; the launch traced here: 89.5 us
  starting transfers between devices  37.4 us (42%)
  waiting for transfers between devices  24.9 us (28%)
  blocking collectives  12.3 us (14%)
  Pallas kernels  12 us (13%)
  local copies, waits for them, and re-layouts  1.44 us (2%)
    all_to_all x3, starting transfers between devices, exchange(): return lax.all_to_all(array, axis, 0, 0, tiled=True)  22.7 us
    ppermute x1, waiting for transfers between devices, body(): natural = lax.ppermute(own, both, to_row_block())  12.6 us
    all_to_all x1, blocking collectives, exchange(): return lax.all_to_all(array, axis, 0, 0, tiled=True)  12.3 us
    ppermute x1, waiting for transfers between devices, body(): jac_piece = lax.ppermute(jac_own, both, reversed_pairs(to_row_block()))  8.05 us
    pallas_call x1, Pallas kernels, update(): pl.pallas_call(update_kernel, in_specs=[HBM] + [VMEM] * 4, out_specs=[HBM...  6.86 us
    ppermute x1, starting transfers between devices, body(): jac_piece = lax.ppermute(jac_own, both, reversed_pairs(to_row_block()))  6.18 us
    ppermute x1, starting transfers between devices, body(): natural = lax.ppermute(own, both, to_row_block())  5.45 us
    all_to_all x3, waiting for transfers between devices, exchange(): return lax.all_to_all(array, axis, 0, 0, tiled=True)  3.4 us
  transfers between devices with their start and end apart: 6, of which 5 were waited for; matrix products, arithmetic and copies ran while one was open for 0% of the time, Pallas kernels for 2%

profile of v4, /device:TPU:1, one launch (start us, length us, event | category | flops | bytes accessed | tf_op | source)
XLA Modules:
  0.0 89.5 jit_solution(11892841014467866856)
XLA Ops:
  0.6 0.8 pad_maximum_fusion
  1.4 0.6 broadcast_in_dim.12
  2.1 6.5 %all-to-all-start = ((bf16[8,32,128]{2,1,0:T(8,128)(2,1)}), bf16[8,32,128]{2,1,0:T(8,128)(2,1)S(1)}, u32[]{:S(2)}, u32[]{:S(2)}) async-start(bf16[8,32,128]{2,1,0:T(8,128)(2,1)} %broadcast_in_dim.12), calls=%async_computation | async-start | bytes 131072 | tf_op jit(solution)/shard_map/all_to_all | solution.py:357
  8.5 1.9 %load.1.early_ref = f32[3,512,512]{2,1,0:T(8,128)S(1)} custom-call(f32[512,2048]{1,0:T(8,128)} %cov_ref.5), custom_call_target="tpu_custom_call" | custom-call | tf_op jit(solution)/shard_map/load/pallas_call | solution.py:106
  10.4 3.0 %all-to-all-done.jac_ref = bf16[8,32,128]{2,1,0:T(8,128)(2,1)S(1)} async-done(((bf16[8,32,128]{2,1,0:T(8,128)(2,1)}), bf16[8,32,128]{2,1,0:T(8,128)(2,1)S(1)}, u32[]{:S(2)}, u32[]{:S(2)}) %all-to-all-start) | async-done | bytes 65568 | tf_op jit(solution)/shard_map/all_to_all | solution.py:357
  13.4 2.1 %product.1 = (f32[32,32,128]{2,1,0:T(8,128)S(1)}, bf16[64,128]{1,0:T(8,128)(2,1)S(1)}) custom-call(bf16[8,32,128]{2,1,0:T(8,128)(2,1)S(1)} %all-to-all-done.jac_ref, f32[3,512,512]{2,1,0:T(8,128)S(1)} %load.1.early_ref, f32[512,2048]{1,0:T(8,128)} %cov_ref.5), custom_call_target="tpu_custom_call" | custom-call | tf_op jit(solution)/shard_map/product/pallas_call | solution.py:145
  15.5 0.0 copy-start
  15.6 0.8 copy-done
  16.3 0.0 copy-start.1
  16.3 0.0 copy-start.2
  16.3 10.7 %all-to-all-start.1 = ((f32[32,32,128]{2,1,0:T(8,128)}), f32[32,32,128]{2,1,0:T(8,128)S(1)}, u32[]{:S(2)}, u32[]{:S(2)}) async-start(f32[32,32,128]{2,1,0:T(8,128)} %copy-done), calls=%async_computation.1 | async-start | bytes 1048576 | tf_op jit(solution)/shard_map/all_to_all | solution.py:357
  27.0 6.2 %collective-permute-start = (bf16[64,128]{1,0:T(8,128)(2,1)S(1)}, bf16[64,128]{1,0:T(8,128)(2,1)S(1)}, u32[]{:S(2)}, u32[]{:S(2)}) collective-permute-start(bf16[64,128]{1,0:T(8,128)(2,1)S(1)} %get-tuple-element.10), channel_id=1, source_target_pairs={{12,0},{60,1},{13,8},{61,9},{20,16},{36,17},{21,24},{37,25},{28,32... | collective-permute-start | bytes 49160 | tf_op jit(solution)/shard_map/ppermute | solution.py:368
  33.2 8.0 %collective-permute-done.jac_ref = bf16[64,128]{1,0:T(8,128)(2,1)S(1)} collective-permute-done((bf16[64,128]{1,0:T(8,128)(2,1)S(1)}, bf16[64,128]{1,0:T(8,128)(2,1)S(1)}, u32[]{:S(2)}, u32[]{:S(2)}) %collective-permute-start) | collective-permute-done | bytes 16416 | tf_op jit(solution)/shard_map/ppermute | solution.py:368
  41.2 0.4 all-to-all-done.1.parts_ref
  41.7 0.2 reduce.1
  41.9 3.1 %collective-permute-start.1 = (f32[8,128]{1,0:T(8,128)S(1)}, f32[8,128]{1,0:T(8,128)S(1)}, u32[]{:S(2)}, u32[]{:S(2)}) collective-permute-start(f32[8,128]{1,0:T(8,128)S(1)} %get-tuple-element.13), channel_id=1, source_target_pairs={{0,1},{1,0},{2,3},{3,2},{4,5},{5,4},{6,7},{7,6},{8,9},{9,8},{10,11... | collective-permute-start | bytes 12296 | tf_op jit(solution)/shard_map/ppermute | solution.py:370
  45.0 0.8 collective-permute-done.1.got_ref
  45.8 0.9 fill.1
  46.7 5.6 %all-to-all-start.2 = ((f32[32,40,128]{2,1,0:T(8,128)}), f32[32,40,128]{2,1,0:T(8,128)S(1)}, u32[]{:S(2)}, u32[]{:S(2)}) async-start(f32[32,40,128]{2,1,0:T(8,128)} %fill.1), calls=%async_computation.2 | async-start | bytes 1310720 | tf_op jit(solution)/shard_map/all_to_all | solution.py:357
  52.3 5.5 %collective-permute-start.2 = (f32[32,128]{1,0:T(8,128)S(1)}, f32[32,128]{1,0:T(8,128)S(1)}, u32[]{:S(2)}, u32[]{:S(2)}) collective-permute-start(f32[32,128]{1,0:T(8,128)S(1)} %get-tuple-element.11.own_ref), channel_id=1, source_target_pairs={{0,12},{1,60},{8,13},{9,61},{16,20},{17,36},{24,21},{25,37},{32,28... | collective-permute-start | bytes 49160 | tf_op jit(solution)/shard_map/ppermute | solution.py:372
  57.8 12.6 %collective-permute-done.2.natural_ref = f32[32,128]{1,0:T(8,128)S(1)} collective-permute-done((f32[32,128]{1,0:T(8,128)S(1)}, f32[32,128]{1,0:T(8,128)S(1)}, u32[]{:S(2)}, u32[]{:S(2)}) %collective-permute-start.2) | collective-permute-done | bytes 16416 | tf_op jit(solution)/shard_map/ppermute | solution.py:372
  70.4 0.0 all-to-all-done.2.parts_ref.cols_ref
  70.4 12.3 %all_to_all.20.rows_ref = f32[8,48,128]{2,1,0:T(8,128)S(1)} all-to-all(f32[8,48,128]{2,1,0:T(8,128)S(1)} %spread.1), channel_id=1, replica_groups=mesh['row'=32,'col'=8] {'col'}, dimensions={0} | all-to-all | bytes 393216 | tf_op jit(solution)/shard_map/all_to_all | solution.py:357
  82.7 0.0 copy-done.1
  82.7 0.0 copy-done.2
  82.7 6.9 %update.1 = (f32[512,2048]{1,0:T(8,128)}, f32[1,64]{1,0:T(1,128)}) custom-call(f32[512,2048]{1,0:T(8,128)} %cov_ref.5, f32[32,40,128]{2,1,0:T(8,128)S(1)} %all-to-all-done.2.parts_ref.cols_ref, f32[8,48,128]{2,1,0:T(8,128)S(1)} %all_to_all.20.rows_ref, f32[1,32]{1,0:T(1,128)S(1)} %bitcast.3, f32[1,32]{1,0:T(1,128)S(1)} %bitcast.4), custom_call_target="tpu_custom_call" | custom-call | tf_op jit(solution)/shard_map/update/pallas_call | solution.py:338
  (1 shorter events, 0.0 us)
Async XLA Ops:
  2.1 11.3 %all-to-all-start = ((bf16[8,32,128]{2,1,0:T(8,128)(2,1)}), bf16[8,32,128]{2,1,0:T(8,128)(2,1)S(1)}, u32[]{:S(2)}, u32[]{:S(2)}) async-start(bf16[8,32,128]{2,1,0:T(8,128)(2,1)} %broadcast_in_dim.12), calls=%async_computation | async-start | bytes 131072 | tf_op jit(solution)/shard_map/all_to_all | solution.py:357
  15.5 0.8 copy-start
  16.3 66.3 %copy-start.1 = (f32[32]{0:T(128)S(1)}, f32[32]{0:T(128)}, u32[]{:S(2)}) copy-start(f32[32]{0:T(128)} %param.8) | copy-start | bytes 388
  16.3 66.3 %copy-start.2 = (f32[32]{0:T(128)S(1)}, f32[32]{0:T(128)}, u32[]{:S(2)}) copy-start(f32[32]{0:T(128)} %param.9) | copy-start | bytes 388
  16.3 25.3 %all-to-all-start.1 = ((f32[32,32,128]{2,1,0:T(8,128)}), f32[32,32,128]{2,1,0:T(8,128)S(1)}, u32[]{:S(2)}, u32[]{:S(2)}) async-start(f32[32,32,128]{2,1,0:T(8,128)} %copy-done), calls=%async_computation.1 | async-start | bytes 1048576 | tf_op jit(solution)/shard_map/all_to_all | solution.py:357
  27.0 14.2 %collective-permute-start = (bf16[64,128]{1,0:T(8,128)(2,1)S(1)}, bf16[64,128]{1,0:T(8,128)(2,1)S(1)}, u32[]{:S(2)}, u32[]{:S(2)}) collective-permute-start(bf16[64,128]{1,0:T(8,128)(2,1)S(1)} %get-tuple-element.10), channel_id=1, source_target_pairs={{12,0},{60,1},{13,8},{61,9},{20,16},{36,17},{21,24},{37,25},{28,32... | collective-permute-start | bytes 49160 | tf_op jit(solution)/shard_map/ppermute | solution.py:368
  41.9 3.9 %collective-permute-start.1 = (f32[8,128]{1,0:T(8,128)S(1)}, f32[8,128]{1,0:T(8,128)S(1)}, u32[]{:S(2)}, u32[]{:S(2)}) collective-permute-start(f32[8,128]{1,0:T(8,128)S(1)} %get-tuple-element.13), channel_id=1, source_target_pairs={{0,1},{1,0},{2,3},{3,2},{4,5},{5,4},{6,7},{7,6},{8,9},{9,8},{10,11... | collective-permute-start | bytes 12296 | tf_op jit(solution)/shard_map/ppermute | solution.py:370
  46.7 23.7 %all-to-all-start.2 = ((f32[32,40,128]{2,1,0:T(8,128)}), f32[32,40,128]{2,1,0:T(8,128)S(1)}, u32[]{:S(2)}, u32[]{:S(2)}) async-start(f32[32,40,128]{2,1,0:T(8,128)} %fill.1), calls=%async_computation.2 | async-start | bytes 1310720 | tf_op jit(solution)/shard_map/all_to_all | solution.py:357
  52.3 18.1 %collective-permute-start.2 = (f32[32,128]{1,0:T(8,128)S(1)}, f32[32,128]{1,0:T(8,128)S(1)}, u32[]{:S(2)}, u32[]{:S(2)}) collective-permute-start(f32[32,128]{1,0:T(8,128)S(1)} %get-tuple-element.11.own_ref), channel_id=1, source_target_pairs={{0,12},{1,60},{8,13},{9,61},{16,20},{17,36},{24,21},{25,37},{32,28... | collective-permute-start | bytes 49160 | tf_op jit(solution)/shard_map/ppermute | solution.py:372

commit v5 on v4

--- a/solution.py
+++ b/solution.py
@@ -18,14 +18,14 @@
     return (x * 8 + z) * 8 + y * 2 + k
 
 
-def to_row_block():
+def to_row_block(swap):
     pairs = []
     for x in range(4):
         for y in range(4):
             for z in range(8):
                 for k in range(2):
                     i = ((z + 2 + 4 * k) % 8) // 2
-                    target = device(y, (x + 2) % 4, 4 * k + i, z % 2)
+                    target = device(y, (x + 2) % 4, 4 * k + i, (z + swap) % 2)
                     pairs.append((device(x, y, z, k), target))
     return pairs
 
@@ -86,6 +86,26 @@
 
 def params(mib):
     return pltpu.CompilerParams(vmem_limit_bytes=int(mib * 1048576))
+
+
+def pack_kernel(first_ref, second_ref, out_ref, copies_ref):
+    jac = jnp.concatenate([first_ref[...], second_ref[...]], axis=1)
+    out_ref[...] = jac
+    copies_ref[...] = jnp.broadcast_to(jac[None], (8, 32, 128))
+
+
+def pack(first, second):
+    return pl.pallas_call(
+        pack_kernel,
+        in_specs=[VMEM] * 2,
+        out_specs=[VMEM] * 2,
+        out_shape=[
+            jax.ShapeDtypeStruct((32, 128), bf16),
+            jax.ShapeDtypeStruct((8, 32, 128), bf16),
+        ],
+        compiler_params=params(4),
+        name="pack",
+    )(first, second)
 
 
 EARLY = 3
@@ -114,20 +134,15 @@
     )(cov)
 
 
-def product_kernel(jac_ref, early_ref, cov_ref, out_ref, own_ref, late_ref, sems):
+def product_kernel(jac_ref, early_ref, cov_ref, out_ref, late_ref, sems):
     copies = [
         pltpu.make_async_copy(group_of(cov_ref, g), late_ref.at[g - EARLY], sems.at[g - EARLY])
         for g in range(EARLY, GROUPS)
     ]
     for copy in copies:
         copy.start()
-    col = lax.axis_index("col")
-    core = lax.rem(col, 2)
+    core = lax.rem(lax.axis_index("col"), 2)
     blocks = [paired(jac_ref[2 * q], jac_ref[2 * q + 1]) for q in range(4)]
-    own = blocks[0]
-    for q in range(1, 4):
-        own = jnp.where(col // 2 == q, blocks[q], own)
-    own_ref[...] = own
     jac = jnp.concatenate(blocks, axis=1)
     dims = ((1,), (0,))
     for group in range(GROUPS):
@@ -145,11 +160,8 @@
     return pl.pallas_call(
         product_kernel,
         in_specs=[VMEM, VMEM, HBM],
-        out_specs=[VMEM] * 2,
-        out_shape=[
-            jax.ShapeDtypeStruct((32, 32, 128), f32),
-            jax.ShapeDtypeStruct((64, 128), bf16),
-        ],
+        out_specs=VMEM,
+        out_shape=jax.ShapeDtypeStruct((32, 32, 128), f32),
         scratch_shapes=[
             pltpu.VMEM((GROUPS - EARLY, 512, GROUP), f32),
             pltpu.SemaphoreType.DMA((GROUPS - EARLY,)),
@@ -159,12 +171,14 @@
     )(jac, early, cov)
 
 
-def reduce_kernel(parts_ref, jac_ref, own_ref, kept_ref, sent_ref):
+def reduce_kernel(parts_ref, same_ref, other_ref, own_ref, kept_ref, sent_ref):
     total = jnp.sum(parts_ref[...], axis=0)
     own_ref[...] = total
     dims = ((1,), (1,))
     hi, mid, low = thirds(total)
-    jac = jac_ref[...]
+    second = lax.rem(lax.axis_index("row"), 2) == 1
+    same, other = same_ref[...].astype(f32), other_ref[...].astype(f32)
+    jac = paired(jnp.where(second, other, same), jnp.where(second, same, other))
     gram = dot(jac, low, dims) + dot(jac, mid, dims) + dot(jac, hi, dims)
     packed = jnp.concatenate([gram[16 * q : 16 * q + 16] for q in range(4)], axis=1)
     first = lax.rem(lax.axis_index("col"), 2) == 0
@@ -172,10 +186,10 @@
     sent_ref[...] = jnp.where(first, packed[8:], packed[:8])
 
 
-def reduce(parts, jac):
+def reduce(parts, same, other):
     return pl.pallas_call(
         reduce_kernel,
-        in_specs=[VMEM] * 2,
+        in_specs=[VMEM] * 3,
         out_specs=[VMEM] * 3,
         out_shape=[
             jax.ShapeDtypeStruct((32, 128), f32),
@@ -184,7 +198,7 @@
         ],
         compiler_params=params(8),
         name="reduce",
-    )(parts, jac)
+    )(parts, same, other)
 
 
 def fill_kernel(own_ref, kept_ref, got_ref, out_ref):
@@ -359,17 +373,21 @@
 
 def body(covariance, first_jacobian, second_jacobian, first_residuals, second_residuals):
     both = ("row", "col")
-    jac = jnp.concatenate([first_jacobian, second_jacobian], axis=1)
-    jac_rows = exchange(jnp.broadcast_to(jac[None], (8, 32, 128)), "col")
-    covariance = pltpu.with_memory_space_constraint(covariance, pltpu.HBM)
+    covariance, first_jacobian, second_jacobian = [
+        pltpu.with_memory_space_constraint(array, pltpu.HBM)
+        for array in (covariance, first_jacobian, second_jacobian)
+    ]
+    jac, jac_copies = pack(first_jacobian, second_jacobian)
+    jac_rows = exchange(jac_copies, "col")
+    same = lax.ppermute(jac, both, reversed_pairs(to_row_block(0)))
+    other = lax.ppermute(jac, both, reversed_pairs(to_row_block(1)))
     held = load(covariance)
-    parts, jac_own = product(jac_rows, held, covariance)
+    parts = product(jac_rows, held, covariance)
     parts = exchange(parts, "row")
-    jac_piece = lax.ppermute(jac_own, both, reversed_pairs(to_row_block()))
-    own, kept, sent = reduce(parts, jac_piece)
+    own, kept, sent = reduce(parts, same, other)
     got = lax.ppermute(sent, "col", [(c, c ^ 1) for c in range(8)])
     cols = exchange(fill(own, kept, got), "row")
-    natural = lax.ppermute(own, both, to_row_block())
+    natural = lax.ppermute(own, both, to_row_block(0))
     rows = exchange(spread(cols, natural), "col")
     out, increment = update(covariance, cols, rows, first_residuals[None], second_residuals[None])
     return out, increment[0]

time: 90 us -> 90 us (level)
  Pallas kernels: 12 us -> 13.5 us
    pallas_call x2 -> x3, Pallas kernels: 2.38 us -> 3.84 us  [the longest x1 2.15 us: product(): pl.pallas_call(product_kernel, in_specs=[VMEM, VMEM, HBM], out_specs=VMEM...]
    ppermute x2 -> x3, starting transfers between devices: 11.6 us -> 12.4 us  [the longest x1 7.07 us: body(): other = lax.ppermute(jac, both, reversed_pairs(to_row_block(1)))]
    ppermute x2 -> x3, waiting for transfers between devices: 20.7 us -> 19.9 us  [the longest x1 12.8 us: body(): natural = lax.ppermute(own, both, to_row_block(0))]
  transfers between devices with their start and end apart: 6 -> 7, of which waited for: 5 -> 6; matrix products, arithmetic and copies ran while one was open for 0% -> 0% of each run, Pallas kernels for 2% -> 2%
where the time goes in v5:
time: 90 us; the launch traced here: 89.6 us
  starting transfers between devices  38.2 us (42%)
  waiting for transfers between devices  24.2 us (27%)
  Pallas kernels  13.5 us (15%)
  blocking collectives  12.3 us (14%)
    all_to_all x3, starting transfers between devices, exchange(): return lax.all_to_all(array, axis, 0, 0, tiled=True)  22.8 us
    ppermute x1, waiting for transfers between devices, body(): natural = lax.ppermute(own, both, to_row_block(0))  12.8 us
    all_to_all x1, blocking collectives, exchange(): return lax.all_to_all(array, axis, 0, 0, tiled=True)  12.3 us
    ppermute x1, starting transfers between devices, body(): other = lax.ppermute(jac, both, reversed_pairs(to_row_block(1)))  7.07 us
    pallas_call x1, Pallas kernels, update(): pl.pallas_call(update_kernel, in_specs=[HBM] + [VMEM] * 4, out_specs=[HBM...  6.86 us
    ppermute x1, starting transfers between devices, body(): natural = lax.ppermute(own, both, to_row_block(0))  5.29 us
    ppermute x1, waiting for transfers between devices, body(): same = lax.ppermute(jac, both, reversed_pairs(to_row_block(0)))  3.88 us
    all_to_all x3, waiting for transfers between devices, exchange(): return lax.all_to_all(array, axis, 0, 0, tiled=True)  3.39 us
  transfers between devices with their start and end apart: 7, of which 6 were waited for; matrix products, arithmetic and copies ran while one was open for 0% of the time, Pallas kernels for 2%

profile of v5, /device:TPU:1, one launch (start us, length us, event | category | flops | bytes accessed | tf_op | source)
XLA Modules:
  0.0 89.6 jit_solution(14372146516589677470)
XLA Ops:
  0.6 1.4 %pack.1 = (bf16[32,128]{1,0:T(8,128)(2,1)S(1)}, bf16[8,32,128]{2,1,0:T(8,128)(2,1)}) custom-call(bf16[32,64]{1,0:T(8,128)(2,1)} %first_ref.1, bf16[32,64]{1,0:T(8,128)(2,1)} %second_ref.1), custom_call_target="tpu_custom_call" | custom-call | tf_op jit(solution)/shard_map/pack/pallas_call | solution.py:98
  2.1 6.5 %all-to-all-start = ((bf16[8,32,128]{2,1,0:T(8,128)(2,1)}), bf16[8,32,128]{2,1,0:T(8,128)(2,1)S(1)}, u32[]{:S(2)}, u32[]{:S(2)}) async-start(bf16[8,32,128]{2,1,0:T(8,128)(2,1)} %get-tuple-element.9), calls=%async_computation | async-start | bytes 131072 | tf_op jit(solution)/shard_map/all_to_all | solution.py:371
  8.5 1.9 %load.1.early_ref = f32[3,512,512]{2,1,0:T(8,128)S(1)} custom-call(f32[512,2048]{1,0:T(8,128)} %cov_ref.5), custom_call_target="tpu_custom_call" | custom-call | tf_op jit(solution)/shard_map/load/pallas_call | solution.py:126
  10.4 3.0 %all-to-all-done.jac_ref = bf16[8,32,128]{2,1,0:T(8,128)(2,1)S(1)} async-done(((bf16[8,32,128]{2,1,0:T(8,128)(2,1)}), bf16[8,32,128]{2,1,0:T(8,128)(2,1)S(1)}, u32[]{:S(2)}, u32[]{:S(2)}) %all-to-all-start) | async-done | bytes 65568 | tf_op jit(solution)/shard_map/all_to_all | solution.py:371
  13.4 2.1 %product.1 = f32[32,32,128]{2,1,0:T(8,128)S(1)} custom-call(bf16[8,32,128]{2,1,0:T(8,128)(2,1)S(1)} %all-to-all-done.jac_ref, f32[3,512,512]{2,1,0:T(8,128)S(1)} %load.1.early_ref, f32[512,2048]{1,0:T(8,128)} %cov_ref.5), custom_call_target="tpu_custom_call" | custom-call | tf_op jit(solution)/shard_map/product/pallas_call | solution.py:160
  15.5 0.0 copy-start
  15.5 0.8 copy-done
  16.3 0.0 copy-start.1
  16.3 0.0 copy-start.2
  16.3 10.7 %all-to-all-start.1 = ((f32[32,32,128]{2,1,0:T(8,128)}), f32[32,32,128]{2,1,0:T(8,128)S(1)}, u32[]{:S(2)}, u32[]{:S(2)}) async-start(f32[32,32,128]{2,1,0:T(8,128)} %copy-done), calls=%async_computation.1 | async-start | bytes 1048576 | tf_op jit(solution)/shard_map/all_to_all | solution.py:371
  27.0 7.1 %collective-permute-start.1 = (bf16[32,128]{1,0:T(8,128)(2,1)S(1)}, bf16[32,128]{1,0:T(8,128)(2,1)S(1)}, u32[]{:S(2)}, u32[]{:S(2)}) collective-permute-start(bf16[32,128]{1,0:T(8,128)(2,1)S(1)} %get-tuple-element.10), channel_id=1, source_target_pairs={{13,0},{61,1},{12,8},{60,9},{21,16},{37,17},{20,24},{36,25},{29,32... | collective-permute-start | bytes 24584 | tf_op jit(solution)/shard_map/ppermute | solution.py:383
  34.1 0.0 collective-permute-start
  34.1 3.3 %collective-permute-done.1.other_ref = bf16[32,128]{1,0:T(8,128)(2,1)S(1)} collective-permute-done((bf16[32,128]{1,0:T(8,128)(2,1)S(1)}, bf16[32,128]{1,0:T(8,128)(2,1)S(1)}, u32[]{:S(2)}, u32[]{:S(2)}) %collective-permute-start.1) | collective-permute-done | bytes 8224 | tf_op jit(solution)/shard_map/ppermute | solution.py:383
  37.4 3.9 %collective-permute-done.same_ref = bf16[32,128]{1,0:T(8,128)(2,1)S(1)} collective-permute-done((bf16[32,128]{1,0:T(8,128)(2,1)S(1)}, bf16[32,128]{1,0:T(8,128)(2,1)S(1)}, u32[]{:S(2)}, u32[]{:S(2)}) %collective-permute-start) | collective-permute-done | bytes 8224 | tf_op jit(solution)/shard_map/ppermute | solution.py:382
  41.2 0.4 all-to-all-done.1.parts_ref
  41.6 0.3 reduce.1
  41.9 3.0 %collective-permute-start.2 = (f32[8,128]{1,0:T(8,128)S(1)}, f32[8,128]{1,0:T(8,128)S(1)}, u32[]{:S(2)}, u32[]{:S(2)}) collective-permute-start(f32[8,128]{1,0:T(8,128)S(1)} %get-tuple-element.13), channel_id=1, source_target_pairs={{0,1},{1,0},{2,3},{3,2},{4,5},{5,4},{6,7},{7,6},{8,9},{9,8},{10,11... | collective-permute-start | bytes 12296 | tf_op jit(solution)/shard_map/ppermute | solution.py:388
  45.0 0.8 collective-permute-done.2.got_ref
  45.8 0.9 fill.1
  46.7 5.7 %all-to-all-start.2 = ((f32[32,40,128]{2,1,0:T(8,128)}), f32[32,40,128]{2,1,0:T(8,128)S(1)}, u32[]{:S(2)}, u32[]{:S(2)}) async-start(f32[32,40,128]{2,1,0:T(8,128)} %fill.1), calls=%async_computation.2 | async-start | bytes 1310720 | tf_op jit(solution)/shard_map/all_to_all | solution.py:371
  52.3 5.3 %collective-permute-start.3 = (f32[32,128]{1,0:T(8,128)S(1)}, f32[32,128]{1,0:T(8,128)S(1)}, u32[]{:S(2)}, u32[]{:S(2)}) collective-permute-start(f32[32,128]{1,0:T(8,128)S(1)} %get-tuple-element.11.own_ref), channel_id=1, source_target_pairs={{0,12},{1,60},{8,13},{9,61},{16,20},{17,36},{24,21},{25,37},{32,28... | collective-permute-start | bytes 49160 | tf_op jit(solution)/shard_map/ppermute | solution.py:390
  57.6 12.8 %collective-permute-done.3.natural_ref = f32[32,128]{1,0:T(8,128)S(1)} collective-permute-done((f32[32,128]{1,0:T(8,128)S(1)}, f32[32,128]{1,0:T(8,128)S(1)}, u32[]{:S(2)}, u32[]{:S(2)}) %collective-permute-start.3) | collective-permute-done | bytes 16416 | tf_op jit(solution)/shard_map/ppermute | solution.py:390
  70.4 0.0 all-to-all-done.2.parts_ref.cols_ref
  70.4 12.3 %all_to_all.20.rows_ref = f32[8,48,128]{2,1,0:T(8,128)S(1)} all-to-all(f32[8,48,128]{2,1,0:T(8,128)S(1)} %spread.1), channel_id=1, replica_groups=mesh['row'=32,'col'=8] {'col'}, dimensions={0} | all-to-all | bytes 393216 | tf_op jit(solution)/shard_map/all_to_all | solution.py:371
  82.7 0.0 copy-done.1
  82.7 0.0 copy-done.2
  82.7 6.9 %update.1 = (f32[512,2048]{1,0:T(8,128)}, f32[1,64]{1,0:T(1,128)}) custom-call(f32[512,2048]{1,0:T(8,128)} %cov_ref.5, f32[32,40,128]{2,1,0:T(8,128)S(1)} %all-to-all-done.2.parts_ref.cols_ref, f32[8,48,128]{2,1,0:T(8,128)S(1)} %all_to_all.20.rows_ref, f32[1,32]{1,0:T(1,128)S(1)} %bitcast.3, f32[1,32]{1,0:T(1,128)S(1)} %bitcast.4), custom_call_target="tpu_custom_call" | custom-call | tf_op jit(solution)/shard_map/update/pallas_call | solution.py:352
  (1 shorter events, 0.0 us)
Async XLA Ops:
  2.1 11.3 %all-to-all-start = ((bf16[8,32,128]{2,1,0:T(8,128)(2,1)}), bf16[8,32,128]{2,1,0:T(8,128)(2,1)S(1)}, u32[]{:S(2)}, u32[]{:S(2)}) async-start(bf16[8,32,128]{2,1,0:T(8,128)(2,1)} %get-tuple-element.9), calls=%async_computation | async-start | bytes 131072 | tf_op jit(solution)/shard_map/all_to_all | solution.py:371
  15.5 0.8 copy-start
  16.3 66.4 %copy-start.1 = (f32[32]{0:T(128)S(1)}, f32[32]{0:T(128)}, u32[]{:S(2)}) copy-start(f32[32]{0:T(128)} %param.8) | copy-start | bytes 388
  16.3 66.4 %copy-start.2 = (f32[32]{0:T(128)S(1)}, f32[32]{0:T(128)}, u32[]{:S(2)}) copy-start(f32[32]{0:T(128)} %param.9) | copy-start | bytes 388
  16.3 25.3 %all-to-all-start.1 = ((f32[32,32,128]{2,1,0:T(8,128)}), f32[32,32,128]{2,1,0:T(8,128)S(1)}, u32[]{:S(2)}, u32[]{:S(2)}) async-start(f32[32,32,128]{2,1,0:T(8,128)} %copy-done), calls=%async_computation.1 | async-start | bytes 1048576 | tf_op jit(solution)/shard_map/all_to_all | solution.py:371
  27.0 10.4 %collective-permute-start.1 = (bf16[32,128]{1,0:T(8,128)(2,1)S(1)}, bf16[32,128]{1,0:T(8,128)(2,1)S(1)}, u32[]{:S(2)}, u32[]{:S(2)}) collective-permute-start(bf16[32,128]{1,0:T(8,128)(2,1)S(1)} %get-tuple-element.10), channel_id=1, source_target_pairs={{13,0},{61,1},{12,8},{60,9},{21,16},{37,17},{20,24},{36,25},{29,32... | collective-permute-start | bytes 24584 | tf_op jit(solution)/shard_map/ppermute | solution.py:383
  34.1 7.2 %collective-permute-start = (bf16[32,128]{1,0:T(8,128)(2,1)S(1)}, bf16[32,128]{1,0:T(8,128)(2,1)S(1)}, u32[]{:S(2)}, u32[]{:S(2)}) collective-permute-start(bf16[32,128]{1,0:T(8,128)(2,1)S(1)} %get-tuple-element.10), channel_id=1, source_target_pairs={{12,0},{60,1},{13,8},{61,9},{20,16},{36,17},{21,24},{37,25},{28,32... | collective-permute-start | bytes 24584 | tf_op jit(solution)/shard_map/ppermute | solution.py:382
  41.9 3.9 %collective-permute-start.2 = (f32[8,128]{1,0:T(8,128)S(1)}, f32[8,128]{1,0:T(8,128)S(1)}, u32[]{:S(2)}, u32[]{:S(2)}) collective-permute-start(f32[8,128]{1,0:T(8,128)S(1)} %get-tuple-element.13), channel_id=1, source_target_pairs={{0,1},{1,0},{2,3},{3,2},{4,5},{5,4},{6,7},{7,6},{8,9},{9,8},{10,11... | collective-permute-start | bytes 12296 | tf_op jit(solution)/shard_map/ppermute | solution.py:388
  46.7 23.7 %all-to-all-start.2 = ((f32[32,40,128]{2,1,0:T(8,128)}), f32[32,40,128]{2,1,0:T(8,128)S(1)}, u32[]{:S(2)}, u32[]{:S(2)}) async-start(f32[32,40,128]{2,1,0:T(8,128)} %fill.1), calls=%async_computation.2 | async-start | bytes 1310720 | tf_op jit(solution)/shard_map/all_to_all | solution.py:371
  52.3 18.1 %collective-permute-start.3 = (f32[32,128]{1,0:T(8,128)S(1)}, f32[32,128]{1,0:T(8,128)S(1)}, u32[]{:S(2)}, u32[]{:S(2)}) collective-permute-start(f32[32,128]{1,0:T(8,128)S(1)} %get-tuple-element.11.own_ref), channel_id=1, source_target_pairs={{0,12},{1,60},{8,13},{9,61},{16,20},{17,36},{24,21},{25,37},{32,28... | collective-permute-start | bytes 49160 | tf_op jit(solution)/shard_map/ppermute | solution.py:390

commit v6 on v4

--- a/solution.py
+++ b/solution.py
@@ -35,9 +35,7 @@
 
 
 def piece_at(tile, h, core):
-    x = (tile % 4 + 2) % 4
-    z = lax.rem(2 * (tile // 4) + h + 6 + 4 * core, 8)
-    return x * 8 + z
+    return (tile % 4 + 2) % 4, lax.rem(2 * (tile // 4) + h + 6 + 4 * core, 8)
 
 
 def halves(value):
@@ -137,8 +135,8 @@
         part = dot(jac, low, dims) + dot(jac, hi, dims)
         for step in range(GROUP // 128):
             for h in range(2):
-                place = piece_at(GROUP // 128 * group + step, h, core)
-                out_ref[place] = part[32 * h : 32 * h + 32, 128 * step : 128 * step + 128]
+                x, z = piece_at(GROUP // 128 * group + step, h, core)
+                out_ref[x * 8 + z] = part[32 * h : 32 * h + 32, 128 * step : 128 * step + 128]
 
 
 def product(jac, early, cov):
@@ -159,7 +157,7 @@
     )(jac, early, cov)
 
 
-def reduce_kernel(parts_ref, jac_ref, own_ref, kept_ref, sent_ref):
+def reduce_kernel(parts_ref, jac_ref, own_ref, line_ref):
     total = jnp.sum(parts_ref[...], axis=0)
     own_ref[...] = total
     dims = ((1,), (1,))
@@ -167,61 +165,64 @@
     jac = jac_ref[...]
     gram = dot(jac, low, dims) + dot(jac, mid, dims) + dot(jac, hi, dims)
     packed = jnp.concatenate([gram[16 * q : 16 * q + 16] for q in range(4)], axis=1)
-    first = lax.rem(lax.axis_index("col"), 2) == 0
-    kept_ref[...] = jnp.where(first, packed[:8], packed[8:])
-    sent_ref[...] = jnp.where(first, packed[8:], packed[:8])
+    line_ref[:, :32] = jnp.broadcast_to(total[None], (8, 32, 128))
+    line_ref[:, 32:] = jnp.broadcast_to(packed[None], (8, 16, 128))
 
 
 def reduce(parts, jac):
     return pl.pallas_call(
         reduce_kernel,
         in_specs=[VMEM] * 2,
-        out_specs=[VMEM] * 3,
+        out_specs=[VMEM] * 2,
         out_shape=[
             jax.ShapeDtypeStruct((32, 128), f32),
-            jax.ShapeDtypeStruct((8, 128), f32),
-            jax.ShapeDtypeStruct((8, 128), f32),
+            jax.ShapeDtypeStruct((8, 48, 128), f32),
         ],
         compiler_params=params(8),
         name="reduce",
     )(parts, jac)
 
 
-def fill_kernel(own_ref, kept_ref, got_ref, out_ref):
-    out_ref[:, :32] = jnp.broadcast_to(own_ref[...][None], (32, 32, 128))
-    gram = kept_ref[...] + got_ref[...]
-    out_ref[:, 32:] = jnp.broadcast_to(gram[None], (32, 8, 128))
-
-
-def fill(own, kept, got):
-    return pl.pallas_call(
-        fill_kernel,
-        in_specs=[VMEM] * 3,
-        out_specs=VMEM,
-        out_shape=jax.ShapeDtypeStruct((32, 40, 128), f32),
-        compiler_params=params(8),
-        name="fill",
-    )(own, kept, got)
-
-
-def spread_kernel(parts_ref, natural_ref, out_ref):
+def spread_kernel(parts_ref, natural_ref, line_ref, out_ref):
+    line_ref[...] = parts_ref[:, :32]
     out_ref[:, :32] = jnp.broadcast_to(natural_ref[...][None], (8, 32, 128))
     for h in range(2):
         total = parts_ref[h, 32:]
-        for t in range(1, 16):
-            total = total + parts_ref[2 * t + h, 32:]
-        out_ref[:, 32 + 8 * h : 40 + 8 * h] = jnp.broadcast_to(total[None], (8, 8, 128))
+        for z in range(h + 2, 8, 2):
+            total = total + parts_ref[z, 32:]
+        out_ref[:, 32 + 16 * h : 48 + 16 * h] = jnp.broadcast_to(total[None], (8, 16, 128))
 
 
 def spread(parts, natural):
     return pl.pallas_call(
         spread_kernel,
         in_specs=[VMEM] * 2,
-        out_specs=VMEM,
-        out_shape=jax.ShapeDtypeStruct((8, 48, 128), f32),
+        out_specs=[VMEM] * 2,
+        out_shape=[
+            jax.ShapeDtypeStruct((8, 32, 128), f32),
+            jax.ShapeDtypeStruct((8, 64, 128), f32),
+        ],
         compiler_params=params(4),
         name="spread",
     )(parts, natural)
+
+
+def gather_kernel(rows_ref, out_ref):
+    total = rows_ref[0, 32:]
+    for c in range(1, 8):
+        total = total + rows_ref[c, 32:]
+    out_ref[...] = total
+
+
+def gather(rows):
+    return pl.pallas_call(
+        gather_kernel,
+        in_specs=[VMEM],
+        out_specs=VMEM,
+        out_shape=jax.ShapeDtypeStruct((32, 128), f32),
+        compiler_params=params(4),
+        name="gather",
+    )(rows)
 
 
 PANEL = 8
@@ -264,22 +265,27 @@
 
 
 def update_kernel(
-    cov_ref, cols_ref, rows_ref, first_ref, second_ref, out_ref, inc_ref, held_ref, in_sems, out_sems
+    cov_ref,
+    line_refs,
+    gram_refs,
+    rows_ref,
+    first_ref,
+    second_ref,
+    out_ref,
+    inc_ref,
+    held_ref,
+    cols_ref,
+    in_sems,
+    out_sems,
 ):
     loads = start_loading(cov_ref, held_ref, in_sems)
     col = lax.axis_index("col")
     core = lax.rem(col, 2)
-    first, second = [
-        jnp.concatenate(
-            [
-                sum(rows_ref[2 * y + k, 32 + 8 * h : 40 + 8 * h] for y in range(1, 4))
-                + rows_ref[k, 32 + 8 * h : 40 + 8 * h]
-                for k in range(2)
-            ],
-            axis=0,
-        )
-        for h in range(2)
-    ]
+    x = lax.axis_index("row") // 8
+    for turn, line_ref in enumerate(line_refs):
+        cols_ref[lax.rem(x + turn, 4)] = line_ref[...]
+    total = (gram_refs[0][...] + gram_refs[1][...]) + (gram_refs[2][...] + gram_refs[3][...])
+    first, second = total[:16], total[16:]
     inverse = inverse_factor(first, second)
     hi, mid, low = thirds(inverse)
     inverse_parts = jnp.concatenate([hi, hi, hi, mid, mid, low], axis=1)
@@ -311,7 +317,7 @@
     cols = whitened(
         jnp.concatenate(
             [
-                jnp.concatenate([cols_ref[piece_at(tile, h, core), :32] for h in range(2)], axis=0)
+                jnp.concatenate([cols_ref[piece_at(tile, h, core)] for h in range(2)], axis=0)
                 for tile in range(16)
             ],
             axis=1,
@@ -334,10 +340,10 @@
         store.wait()
 
 
-def update(cov, cols, rows, first, second):
+def update(cov, lines, grams, rows, first, second):
     return pl.pallas_call(
         update_kernel,
-        in_specs=[HBM] + [VMEM] * 4,
+        in_specs=[HBM, [VMEM] * 4, [VMEM] * 4] + [VMEM] * 3,
         out_specs=[HBM, VMEM],
         out_shape=[
             jax.ShapeDtypeStruct((512, 2048), f32),
@@ -345,16 +351,28 @@
         ],
         scratch_shapes=[
             pltpu.VMEM((GROUPS, 512, GROUP), f32),
+            pltpu.VMEM((4, 8, 32, 128), f32),
             pltpu.SemaphoreType.DMA((GROUPS,)),
             pltpu.SemaphoreType.DMA((GROUPS,)),
         ],
         compiler_params=params(16),
         name="update",
-    )(cov, cols, rows, first, second)
-
-
-def exchange(array, axis):
-    return lax.all_to_all(array, axis, 0, 0, tiled=True)
+    )(cov, lines, grams, rows, first, second)
+
+
+def exchange(array, axis, groups=None):
+    return lax.all_to_all(array, axis, 0, 0, axis_index_groups=groups, tiled=True)
+
+
+Z_LINES = [[8 * x + z for z in range(8)] for x in range(4)]
+
+
+def along_x(array):
+    def at(turn):
+        pairs = [((r + 8 * turn) % 32, r) for r in range(32)]
+        return lax.ppermute(array, "row", pairs)
+
+    return [array] + [at(turn) for turn in (1, 2, 3)]
 
 
 def body(covariance, first_jacobian, second_jacobian, first_residuals, second_residuals):
@@ -366,12 +384,16 @@
     parts, jac_own = product(jac_rows, held, covariance)
     parts = exchange(parts, "row")
     jac_piece = lax.ppermute(jac_own, both, reversed_pairs(to_row_block()))
-    own, kept, sent = reduce(parts, jac_piece)
-    got = lax.ppermute(sent, "col", [(c, c ^ 1) for c in range(8)])
-    cols = exchange(fill(own, kept, got), "row")
+    own, line = reduce(parts, jac_piece)
+    line = exchange(line, "row", Z_LINES)
     natural = lax.ppermute(own, both, to_row_block())
-    rows = exchange(spread(cols, natural), "col")
-    out, increment = update(covariance, cols, rows, first_residuals[None], second_residuals[None])
+    line, rows = spread(line, natural)
+    rows = exchange(rows, "col")
+    lines = along_x(line)
+    grams = along_x(gather(rows))
+    out, increment = update(
+        covariance, lines, grams, rows, first_residuals[None], second_residuals[None]
+    )
     return out, increment[0]
 
 

time: 90 us -> 85.6 us (0.951)
  the two profiles are of different devices: /device:TPU:1 before, /device:TPU:6 now
where the time goes in v6:
time: 85.6 us; the launch traced here: 85 us
  starting transfers between devices  38.2 us (45%)
  waiting for transfers between devices  31.3 us (37%)
  Pallas kernels  12.6 us (15%)
  local copies, waits for them, and re-layouts  1.44 us (2%)
    all_to_all x4, starting transfers between devices, exchange(): lax.all_to_all(array, axis, 0, 0, axis_index_groups=groups, tiled=True)  23.7 us
    all_to_all x4, waiting for transfers between devices, exchange(): lax.all_to_all(array, axis, 0, 0, axis_index_groups=groups, tiled=True)  9.91 us
    ppermute x1, waiting for transfers between devices, body(): jac_piece = lax.ppermute(jac_own, both, reversed_pairs(to_row_block()))  8.57 us
    ppermute x1, waiting for transfers between devices, body(): natural = lax.ppermute(own, both, to_row_block())  7.83 us
    pallas_call x1, Pallas kernels, update(): pl.pallas_call(update_kernel, in_specs=[HBM, [VMEM] * 4, [VMEM] * 4] + [V...  6.92 us
    ppermute x6, starting transfers between devices, at(): return lax.ppermute(array, 'row', pairs)  6.38 us
    ppermute x6, waiting for transfers between devices, at(): return lax.ppermute(array, 'row', pairs)  4.94 us
    ppermute x1, starting transfers between devices, body(): jac_piece = lax.ppermute(jac_own, both, reversed_pairs(to_row_block()))  4.53 us
  transfers between devices with their start and end apart: 12, of which 8 were waited for; matrix products, arithmetic and copies ran while one was open for 0% of the time, Pallas kernels for 2%

profile of v6, /device:TPU:6, one launch (start us, length us, event | category | flops | bytes accessed | tf_op | source)
XLA Modules:
  0.0 85.0 jit_solution(3669988814625130374)
XLA Ops:
  0.6 0.8 pad_maximum_fusion
  1.4 0.6 broadcast_in_dim.12
  2.1 4.5 %all-to-all-start = ((bf16[8,32,128]{2,1,0:T(8,128)(2,1)}), bf16[8,32,128]{2,1,0:T(8,128)(2,1)S(1)}, u32[]{:S(2)}, u32[]{:S(2)}) async-start(bf16[8,32,128]{2,1,0:T(8,128)(2,1)} %broadcast_in_dim.12), calls=%async_computation | async-start | bytes 131072 | tf_op jit(solution)/shard_map/all_to_all | solution.py:364
  6.5 1.9 %load.1.early_ref = f32[3,512,512]{2,1,0:T(8,128)S(1)} custom-call(f32[512,2048]{1,0:T(8,128)} %cov_ref.5), custom_call_target="tpu_custom_call" | custom-call | tf_op jit(solution)/shard_map/load/pallas_call | solution.py:104
  8.4 0.0 copy-start.1
  8.4 0.0 copy-start.2
  8.5 3.7 %all-to-all-done.jac_ref = bf16[8,32,128]{2,1,0:T(8,128)(2,1)S(1)} async-done(((bf16[8,32,128]{2,1,0:T(8,128)(2,1)}), bf16[8,32,128]{2,1,0:T(8,128)(2,1)S(1)}, u32[]{:S(2)}, u32[]{:S(2)}) %all-to-all-start) | async-done | bytes 65568 | tf_op jit(solution)/shard_map/all_to_all | solution.py:364
  12.2 2.1 %product.1 = (f32[32,32,128]{2,1,0:T(8,128)S(1)}, bf16[64,128]{1,0:T(8,128)(2,1)S(1)}) custom-call(bf16[8,32,128]{2,1,0:T(8,128)(2,1)S(1)} %all-to-all-done.jac_ref, f32[3,512,512]{2,1,0:T(8,128)S(1)} %load.1.early_ref, f32[512,2048]{1,0:T(8,128)} %cov_ref.5), custom_call_target="tpu_custom_call" | custom-call | tf_op jit(solution)/shard_map/product/pallas_call | solution.py:143
  14.3 0.0 copy-start
  14.3 0.8 copy-done
  15.1 11.6 %all-to-all-start.1 = ((f32[32,32,128]{2,1,0:T(8,128)}), f32[32,32,128]{2,1,0:T(8,128)S(1)}, u32[]{:S(2)}, u32[]{:S(2)}) async-start(f32[32,32,128]{2,1,0:T(8,128)} %copy-done), calls=%async_computation.1 | async-start | bytes 1048576 | tf_op jit(solution)/shard_map/all_to_all | solution.py:364
  26.7 4.5 %collective-permute-start = (bf16[64,128]{1,0:T(8,128)(2,1)S(1)}, bf16[64,128]{1,0:T(8,128)(2,1)S(1)}, u32[]{:S(2)}, u32[]{:S(2)}) collective-permute-start(bf16[64,128]{1,0:T(8,128)(2,1)S(1)} %get-tuple-element.11), channel_id=1, source_target_pairs={{12,0},{60,1},{13,8},{61,9},{20,16},{36,17},{21,24},{37,25},{28,32... | collective-permute-start | bytes 49160 | tf_op jit(solution)/shard_map/ppermute | solution.py:386
  31.3 8.6 %collective-permute-done.jac_ref = bf16[64,128]{1,0:T(8,128)(2,1)S(1)} collective-permute-done((bf16[64,128]{1,0:T(8,128)(2,1)S(1)}, bf16[64,128]{1,0:T(8,128)(2,1)S(1)}, u32[]{:S(2)}, u32[]{:S(2)}) %collective-permute-start) | collective-permute-done | bytes 16416 | tf_op jit(solution)/shard_map/ppermute | solution.py:386
  39.8 1.9 %all-to-all-done.1.parts_ref = f32[32,32,128]{2,1,0:T(8,128)S(1)} async-done(((f32[32,32,128]{2,1,0:T(8,128)}), f32[32,32,128]{2,1,0:T(8,128)S(1)}, u32[]{:S(2)}, u32[]{:S(2)}) %all-to-all-start.1) | async-done | bytes 524320 | tf_op jit(solution)/shard_map/all_to_all | solution.py:364
  41.7 0.9 %reduce.1 = (f32[32,128]{1,0:T(8,128)S(1)}, f32[8,48,128]{2,1,0:T(8,128)}) custom-call(f32[32,32,128]{2,1,0:T(8,128)S(1)} %all-to-all-done.1.parts_ref, bf16[64,128]{1,0:T(8,128)(2,1)S(1)} %collective-permute-done.jac_ref), custom_call_target="tpu_custom_call" | custom-call | tf_op jit(solution)/shard_map/reduce/pallas_call | solution.py:173
  42.6 4.3 %all-to-all-start.2 = ((f32[8,48,128]{2,1,0:T(8,128)}), f32[8,48,128]{2,1,0:T(8,128)S(1)}, u32[]{:S(2)}, u32[]{:S(2)}) async-start(f32[8,48,128]{2,1,0:T(8,128)} %get-tuple-element.12), calls=%async_computation.2 | async-start | bytes 393216 | tf_op jit(solution)/shard_map/all_to_all | solution.py:364
  46.9 3.6 %collective-permute-start.1 = (f32[32,128]{1,0:T(8,128)S(1)}, f32[32,128]{1,0:T(8,128)S(1)}, u32[]{:S(2)}, u32[]{:S(2)}) collective-permute-start(f32[32,128]{1,0:T(8,128)S(1)} %get-tuple-element.13), channel_id=1, source_target_pairs={{0,12},{1,60},{8,13},{9,61},{16,20},{17,36},{24,21},{25,37},{32,28... | collective-permute-start | bytes 49160 | tf_op jit(solution)/shard_map/ppermute | solution.py:389
  50.5 7.8 %collective-permute-done.1.natural_ref = f32[32,128]{1,0:T(8,128)S(1)} collective-permute-done((f32[32,128]{1,0:T(8,128)S(1)}, f32[32,128]{1,0:T(8,128)S(1)}, u32[]{:S(2)}, u32[]{:S(2)}) %collective-permute-start.1) | collective-permute-done | bytes 16416 | tf_op jit(solution)/shard_map/ppermute | solution.py:389
  58.3 0.7 spread.1
  59.0 3.4 %all-to-all-start.3 = ((f32[8,64,128]{2,1,0:T(8,128)}), f32[8,64,128]{2,1,0:T(8,128)S(1)}, u32[]{:S(2)}, u32[]{:S(2)}) async-start(f32[8,64,128]{2,1,0:T(8,128)} %get-tuple-element.15), calls=%async_computation.3 | async-start | bytes 524288 | tf_op jit(solution)/shard_map/all_to_all | solution.py:364
  62.5 0.8 collective-permute-start.4
  63.3 2.3 %collective-permute-start.3 = (f32[8,32,128]{2,1,0:T(8,128)S(1)}, f32[8,32,128]{2,1,0:T(8,128)S(1)}, u32[]{:S(2)}, u32[]{:S(2)}) collective-permute-start(f32[8,32,128]{2,1,0:T(8,128)S(1)} %get-tuple-element.14.line_refs_0_), channel_id=1, source_target_pairs={{128,0},{136,8},{144,16},{152,24},{160,32},{168,40},{176,48},{184,... | collective-permute-start | bytes 393224 | tf_op jit(solution)/shard_map/ppermute | solution.py:373
  65.6 4.3 %all-to-all-done.3.rows_ref = f32[8,64,128]{2,1,0:T(8,128)S(1)} async-done(((f32[8,64,128]{2,1,0:T(8,128)}), f32[8,64,128]{2,1,0:T(8,128)S(1)}, u32[]{:S(2)}, u32[]{:S(2)}) %all-to-all-start.3) | async-done | bytes 262176 | tf_op jit(solution)/shard_map/all_to_all | solution.py:364
  69.9 1.0 %collective-permute-start.7 = (f32[32,128]{1,0:T(8,128)S(1)}, f32[32,128]{1,0:T(8,128)S(1)}, u32[]{:S(2)}, u32[]{:S(2)}) collective-permute-start(f32[32,128]{1,0:T(8,128)S(1)} %gather.1.gram_refs_0_), channel_id=1, source_target_pairs={{192,0},{200,8},{208,16},{216,24},{224,32},{232,40},{240,48},{248,... | collective-permute-start | bytes 49160 | tf_op jit(solution)/shard_map/ppermute | solution.py:373
  70.9 2.3 %collective-permute-start.6 = (f32[32,128]{1,0:T(8,128)S(1)}, f32[32,128]{1,0:T(8,128)S(1)}, u32[]{:S(2)}, u32[]{:S(2)}) collective-permute-start(f32[32,128]{1,0:T(8,128)S(1)} %gather.1.gram_refs_0_), channel_id=1, source_target_pairs={{128,0},{136,8},{144,16},{152,24},{160,32},{168,40},{176,48},{184,... | collective-permute-start | bytes 49160 | tf_op jit(solution)/shard_map/ppermute | solution.py:373
  73.2 0.0 collective-permute-start.5
  73.2 0.0 collective-permute-done.3.line_refs_2_
  73.2 0.0 collective-permute-done.2.line_refs_1_
  73.2 0.5 collective-permute-done.7.gram_refs_3_
  73.7 2.5 %collective-permute-done.6.gram_refs_2_ = f32[32,128]{1,0:T(8,128)S(1)} collective-permute-done((f32[32,128]{1,0:T(8,128)S(1)}, f32[32,128]{1,0:T(8,128)S(1)}, u32[]{:S(2)}, u32[]{:S(2)}) %collective-permute-start.6) | collective-permute-done | bytes 16416 | tf_op jit(solution)/shard_map/ppermute | solution.py:373
  76.3 1.9 %collective-permute-done.5.gram_refs_1_ = f32[32,128]{1,0:T(8,128)S(1)} collective-permute-done((f32[32,128]{1,0:T(8,128)S(1)}, f32[32,128]{1,0:T(8,128)S(1)}, u32[]{:S(2)}, u32[]{:S(2)}) %collective-permute-start.5) | collective-permute-done | bytes 16416 | tf_op jit(solution)/shard_map/ppermute | solution.py:373
  78.1 6.9 %update.1 = (f32[512,2048]{1,0:T(8,128)}, f32[1,64]{1,0:T(1,128)}) custom-call(f32[512,2048]{1,0:T(8,128)} %cov_ref.5, f32[8,32,128]{2,1,0:T(8,128)S(1)} %get-tuple-element.14.line_refs_0_, f32[8,32,128]{2,1,0:T(8,128)S(1)} %collective-permute-done.2.line_refs_1_, f32[8,32,128]{2,1,0:T(8,128)S(1)} %collective-permute-done.3.line_refs_2_, ...), custom_call_target="tpu_custom_call" | custom-call | tf_op jit(solution)/shard_map/update/pallas_call | solution.py:344
  (6 shorter events, 0.0 us)
Async XLA Ops:
  2.1 10.1 %all-to-all-start = ((bf16[8,32,128]{2,1,0:T(8,128)(2,1)}), bf16[8,32,128]{2,1,0:T(8,128)(2,1)S(1)}, u32[]{:S(2)}, u32[]{:S(2)}) async-start(bf16[8,32,128]{2,1,0:T(8,128)(2,1)} %broadcast_in_dim.12), calls=%async_computation | async-start | bytes 131072 | tf_op jit(solution)/shard_map/all_to_all | solution.py:364
  8.4 69.7 %copy-start.1 = (f32[32]{0:T(128)S(1)}, f32[32]{0:T(128)}, u32[]{:S(2)}) copy-start(f32[32]{0:T(128)} %param.8) | copy-start | bytes 388
  8.4 69.7 %copy-start.2 = (f32[32]{0:T(128)S(1)}, f32[32]{0:T(128)}, u32[]{:S(2)}) copy-start(f32[32]{0:T(128)} %param.9) | copy-start | bytes 388
  14.3 0.8 copy-start
  15.1 26.6 %all-to-all-start.1 = ((f32[32,32,128]{2,1,0:T(8,128)}), f32[32,32,128]{2,1,0:T(8,128)S(1)}, u32[]{:S(2)}, u32[]{:S(2)}) async-start(f32[32,32,128]{2,1,0:T(8,128)} %copy-done), calls=%async_computation.1 | async-start | bytes 1048576 | tf_op jit(solution)/shard_map/all_to_all | solution.py:364
  26.7 13.1 %collective-permute-start = (bf16[64,128]{1,0:T(8,128)(2,1)S(1)}, bf16[64,128]{1,0:T(8,128)(2,1)S(1)}, u32[]{:S(2)}, u32[]{:S(2)}) collective-permute-start(bf16[64,128]{1,0:T(8,128)(2,1)S(1)} %get-tuple-element.11), channel_id=1, source_target_pairs={{12,0},{60,1},{13,8},{61,9},{20,16},{36,17},{21,24},{37,25},{28,32... | collective-permute-start | bytes 49160 | tf_op jit(solution)/shard_map/ppermute | solution.py:386
  42.6 15.7 %all-to-all-start.2 = ((f32[8,48,128]{2,1,0:T(8,128)}), f32[8,48,128]{2,1,0:T(8,128)S(1)}, u32[]{:S(2)}, u32[]{:S(2)}) async-start(f32[8,48,128]{2,1,0:T(8,128)} %get-tuple-element.12), calls=%async_computation.2 | async-start | bytes 393216 | tf_op jit(solution)/shard_map/all_to_all | solution.py:364
  46.9 11.4 %collective-permute-start.1 = (f32[32,128]{1,0:T(8,128)S(1)}, f32[32,128]{1,0:T(8,128)S(1)}, u32[]{:S(2)}, u32[]{:S(2)}) collective-permute-start(f32[32,128]{1,0:T(8,128)S(1)} %get-tuple-element.13), channel_id=1, source_target_pairs={{0,12},{1,60},{8,13},{9,61},{16,20},{17,36},{24,21},{25,37},{32,28... | collective-permute-start | bytes 49160 | tf_op jit(solution)/shard_map/ppermute | solution.py:389
  59.0 10.9 %all-to-all-start.3 = ((f32[8,64,128]{2,1,0:T(8,128)}), f32[8,64,128]{2,1,0:T(8,128)S(1)}, u32[]{:S(2)}, u32[]{:S(2)}) async-start(f32[8,64,128]{2,1,0:T(8,128)} %get-tuple-element.15), calls=%async_computation.3 | async-start | bytes 524288 | tf_op jit(solution)/shard_map/all_to_all | solution.py:364
  62.5 10.7 %collective-permute-start.4 = (f32[8,32,128]{2,1,0:T(8,128)S(1)}, f32[8,32,128]{2,1,0:T(8,128)S(1)}, u32[]{:S(2)}, u32[]{:S(2)}) collective-permute-start(f32[8,32,128]{2,1,0:T(8,128)S(1)} %get-tuple-element.14.line_refs_0_), channel_id=1, source_target_pairs={{192,0},{200,8},{208,16},{216,24},{224,32},{232,40},{240,48},{248,... | collective-permute-start | bytes 393224 | tf_op jit(solution)/shard_map/ppermute | solution.py:373
  63.3 9.9 %collective-permute-start.3 = (f32[8,32,128]{2,1,0:T(8,128)S(1)}, f32[8,32,128]{2,1,0:T(8,128)S(1)}, u32[]{:S(2)}, u32[]{:S(2)}) collective-permute-start(f32[8,32,128]{2,1,0:T(8,128)S(1)} %get-tuple-element.14.line_refs_0_), channel_id=1, source_target_pairs={{128,0},{136,8},{144,16},{152,24},{160,32},{168,40},{176,48},{184,... | collective-permute-start | bytes 393224 | tf_op jit(solution)/shard_map/ppermute | solution.py:373
  65.6 7.6 %collective-permute-start.2 = (f32[8,32,128]{2,1,0:T(8,128)S(1)}, f32[8,32,128]{2,1,0:T(8,128)S(1)}, u32[]{:S(2)}, u32[]{:S(2)}) collective-permute-start(f32[8,32,128]{2,1,0:T(8,128)S(1)} %get-tuple-element.14.line_refs_0_), channel_id=1, source_target_pairs={{64,0},{72,8},{80,16},{88,24},{96,32},{104,40},{112,48},{120,56},{... | collective-permute-start | bytes 393224 | tf_op jit(solution)/shard_map/ppermute | solution.py:373
  69.9 3.8 %collective-permute-start.7 = (f32[32,128]{1,0:T(8,128)S(1)}, f32[32,128]{1,0:T(8,128)S(1)}, u32[]{:S(2)}, u32[]{:S(2)}) collective-permute-start(f32[32,128]{1,0:T(8,128)S(1)} %gather.1.gram_refs_0_), channel_id=1, source_target_pairs={{192,0},{200,8},{208,16},{216,24},{224,32},{232,40},{240,48},{248,... | collective-permute-start | bytes 49160 | tf_op jit(solution)/shard_map/ppermute | solution.py:373
  70.9 5.4 %collective-permute-start.6 = (f32[32,128]{1,0:T(8,128)S(1)}, f32[32,128]{1,0:T(8,128)S(1)}, u32[]{:S(2)}, u32[]{:S(2)}) collective-permute-start(f32[32,128]{1,0:T(8,128)S(1)} %gather.1.gram_refs_0_), channel_id=1, source_target_pairs={{128,0},{136,8},{144,16},{152,24},{160,32},{168,40},{176,48},{184,... | collective-permute-start | bytes 49160 | tf_op jit(solution)/shard_map/ppermute | solution.py:373
  73.2 5.0 %collective-permute-start.5 = (f32[32,128]{1,0:T(8,128)S(1)}, f32[32,128]{1,0:T(8,128)S(1)}, u32[]{:S(2)}, u32[]{:S(2)}) collective-permute-start(f32[32,128]{1,0:T(8,128)S(1)} %gather.1.gram_refs_0_), channel_id=1, source_target_pairs={{64,0},{72,8},{80,16},{88,24},{96,32},{104,40},{112,48},{120,56},{... | collective-permute-start | bytes 49160 | tf_op jit(solution)/shard_map/ppermute | solution.py:373

commit v7 on v6

--- a/solution.py
+++ b/solution.py
@@ -72,10 +72,10 @@
     return ref.at[:, pl.ds(GROUP * group, GROUP)]
 
 
-def start_loading(cov_ref, held_ref, sems):
+def start_loading(cov_ref, held_ref, sems, first):
     copies = [
         pltpu.make_async_copy(group_of(cov_ref, g), held_ref.at[g], sems.at[g])
-        for g in range(GROUPS)
+        for g in range(first, GROUPS)
     ]
     for copy in copies:
         copy.start()
@@ -86,33 +86,33 @@
     return pltpu.CompilerParams(vmem_limit_bytes=int(mib * 1048576))
 
 
-EARLY = 3
-
-
-def load_kernel(cov_ref, out_ref, sems):
-    copies = [
-        pltpu.make_async_copy(group_of(cov_ref, g), out_ref.at[g], sems.at[g])
-        for g in range(EARLY)
-    ]
-    for copy in copies:
-        copy.start()
-    for copy in copies:
-        copy.wait()
-
-
-def load(cov):
+def load(cov, count):
+    def load_kernel(cov_ref, out_ref, sems):
+        copies = [
+            pltpu.make_async_copy(group_of(cov_ref, g), out_ref.at[g], sems.at[g])
+            for g in range(count)
+        ]
+        for copy in copies:
+            copy.start()
+        for copy in copies:
+            copy.wait()
+
     return pl.pallas_call(
         load_kernel,
         in_specs=[HBM],
         out_specs=VMEM,
-        out_shape=jax.ShapeDtypeStruct((EARLY, 512, GROUP), f32),
-        scratch_shapes=[pltpu.SemaphoreType.DMA((EARLY,))],
+        out_shape=jax.ShapeDtypeStruct((count, 512, GROUP), f32),
+        scratch_shapes=[pltpu.SemaphoreType.DMA((count,))],
         compiler_params=params(16),
-        name="load",
+        name="fetch",
     )(cov)
 
 
-def product_kernel(jac_ref, early_ref, cov_ref, out_ref, own_ref, late_ref, sems):
+EARLY = 3
+AGAIN = 2
+
+
+def product_kernel(jac_ref, early_ref, cov_ref, out_refs, own_ref, late_ref, whole_ref, sems):
     copies = [
         pltpu.make_async_copy(group_of(cov_ref, g), late_ref.at[g - EARLY], sems.at[g - EARLY])
         for g in range(EARLY, GROUPS)
@@ -136,25 +136,44 @@
         for step in range(GROUP // 128):
             for h in range(2):
                 x, z = piece_at(GROUP // 128 * group + step, h, core)
-                out_ref[x * 8 + z] = part[32 * h : 32 * h + 32, 128 * step : 128 * step + 128]
+                whole_ref[x, z] = part[32 * h : 32 * h + 32, 128 * step : 128 * step + 128]
+    x = lax.axis_index("row") // 8
+    for turn in range(4):
+        out_refs[turn][...] = whole_ref[lax.rem(x + turn, 4)]
 
 
 def product(jac, early, cov):
     return pl.pallas_call(
         product_kernel,
         in_specs=[VMEM, VMEM, HBM],
-        out_specs=[VMEM] * 2,
+        out_specs=[[VMEM] * 4, VMEM],
         out_shape=[
-            jax.ShapeDtypeStruct((32, 32, 128), f32),
+            [jax.ShapeDtypeStruct((8, 32, 128), f32)] * 4,
             jax.ShapeDtypeStruct((64, 128), bf16),
         ],
         scratch_shapes=[
             pltpu.VMEM((GROUPS - EARLY, 512, GROUP), f32),
+            pltpu.VMEM((4, 8, 32, 128), f32),
             pltpu.SemaphoreType.DMA((GROUPS - EARLY,)),
         ],
         compiler_params=params(16),
         name="product",
     )(jac, early, cov)
+
+
+def add_kernel(first_ref, second_ref, third_ref, fourth_ref, out_ref):
+    out_ref[...] = (first_ref[...] + second_ref[...]) + (third_ref[...] + fourth_ref[...])
+
+
+def add(parts):
+    return pl.pallas_call(
+        add_kernel,
+        in_specs=[VMEM] * 4,
+        out_specs=VMEM,
+        out_shape=jax.ShapeDtypeStruct((8, 32, 128), f32),
+        compiler_params=params(8),
+        name="add",
+    )(*parts)
 
 
 def reduce_kernel(parts_ref, jac_ref, own_ref, line_ref):
@@ -265,6 +284,7 @@
 
 
 def update_kernel(
+    early_ref,
     cov_ref,
     line_refs,
     gram_refs,
@@ -278,7 +298,7 @@
     in_sems,
     out_sems,
 ):
-    loads = start_loading(cov_ref, held_ref, in_sems)
+    loads = start_loading(cov_ref, held_ref, in_sems, AGAIN)
     col = lax.axis_index("col")
     core = lax.rem(col, 2)
     x = lax.axis_index("row") // 8
@@ -325,12 +345,13 @@
     )
     hi, low = halves(cols)
     right = jnp.concatenate([hi, low, hi, low], axis=0)
-    for load in loads:
-        load.wait()
     stores = []
     for group in range(GROUPS):
         change = dot(left, right[:, GROUP * group : GROUP * group + GROUP], ((1,), (0,)))
-        held_ref[group] = (held_ref[group] - change) * (1.0 / (lam_start * lam_next))
+        if group >= AGAIN:
+            loads[group - AGAIN].wait()
+        old = early_ref[group] if group < AGAIN else held_ref[group]
+        held_ref[group] = (old - change) * (1.0 / (lam_start * lam_next))
         store = pltpu.make_async_copy(
             held_ref.at[group], group_of(out_ref, group), out_sems.at[group]
         )
@@ -340,10 +361,10 @@
         store.wait()
 
 
-def update(cov, lines, grams, rows, first, second):
+def update(early, cov, lines, grams, rows, first, second):
     return pl.pallas_call(
         update_kernel,
-        in_specs=[HBM, [VMEM] * 4, [VMEM] * 4] + [VMEM] * 3,
+        in_specs=[VMEM, HBM, [VMEM] * 4, [VMEM] * 4] + [VMEM] * 3,
         out_specs=[HBM, VMEM],
         out_shape=[
             jax.ShapeDtypeStruct((512, 2048), f32),
@@ -357,7 +378,7 @@
         ],
         compiler_params=params(16),
         name="update",
-    )(cov, lines, grams, rows, first, second)
+    )(early, cov, lines, grams, rows, first, second)
 
 
 def exchange(array, axis, groups=None):
@@ -367,12 +388,12 @@
 Z_LINES = [[8 * x + z for z in range(8)] for x in range(4)]
 
 
+def moved(array, turn):
+    return lax.ppermute(array, "row", [(r, (r + 8 * turn) % 32) for r in range(32)])
+
+
 def along_x(array):
-    def at(turn):
-        pairs = [((r + 8 * turn) % 32, r) for r in range(32)]
-        return lax.ppermute(array, "row", pairs)
-
-    return [array] + [at(turn) for turn in (1, 2, 3)]
+    return [array] + [moved(array, 4 - turn) for turn in (1, 2, 3)]
 
 
 def body(covariance, first_jacobian, second_jacobian, first_residuals, second_residuals):
@@ -380,9 +401,11 @@
     jac = jnp.concatenate([first_jacobian, second_jacobian], axis=1)
     jac_rows = exchange(jnp.broadcast_to(jac[None], (8, 32, 128)), "col")
     covariance = pltpu.with_memory_space_constraint(covariance, pltpu.HBM)
-    held = load(covariance)
+    held = load(covariance, EARLY)
     parts, jac_own = product(jac_rows, held, covariance)
-    parts = exchange(parts, "row")
+    parts = parts[:1] + [moved(parts[turn], turn) for turn in (1, 2, 3)]
+    parts = add(parts)
+    parts = exchange(parts, "row", Z_LINES)
     jac_piece = lax.ppermute(jac_own, both, reversed_pairs(to_row_block()))
     own, line = reduce(parts, jac_piece)
     line = exchange(line, "row", Z_LINES)
@@ -390,9 +413,10 @@
     line, rows = spread(line, natural)
     rows = exchange(rows, "col")
     lines = along_x(line)
+    held = load(covariance, AGAIN)
     grams = along_x(gather(rows))
     out, increment = update(
-        covariance, lines, grams, rows, first_residuals[None], second_residuals[None]
+        held, covariance, lines, grams, rows, first_residuals[None], second_residuals[None]
     )
     return out, increment[0]
 

time: 85.6 us -> 84.4 us (0.986)
  the two profiles are of different devices: /device:TPU:6 before, /device:TPU:8 now
where the time goes in v7:
time: 84.4 us; the launch traced here: 83.3 us
  starting transfers between devices  47.9 us (57%)
  waiting for transfers between devices  20 us (24%)
  Pallas kernels  13.3 us (16%)
    all_to_all x4, starting transfers between devices, exchange(): lax.all_to_all(array, axis, 0, 0, axis_index_groups=groups, tiled=True)  22.6 us
    ppermute x9, starting transfers between devices, moved(): lax.ppermute(array, 'row', [(r, (r + 8 * turn) % 32) for r in range(32)])  15.9 us
    ppermute x1, waiting for transfers between devices, body(): natural = lax.ppermute(own, both, to_row_block())  8.94 us
    ppermute x1, starting transfers between devices, body(): jac_piece = lax.ppermute(jac_own, both, reversed_pairs(to_row_block()))  6.84 us
    ppermute x9, waiting for transfers between devices, moved(): lax.ppermute(array, 'row', [(r, (r + 8 * turn) % 32) for r in range(32)])  5.73 us
    pallas_call x1, Pallas kernels, update(): pl.pallas_call(update_kernel, in_specs=[VMEM, HBM, [VMEM] * 4, [VMEM] * 4...  5.34 us
    all_to_all x4, waiting for transfers between devices, exchange(): lax.all_to_all(array, axis, 0, 0, axis_index_groups=groups, tiled=True)  3.88 us
    pallas_call x2, Pallas kernels, load(): pl.pallas_call(load_kernel, in_specs=[HBM], out_specs=VMEM, out_shape=jax...  3.45 us
  transfers between devices with their start and end apart: 15, of which 10 were waited for; matrix products, arithmetic and copies ran while one was open for 0% of the time, Pallas kernels for 4%

profile of v7, /device:TPU:8, one launch (start us, length us, event | category | flops | bytes accessed | tf_op | source)
XLA Modules:
  0.0 83.3 jit_solution(4286936483365072358)
XLA Ops:
  0.6 0.8 pad_maximum_fusion
  1.4 0.6 broadcast_in_dim.12
  2.1 5.4 %all-to-all-start = ((bf16[8,32,128]{2,1,0:T(8,128)(2,1)}), bf16[8,32,128]{2,1,0:T(8,128)(2,1)S(1)}, u32[]{:S(2)}, u32[]{:S(2)}) async-start(bf16[8,32,128]{2,1,0:T(8,128)(2,1)} %broadcast_in_dim.12), calls=%async_computation | async-start | bytes 131072 | tf_op jit(solution)/shard_map/all_to_all | solution.py:385
  7.5 1.9 %fetch.3.early_ref = f32[3,512,512]{2,1,0:T(8,128)S(1)} custom-call(f32[512,2048]{1,0:T(8,128)} %cov_ref.7), custom_call_target="tpu_custom_call" | custom-call | tf_op jit(solution)/shard_map/fetch/pallas_call | solution.py:100
  9.4 2.3 %all-to-all-done.jac_ref = bf16[8,32,128]{2,1,0:T(8,128)(2,1)S(1)} async-done(((bf16[8,32,128]{2,1,0:T(8,128)(2,1)}), bf16[8,32,128]{2,1,0:T(8,128)(2,1)S(1)}, u32[]{:S(2)}, u32[]{:S(2)}) %all-to-all-start) | async-done | bytes 65568 | tf_op jit(solution)/shard_map/all_to_all | solution.py:385
  11.7 2.2 %product.1 = (f32[8,32,128]{2,1,0:T(8,128)S(1)}, f32[8,32,128]{2,1,0:T(8,128)S(1)}, f32[8,32,128]{2,1,0:T(8,128)S(1)}, f32[8,32,128]{2,1,0:T(8,128)S(1)}, bf16[64,128]{1,0:T(8,128)(2,1)S(1)}) custom-call(bf16[8,32,128]{2,1,0:T(8,128)(2,1)S(1)} %all-to-all-done.jac_ref, f32[3,512,512]{2,1,0:T(8,128)S(1)} %fetch.3.early_ref, f32[512,2048]{1,0:T(8,128)} %cov_ref.7), custom_call_target="tpu_custom_call" | custom-call | tf_op jit(solution)/shard_map/product/pallas_call | solution.py:146
  13.9 1.1 %collective-permute-start = (f32[8,32,128]{2,1,0:T(8,128)S(1)}, f32[8,32,128]{2,1,0:T(8,128)S(1)}, u32[]{:S(2)}, u32[]{:S(2)}) collective-permute-start(f32[8,32,128]{2,1,0:T(8,128)S(1)} %get-tuple-element.14), channel_id=1, source_target_pairs={{0,64},{8,72},{16,80},{24,88},{32,96},{40,104},{48,112},{56,120},{... | collective-permute-start | bytes 393224 | tf_op jit(solution)/shard_map/ppermute | solution.py:392
  14.9 2.7 %collective-permute-start.1 = (f32[8,32,128]{2,1,0:T(8,128)S(1)}, f32[8,32,128]{2,1,0:T(8,128)S(1)}, u32[]{:S(2)}, u32[]{:S(2)}) collective-permute-start(f32[8,32,128]{2,1,0:T(8,128)S(1)} %get-tuple-element.15), channel_id=1, source_target_pairs={{0,128},{8,136},{16,144},{24,152},{32,160},{40,168},{48,176},{56,1... | collective-permute-start | bytes 393224 | tf_op jit(solution)/shard_map/ppermute | solution.py:392
  17.6 1.4 %collective-permute-start.2 = (f32[8,32,128]{2,1,0:T(8,128)S(1)}, f32[8,32,128]{2,1,0:T(8,128)S(1)}, u32[]{:S(2)}, u32[]{:S(2)}) collective-permute-start(f32[8,32,128]{2,1,0:T(8,128)S(1)} %get-tuple-element.16), channel_id=1, source_target_pairs={{0,192},{8,200},{16,208},{24,216},{32,224},{40,232},{48,240},{56,2... | collective-permute-start | bytes 393224 | tf_op jit(solution)/shard_map/ppermute | solution.py:392
  19.1 2.0 %collective-permute-done.second_ref = f32[8,32,128]{2,1,0:T(8,128)S(1)} collective-permute-done((f32[8,32,128]{2,1,0:T(8,128)S(1)}, f32[8,32,128]{2,1,0:T(8,128)S(1)}, u32[]{:S(2)}, u32[]{:S(2)}) %collective-permute-start) | collective-permute-done | bytes 131104 | tf_op jit(solution)/shard_map/ppermute | solution.py:392
  21.1 2.5 %collective-permute-done.1.third_ref = f32[8,32,128]{2,1,0:T(8,128)S(1)} collective-permute-done((f32[8,32,128]{2,1,0:T(8,128)S(1)}, f32[8,32,128]{2,1,0:T(8,128)S(1)}, u32[]{:S(2)}, u32[]{:S(2)}) %collective-permute-start.1) | collective-permute-done | bytes 131104 | tf_op jit(solution)/shard_map/ppermute | solution.py:392
  23.7 0.7 add.1
  24.4 8.5 %all-to-all-start.1 = ((f32[8,32,128]{2,1,0:T(8,128)}), f32[8,32,128]{2,1,0:T(8,128)S(1)}, u32[]{:S(2)}, u32[]{:S(2)}) async-start(f32[8,32,128]{2,1,0:T(8,128)} %add.1), calls=%async_computation.1 | async-start | bytes 262144 | tf_op jit(solution)/shard_map/all_to_all | solution.py:385
  32.8 6.8 %collective-permute-start.3 = (bf16[64,128]{1,0:T(8,128)(2,1)S(1)}, bf16[64,128]{1,0:T(8,128)(2,1)S(1)}, u32[]{:S(2)}, u32[]{:S(2)}) collective-permute-start(bf16[64,128]{1,0:T(8,128)(2,1)S(1)} %get-tuple-element.17), channel_id=1, source_target_pairs={{12,0},{60,1},{13,8},{61,9},{20,16},{36,17},{21,24},{37,25},{28,32... | collective-permute-start | bytes 49160 | tf_op jit(solution)/shard_map/ppermute | solution.py:409
  39.7 1.4 %collective-permute-done.3.jac_ref = bf16[64,128]{1,0:T(8,128)(2,1)S(1)} collective-permute-done((bf16[64,128]{1,0:T(8,128)(2,1)S(1)}, bf16[64,128]{1,0:T(8,128)(2,1)S(1)}, u32[]{:S(2)}, u32[]{:S(2)}) %collective-permute-start.3) | collective-permute-done | bytes 16416 | tf_op jit(solution)/shard_map/ppermute | solution.py:409
  41.1 0.8 all-to-all-done.1.parts_ref
  41.9 0.9 %reduce.1 = (f32[32,128]{1,0:T(8,128)S(1)}, f32[8,48,128]{2,1,0:T(8,128)}) custom-call(f32[8,32,128]{2,1,0:T(8,128)S(1)} %all-to-all-done.1.parts_ref, bf16[64,128]{1,0:T(8,128)(2,1)S(1)} %collective-permute-done.3.jac_ref), custom_call_target="tpu_custom_call" | custom-call | tf_op jit(solution)/shard_map/reduce/pallas_call | solution.py:192
  42.8 4.9 %all-to-all-start.2 = ((f32[8,48,128]{2,1,0:T(8,128)}), f32[8,48,128]{2,1,0:T(8,128)S(1)}, u32[]{:S(2)}, u32[]{:S(2)}) async-start(f32[8,48,128]{2,1,0:T(8,128)} %get-tuple-element.18), calls=%async_computation.2 | async-start | bytes 393216 | tf_op jit(solution)/shard_map/all_to_all | solution.py:385
  47.7 2.6 %collective-permute-start.4 = (f32[32,128]{1,0:T(8,128)S(1)}, f32[32,128]{1,0:T(8,128)S(1)}, u32[]{:S(2)}, u32[]{:S(2)}) collective-permute-start(f32[32,128]{1,0:T(8,128)S(1)} %get-tuple-element.19), channel_id=1, source_target_pairs={{0,12},{1,60},{8,13},{9,61},{16,20},{17,36},{24,21},{25,37},{32,28... | collective-permute-start | bytes 49160 | tf_op jit(solution)/shard_map/ppermute | solution.py:412
  50.3 8.9 %collective-permute-done.4.natural_ref = f32[32,128]{1,0:T(8,128)S(1)} collective-permute-done((f32[32,128]{1,0:T(8,128)S(1)}, f32[32,128]{1,0:T(8,128)S(1)}, u32[]{:S(2)}, u32[]{:S(2)}) %collective-permute-start.4) | collective-permute-done | bytes 16416 | tf_op jit(solution)/shard_map/ppermute | solution.py:412
  59.3 0.7 spread.1
  60.0 3.8 %all-to-all-start.3 = ((f32[8,64,128]{2,1,0:T(8,128)}), f32[8,64,128]{2,1,0:T(8,128)S(1)}, u32[]{:S(2)}, u32[]{:S(2)}) async-start(f32[8,64,128]{2,1,0:T(8,128)} %get-tuple-element.21), calls=%async_computation.3 | async-start | bytes 524288 | tf_op jit(solution)/shard_map/all_to_all | solution.py:385
  63.8 1.9 %collective-permute-start.7 = (f32[8,32,128]{2,1,0:T(8,128)S(1)}, f32[8,32,128]{2,1,0:T(8,128)S(1)}, u32[]{:S(2)}, u32[]{:S(2)}) collective-permute-start(f32[8,32,128]{2,1,0:T(8,128)S(1)} %get-tuple-element.20.line_refs_0_), channel_id=1, source_target_pairs={{0,64},{8,72},{16,80},{24,88},{32,96},{40,104},{48,112},{56,120},{... | collective-permute-start | bytes 393224 | tf_op jit(solution)/shard_map/ppermute | solution.py:392
  65.7 2.3 %collective-permute-start.6 = (f32[8,32,128]{2,1,0:T(8,128)S(1)}, f32[8,32,128]{2,1,0:T(8,128)S(1)}, u32[]{:S(2)}, u32[]{:S(2)}) collective-permute-start(f32[8,32,128]{2,1,0:T(8,128)S(1)} %get-tuple-element.20.line_refs_0_), channel_id=1, source_target_pairs={{0,128},{8,136},{16,144},{24,152},{32,160},{40,168},{48,176},{56,1... | collective-permute-start | bytes 393224 | tf_op jit(solution)/shard_map/ppermute | solution.py:392
  68.0 1.0 %collective-permute-start.5 = (f32[8,32,128]{2,1,0:T(8,128)S(1)}, f32[8,32,128]{2,1,0:T(8,128)S(1)}, u32[]{:S(2)}, u32[]{:S(2)}) collective-permute-start(f32[8,32,128]{2,1,0:T(8,128)S(1)} %get-tuple-element.20.line_refs_0_), channel_id=1, source_target_pairs={{0,192},{8,200},{16,208},{24,216},{32,224},{40,232},{48,240},{56,2... | collective-permute-start | bytes 393224 | tf_op jit(solution)/shard_map/ppermute | solution.py:392
  69.1 0.8 all-to-all-done.3.rows_ref
  69.9 2.0 %collective-permute-start.10 = (f32[32,128]{1,0:T(8,128)S(1)}, f32[32,128]{1,0:T(8,128)S(1)}, u32[]{:S(2)}, u32[]{:S(2)}) collective-permute-start(f32[32,128]{1,0:T(8,128)S(1)} %gather.1.gram_refs_0_), channel_id=1, source_target_pairs={{0,64},{8,72},{16,80},{24,88},{32,96},{40,104},{48,112},{56,120},{... | collective-permute-start | bytes 49160 | tf_op jit(solution)/shard_map/ppermute | solution.py:392
  71.9 2.3 %collective-permute-start.9 = (f32[32,128]{1,0:T(8,128)S(1)}, f32[32,128]{1,0:T(8,128)S(1)}, u32[]{:S(2)}, u32[]{:S(2)}) collective-permute-start(f32[32,128]{1,0:T(8,128)S(1)} %gather.1.gram_refs_0_), channel_id=1, source_target_pairs={{0,128},{8,136},{16,144},{24,152},{32,160},{40,168},{48,176},{56,1... | collective-permute-start | bytes 49160 | tf_op jit(solution)/shard_map/ppermute | solution.py:392
  74.2 1.0 %collective-permute-start.8 = (f32[32,128]{1,0:T(8,128)S(1)}, f32[32,128]{1,0:T(8,128)S(1)}, u32[]{:S(2)}, u32[]{:S(2)}) collective-permute-start(f32[32,128]{1,0:T(8,128)S(1)} %gather.1.gram_refs_0_), channel_id=1, source_target_pairs={{0,192},{8,200},{16,208},{24,216},{32,224},{40,232},{48,240},{56,2... | collective-permute-start | bytes 49160 | tf_op jit(solution)/shard_map/ppermute | solution.py:392
  75.2 1.6 %fetch.2.early_ref = f32[2,512,512]{2,1,0:T(8,128)S(1)} custom-call(f32[512,2048]{1,0:T(8,128)} %cov_ref.7), custom_call_target="tpu_custom_call" | custom-call | tf_op jit(solution)/shard_map/fetch/pallas_call | solution.py:100
  77.1 0.8 collective-permute-done.8.gram_refs_1_
  78.0 5.3 %update.1 = (f32[512,2048]{1,0:T(8,128)}, f32[1,64]{1,0:T(1,128)}) custom-call(f32[2,512,512]{2,1,0:T(8,128)S(1)} %fetch.2.early_ref, f32[512,2048]{1,0:T(8,128)} %cov_ref.7, f32[8,32,128]{2,1,0:T(8,128)S(1)} %get-tuple-element.20.line_refs_0_, f32[8,32,128]{2,1,0:T(8,128)S(1)} %collective-permute-done.5.line_refs_1_, ...), custom_call_target="tpu_custom_call" | custom-call | tf_op jit(solution)/shard_map/update/pallas_call | solution.py:365
  (12 shorter events, 0.4 us)
Async XLA Ops:
  2.1 9.6 %all-to-all-start = ((bf16[8,32,128]{2,1,0:T(8,128)(2,1)}), bf16[8,32,128]{2,1,0:T(8,128)(2,1)S(1)}, u32[]{:S(2)}, u32[]{:S(2)}) async-start(bf16[8,32,128]{2,1,0:T(8,128)(2,1)} %broadcast_in_dim.12), calls=%async_computation | async-start | bytes 131072 | tf_op jit(solution)/shard_map/all_to_all | solution.py:385
  13.9 7.2 %collective-permute-start = (f32[8,32,128]{2,1,0:T(8,128)S(1)}, f32[8,32,128]{2,1,0:T(8,128)S(1)}, u32[]{:S(2)}, u32[]{:S(2)}) collective-permute-start(f32[8,32,128]{2,1,0:T(8,128)S(1)} %get-tuple-element.14), channel_id=1, source_target_pairs={{0,64},{8,72},{16,80},{24,88},{32,96},{40,104},{48,112},{56,120},{... | collective-permute-start | bytes 393224 | tf_op jit(solution)/shard_map/ppermute | solution.py:392
  14.9 8.6 %collective-permute-start.1 = (f32[8,32,128]{2,1,0:T(8,128)S(1)}, f32[8,32,128]{2,1,0:T(8,128)S(1)}, u32[]{:S(2)}, u32[]{:S(2)}) collective-permute-start(f32[8,32,128]{2,1,0:T(8,128)S(1)} %get-tuple-element.15), channel_id=1, source_target_pairs={{0,128},{8,136},{16,144},{24,152},{32,160},{40,168},{48,176},{56,1... | collective-permute-start | bytes 393224 | tf_op jit(solution)/shard_map/ppermute | solution.py:392
  17.6 6.0 %collective-permute-start.2 = (f32[8,32,128]{2,1,0:T(8,128)S(1)}, f32[8,32,128]{2,1,0:T(8,128)S(1)}, u32[]{:S(2)}, u32[]{:S(2)}) collective-permute-start(f32[8,32,128]{2,1,0:T(8,128)S(1)} %get-tuple-element.16), channel_id=1, source_target_pairs={{0,192},{8,200},{16,208},{24,216},{32,224},{40,232},{48,240},{56,2... | collective-permute-start | bytes 393224 | tf_op jit(solution)/shard_map/ppermute | solution.py:392
  24.4 53.6 %copy-start = (f32[32]{0:T(128)S(1)}, f32[32]{0:T(128)}, u32[]{:S(2)}) copy-start(f32[32]{0:T(128)} %param.8) | copy-start | bytes 388
  24.4 53.6 %copy-start.1 = (f32[32]{0:T(128)S(1)}, f32[32]{0:T(128)}, u32[]{:S(2)}) copy-start(f32[32]{0:T(128)} %param.9) | copy-start | bytes 388
  24.4 17.6 %all-to-all-start.1 = ((f32[8,32,128]{2,1,0:T(8,128)}), f32[8,32,128]{2,1,0:T(8,128)S(1)}, u32[]{:S(2)}, u32[]{:S(2)}) async-start(f32[8,32,128]{2,1,0:T(8,128)} %add.1), calls=%async_computation.1 | async-start | bytes 262144 | tf_op jit(solution)/shard_map/all_to_all | solution.py:385
  32.8 8.3 %collective-permute-start.3 = (bf16[64,128]{1,0:T(8,128)(2,1)S(1)}, bf16[64,128]{1,0:T(8,128)(2,1)S(1)}, u32[]{:S(2)}, u32[]{:S(2)}) collective-permute-start(bf16[64,128]{1,0:T(8,128)(2,1)S(1)} %get-tuple-element.17), channel_id=1, source_target_pairs={{12,0},{60,1},{13,8},{61,9},{20,16},{36,17},{21,24},{37,25},{28,32... | collective-permute-start | bytes 49160 | tf_op jit(solution)/shard_map/ppermute | solution.py:409
  42.8 16.4 %all-to-all-start.2 = ((f32[8,48,128]{2,1,0:T(8,128)}), f32[8,48,128]{2,1,0:T(8,128)S(1)}, u32[]{:S(2)}, u32[]{:S(2)}) async-start(f32[8,48,128]{2,1,0:T(8,128)} %get-tuple-element.18), calls=%async_computation.2 | async-start | bytes 393216 | tf_op jit(solution)/shard_map/all_to_all | solution.py:385
  47.7 11.6 %collective-permute-start.4 = (f32[32,128]{1,0:T(8,128)S(1)}, f32[32,128]{1,0:T(8,128)S(1)}, u32[]{:S(2)}, u32[]{:S(2)}) collective-permute-start(f32[32,128]{1,0:T(8,128)S(1)} %get-tuple-element.19), channel_id=1, source_target_pairs={{0,12},{1,60},{8,13},{9,61},{16,20},{17,36},{24,21},{25,37},{32,28... | collective-permute-start | bytes 49160 | tf_op jit(solution)/shard_map/ppermute | solution.py:412
  60.0 9.9 %all-to-all-start.3 = ((f32[8,64,128]{2,1,0:T(8,128)}), f32[8,64,128]{2,1,0:T(8,128)S(1)}, u32[]{:S(2)}, u32[]{:S(2)}) async-start(f32[8,64,128]{2,1,0:T(8,128)} %get-tuple-element.21), calls=%async_computation.3 | async-start | bytes 524288 | tf_op jit(solution)/shard_map/all_to_all | solution.py:385
  63.8 10.4 %collective-permute-start.7 = (f32[8,32,128]{2,1,0:T(8,128)S(1)}, f32[8,32,128]{2,1,0:T(8,128)S(1)}, u32[]{:S(2)}, u32[]{:S(2)}) collective-permute-start(f32[8,32,128]{2,1,0:T(8,128)S(1)} %get-tuple-element.20.line_refs_0_), channel_id=1, source_target_pairs={{0,64},{8,72},{16,80},{24,88},{32,96},{40,104},{48,112},{56,120},{... | collective-permute-start | bytes 393224 | tf_op jit(solution)/shard_map/ppermute | solution.py:392
  65.7 11.1 %collective-permute-start.6 = (f32[8,32,128]{2,1,0:T(8,128)S(1)}, f32[8,32,128]{2,1,0:T(8,128)S(1)}, u32[]{:S(2)}, u32[]{:S(2)}) collective-permute-start(f32[8,32,128]{2,1,0:T(8,128)S(1)} %get-tuple-element.20.line_refs_0_), channel_id=1, source_target_pairs={{0,128},{8,136},{16,144},{24,152},{32,160},{40,168},{48,176},{56,1... | collective-permute-start | bytes 393224 | tf_op jit(solution)/shard_map/ppermute | solution.py:392
  68.0 8.8 %collective-permute-start.5 = (f32[8,32,128]{2,1,0:T(8,128)S(1)}, f32[8,32,128]{2,1,0:T(8,128)S(1)}, u32[]{:S(2)}, u32[]{:S(2)}) collective-permute-start(f32[8,32,128]{2,1,0:T(8,128)S(1)} %get-tuple-element.20.line_refs_0_), channel_id=1, source_target_pairs={{0,192},{8,200},{16,208},{24,216},{32,224},{40,232},{48,240},{56,2... | collective-permute-start | bytes 393224 | tf_op jit(solution)/shard_map/ppermute | solution.py:392
  69.9 7.0 %collective-permute-start.10 = (f32[32,128]{1,0:T(8,128)S(1)}, f32[32,128]{1,0:T(8,128)S(1)}, u32[]{:S(2)}, u32[]{:S(2)}) collective-permute-start(f32[32,128]{1,0:T(8,128)S(1)} %gather.1.gram_refs_0_), channel_id=1, source_target_pairs={{0,64},{8,72},{16,80},{24,88},{32,96},{40,104},{48,112},{56,120},{... | collective-permute-start | bytes 49160 | tf_op jit(solution)/shard_map/ppermute | solution.py:392
  71.9 5.2 %collective-permute-start.9 = (f32[32,128]{1,0:T(8,128)S(1)}, f32[32,128]{1,0:T(8,128)S(1)}, u32[]{:S(2)}, u32[]{:S(2)}) collective-permute-start(f32[32,128]{1,0:T(8,128)S(1)} %gather.1.gram_refs_0_), channel_id=1, source_target_pairs={{0,128},{8,136},{16,144},{24,152},{32,160},{40,168},{48,176},{56,1... | collective-permute-start | bytes 49160 | tf_op jit(solution)/shard_map/ppermute | solution.py:392
  74.2 3.7 %collective-permute-start.8 = (f32[32,128]{1,0:T(8,128)S(1)}, f32[32,128]{1,0:T(8,128)S(1)}, u32[]{:S(2)}, u32[]{:S(2)}) collective-permute-start(f32[32,128]{1,0:T(8,128)S(1)} %gather.1.gram_refs_0_), channel_id=1, source_target_pairs={{0,192},{8,200},{16,208},{24,216},{32,224},{40,232},{48,240},{56,2... | collective-permute-start | bytes 49160 | tf_op jit(solution)/shard_map/ppermute | solution.py:392

commit v8 on v7

--- a/solution.py
+++ b/solution.py
@@ -388,6 +388,11 @@
 Z_LINES = [[8 * x + z for z in range(8)] for x in range(4)]
 
 
+def copies_of(first, second):
+    pair = [jnp.broadcast_to(array[None], (8, 32, 64)) for array in (first, second)]
+    return jnp.concatenate(pair, axis=2)
+
+
 def moved(array, turn):
     return lax.ppermute(array, "row", [(r, (r + 8 * turn) % 32) for r in range(32)])
 
@@ -398,8 +403,7 @@
 
 def body(covariance, first_jacobian, second_jacobian, first_residuals, second_residuals):
     both = ("row", "col")
-    jac = jnp.concatenate([first_jacobian, second_jacobian], axis=1)
-    jac_rows = exchange(jnp.broadcast_to(jac[None], (8, 32, 128)), "col")
+    jac_rows = exchange(copies_of(first_jacobian, second_jacobian), "col")
     covariance = pltpu.with_memory_space_constraint(covariance, pltpu.HBM)
     held = load(covariance, EARLY)
     parts, jac_own = product(jac_rows, held, covariance)

time: 84.4 us -> 85.3 us (1.011)
  no operation moved by 1% of the time
where the time goes in v8:
time: 85.3 us; the launch traced here: 84.2 us
  starting transfers between devices  47.9 us (56%)
  waiting for transfers between devices  20 us (23%)
  Pallas kernels  13.3 us (16%)
  local copies, waits for them, and re-layouts  1.42 us (2%)
  between operations  0.86 us (1%)
    all_to_all x4, starting transfers between devices, exchange(): lax.all_to_all(array, axis, 0, 0, axis_index_groups=groups, tiled=True)  22.6 us
    ppermute x9, starting transfers between devices, moved(): lax.ppermute(array, 'row', [(r, (r + 8 * turn) % 32) for r in range(32)])  15.9 us
    ppermute x1, waiting for transfers between devices, body(): natural = lax.ppermute(own, both, to_row_block())  8.94 us
    ppermute x1, starting transfers between devices, body(): jac_piece = lax.ppermute(jac_own, both, reversed_pairs(to_row_block()))  6.85 us
    ppermute x9, waiting for transfers between devices, moved(): lax.ppermute(array, 'row', [(r, (r + 8 * turn) % 32) for r in range(32)])  5.73 us
    pallas_call x1, Pallas kernels, update(): pl.pallas_call(update_kernel, in_specs=[VMEM, HBM, [VMEM] * 4, [VMEM] * 4...  5.34 us
    all_to_all x4, waiting for transfers between devices, exchange(): lax.all_to_all(array, axis, 0, 0, axis_index_groups=groups, tiled=True)  3.87 us
    pallas_call x2, Pallas kernels, load(): pl.pallas_call(load_kernel, in_specs=[HBM], out_specs=VMEM, out_shape=jax...  3.45 us
  transfers between devices with their start and end apart: 15, of which 10 were waited for; matrix products, arithmetic and copies ran while one was open for 0% of the time, Pallas kernels for 4%

profile of v8, /device:TPU:8, one launch (start us, length us, event | category | flops | bytes accessed | tf_op | source)
XLA Modules:
  0.0 84.2 jit_solution(16565143220963335258)
XLA Ops:
  0.6 0.7 broadcast_in_dim.8
  1.3 0.7 broadcast_in_dim.9
  2.1 0.7 pad_maximum_fusion
  2.8 5.4 %all-to-all-start = ((bf16[8,32,128]{2,1,0:T(8,128)(2,1)}), bf16[8,32,128]{2,1,0:T(8,128)(2,1)S(1)}, u32[]{:S(2)}, u32[]{:S(2)}) async-start(bf16[8,32,128]{2,1,0:T(8,128)(2,1)} %pad_maximum_fusion), calls=%async_computation | async-start | bytes 131072 | tf_op jit(solution)/shard_map/all_to_all | solution.py:385
  8.2 1.9 %fetch.3.early_ref = f32[3,512,512]{2,1,0:T(8,128)S(1)} custom-call(f32[512,2048]{1,0:T(8,128)} %cov_ref.7), custom_call_target="tpu_custom_call" | custom-call | tf_op jit(solution)/shard_map/fetch/pallas_call | solution.py:100
  10.1 2.3 %all-to-all-done.jac_ref = bf16[8,32,128]{2,1,0:T(8,128)(2,1)S(1)} async-done(((bf16[8,32,128]{2,1,0:T(8,128)(2,1)}), bf16[8,32,128]{2,1,0:T(8,128)(2,1)S(1)}, u32[]{:S(2)}, u32[]{:S(2)}) %all-to-all-start) | async-done | bytes 65568 | tf_op jit(solution)/shard_map/all_to_all | solution.py:385
  12.4 2.2 %product.1 = (f32[8,32,128]{2,1,0:T(8,128)S(1)}, f32[8,32,128]{2,1,0:T(8,128)S(1)}, f32[8,32,128]{2,1,0:T(8,128)S(1)}, f32[8,32,128]{2,1,0:T(8,128)S(1)}, bf16[64,128]{1,0:T(8,128)(2,1)S(1)}) custom-call(bf16[8,32,128]{2,1,0:T(8,128)(2,1)S(1)} %all-to-all-done.jac_ref, f32[3,512,512]{2,1,0:T(8,128)S(1)} %fetch.3.early_ref, f32[512,2048]{1,0:T(8,128)} %cov_ref.7), custom_call_target="tpu_custom_call" | custom-call | tf_op jit(solution)/shard_map/product/pallas_call | solution.py:146
  14.6 1.0 %collective-permute-start = (f32[8,32,128]{2,1,0:T(8,128)S(1)}, f32[8,32,128]{2,1,0:T(8,128)S(1)}, u32[]{:S(2)}, u32[]{:S(2)}) collective-permute-start(f32[8,32,128]{2,1,0:T(8,128)S(1)} %get-tuple-element.14), channel_id=1, source_target_pairs={{0,64},{8,72},{16,80},{24,88},{32,96},{40,104},{48,112},{56,120},{... | collective-permute-start | bytes 393224 | tf_op jit(solution)/shard_map/ppermute | solution.py:397
  15.6 2.7 %collective-permute-start.1 = (f32[8,32,128]{2,1,0:T(8,128)S(1)}, f32[8,32,128]{2,1,0:T(8,128)S(1)}, u32[]{:S(2)}, u32[]{:S(2)}) collective-permute-start(f32[8,32,128]{2,1,0:T(8,128)S(1)} %get-tuple-element.15), channel_id=1, source_target_pairs={{0,128},{8,136},{16,144},{24,152},{32,160},{40,168},{48,176},{56,1... | collective-permute-start | bytes 393224 | tf_op jit(solution)/shard_map/ppermute | solution.py:397
  18.3 1.4 %collective-permute-start.2 = (f32[8,32,128]{2,1,0:T(8,128)S(1)}, f32[8,32,128]{2,1,0:T(8,128)S(1)}, u32[]{:S(2)}, u32[]{:S(2)}) collective-permute-start(f32[8,32,128]{2,1,0:T(8,128)S(1)} %get-tuple-element.16), channel_id=1, source_target_pairs={{0,192},{8,200},{16,208},{24,216},{32,224},{40,232},{48,240},{56,2... | collective-permute-start | bytes 393224 | tf_op jit(solution)/shard_map/ppermute | solution.py:397
  19.8 2.0 %collective-permute-done.second_ref = f32[8,32,128]{2,1,0:T(8,128)S(1)} collective-permute-done((f32[8,32,128]{2,1,0:T(8,128)S(1)}, f32[8,32,128]{2,1,0:T(8,128)S(1)}, u32[]{:S(2)}, u32[]{:S(2)}) %collective-permute-start) | collective-permute-done | bytes 131104 | tf_op jit(solution)/shard_map/ppermute | solution.py:397
  21.8 2.5 %collective-permute-done.1.third_ref = f32[8,32,128]{2,1,0:T(8,128)S(1)} collective-permute-done((f32[8,32,128]{2,1,0:T(8,128)S(1)}, f32[8,32,128]{2,1,0:T(8,128)S(1)}, u32[]{:S(2)}, u32[]{:S(2)}) %collective-permute-start.1) | collective-permute-done | bytes 131104 | tf_op jit(solution)/shard_map/ppermute | solution.py:397
  25.1 8.5 %all-to-all-start.1 = ((f32[8,32,128]{2,1,0:T(8,128)}), f32[8,32,128]{2,1,0:T(8,128)S(1)}, u32[]{:S(2)}, u32[]{:S(2)}) async-start(f32[8,32,128]{2,1,0:T(8,128)} %add.1), calls=%async_computation.1 | async-start | bytes 262144 | tf_op jit(solution)/shard_map/all_to_all | solution.py:385
  33.5 6.9 %collective-permute-start.3 = (bf16[64,128]{1,0:T(8,128)(2,1)S(1)}, bf16[64,128]{1,0:T(8,128)(2,1)S(1)}, u32[]{:S(2)}, u32[]{:S(2)}) collective-permute-start(bf16[64,128]{1,0:T(8,128)(2,1)S(1)} %get-tuple-element.17), channel_id=1, source_target_pairs={{12,0},{60,1},{13,8},{61,9},{20,16},{36,17},{21,24},{37,25},{28,32... | collective-permute-start | bytes 49160 | tf_op jit(solution)/shard_map/ppermute | solution.py:413
  40.4 1.4 %collective-permute-done.3.jac_ref = bf16[64,128]{1,0:T(8,128)(2,1)S(1)} collective-permute-done((bf16[64,128]{1,0:T(8,128)(2,1)S(1)}, bf16[64,128]{1,0:T(8,128)(2,1)S(1)}, u32[]{:S(2)}, u32[]{:S(2)}) %collective-permute-start.3) | collective-permute-done | bytes 16416 | tf_op jit(solution)/shard_map/ppermute | solution.py:413
  41.8 0.8 all-to-all-done.1.parts_ref
  42.6 0.9 %reduce.1 = (f32[32,128]{1,0:T(8,128)S(1)}, f32[8,48,128]{2,1,0:T(8,128)}) custom-call(f32[8,32,128]{2,1,0:T(8,128)S(1)} %all-to-all-done.1.parts_ref, bf16[64,128]{1,0:T(8,128)(2,1)S(1)} %collective-permute-done.3.jac_ref), custom_call_target="tpu_custom_call" | custom-call | tf_op jit(solution)/shard_map/reduce/pallas_call | solution.py:192
  43.5 4.9 %all-to-all-start.2 = ((f32[8,48,128]{2,1,0:T(8,128)}), f32[8,48,128]{2,1,0:T(8,128)S(1)}, u32[]{:S(2)}, u32[]{:S(2)}) async-start(f32[8,48,128]{2,1,0:T(8,128)} %get-tuple-element.18), calls=%async_computation.2 | async-start | bytes 393216 | tf_op jit(solution)/shard_map/all_to_all | solution.py:385
  48.4 2.6 %collective-permute-start.4 = (f32[32,128]{1,0:T(8,128)S(1)}, f32[32,128]{1,0:T(8,128)S(1)}, u32[]{:S(2)}, u32[]{:S(2)}) collective-permute-start(f32[32,128]{1,0:T(8,128)S(1)} %get-tuple-element.19), channel_id=1, source_target_pairs={{0,12},{1,60},{8,13},{9,61},{16,20},{17,36},{24,21},{25,37},{32,28... | collective-permute-start | bytes 49160 | tf_op jit(solution)/shard_map/ppermute | solution.py:416
  51.0 8.9 %collective-permute-done.4.natural_ref = f32[32,128]{1,0:T(8,128)S(1)} collective-permute-done((f32[32,128]{1,0:T(8,128)S(1)}, f32[32,128]{1,0:T(8,128)S(1)}, u32[]{:S(2)}, u32[]{:S(2)}) %collective-permute-start.4) | collective-permute-done | bytes 16416 | tf_op jit(solution)/shard_map/ppermute | solution.py:416
  60.0 0.7 spread.1
  60.7 3.8 %all-to-all-start.3 = ((f32[8,64,128]{2,1,0:T(8,128)}), f32[8,64,128]{2,1,0:T(8,128)S(1)}, u32[]{:S(2)}, u32[]{:S(2)}) async-start(f32[8,64,128]{2,1,0:T(8,128)} %get-tuple-element.21), calls=%async_computation.3 | async-start | bytes 524288 | tf_op jit(solution)/shard_map/all_to_all | solution.py:385
  64.5 1.9 %collective-permute-start.7 = (f32[8,32,128]{2,1,0:T(8,128)S(1)}, f32[8,32,128]{2,1,0:T(8,128)S(1)}, u32[]{:S(2)}, u32[]{:S(2)}) collective-permute-start(f32[8,32,128]{2,1,0:T(8,128)S(1)} %get-tuple-element.20.line_refs_0_), channel_id=1, source_target_pairs={{0,64},{8,72},{16,80},{24,88},{32,96},{40,104},{48,112},{56,120},{... | collective-permute-start | bytes 393224 | tf_op jit(solution)/shard_map/ppermute | solution.py:397
  66.4 2.3 %collective-permute-start.6 = (f32[8,32,128]{2,1,0:T(8,128)S(1)}, f32[8,32,128]{2,1,0:T(8,128)S(1)}, u32[]{:S(2)}, u32[]{:S(2)}) collective-permute-start(f32[8,32,128]{2,1,0:T(8,128)S(1)} %get-tuple-element.20.line_refs_0_), channel_id=1, source_target_pairs={{0,128},{8,136},{16,144},{24,152},{32,160},{40,168},{48,176},{56,1... | collective-permute-start | bytes 393224 | tf_op jit(solution)/shard_map/ppermute | solution.py:397
  68.8 1.0 %collective-permute-start.5 = (f32[8,32,128]{2,1,0:T(8,128)S(1)}, f32[8,32,128]{2,1,0:T(8,128)S(1)}, u32[]{:S(2)}, u32[]{:S(2)}) collective-permute-start(f32[8,32,128]{2,1,0:T(8,128)S(1)} %get-tuple-element.20.line_refs_0_), channel_id=1, source_target_pairs={{0,192},{8,200},{16,208},{24,216},{32,224},{40,232},{48,240},{56,2... | collective-permute-start | bytes 393224 | tf_op jit(solution)/shard_map/ppermute | solution.py:397
  69.8 0.8 all-to-all-done.3.rows_ref
  70.6 2.0 %collective-permute-start.10 = (f32[32,128]{1,0:T(8,128)S(1)}, f32[32,128]{1,0:T(8,128)S(1)}, u32[]{:S(2)}, u32[]{:S(2)}) collective-permute-start(f32[32,128]{1,0:T(8,128)S(1)} %gather.1.gram_refs_0_), channel_id=1, source_target_pairs={{0,64},{8,72},{16,80},{24,88},{32,96},{40,104},{48,112},{56,120},{... | collective-permute-start | bytes 49160 | tf_op jit(solution)/shard_map/ppermute | solution.py:397
  72.6 2.3 %collective-permute-start.9 = (f32[32,128]{1,0:T(8,128)S(1)}, f32[32,128]{1,0:T(8,128)S(1)}, u32[]{:S(2)}, u32[]{:S(2)}) collective-permute-start(f32[32,128]{1,0:T(8,128)S(1)} %gather.1.gram_refs_0_), channel_id=1, source_target_pairs={{0,128},{8,136},{16,144},{24,152},{32,160},{40,168},{48,176},{56,1... | collective-permute-start | bytes 49160 | tf_op jit(solution)/shard_map/ppermute | solution.py:397
  74.9 1.0 %collective-permute-start.8 = (f32[32,128]{1,0:T(8,128)S(1)}, f32[32,128]{1,0:T(8,128)S(1)}, u32[]{:S(2)}, u32[]{:S(2)}) collective-permute-start(f32[32,128]{1,0:T(8,128)S(1)} %gather.1.gram_refs_0_), channel_id=1, source_target_pairs={{0,192},{8,200},{16,208},{24,216},{32,224},{40,232},{48,240},{56,2... | collective-permute-start | bytes 49160 | tf_op jit(solution)/shard_map/ppermute | solution.py:397
  76.0 1.6 %fetch.2.early_ref = f32[2,512,512]{2,1,0:T(8,128)S(1)} custom-call(f32[512,2048]{1,0:T(8,128)} %cov_ref.7), custom_call_target="tpu_custom_call" | custom-call | tf_op jit(solution)/shard_map/fetch/pallas_call | solution.py:100
  77.8 0.8 collective-permute-done.8.gram_refs_1_
  78.7 5.3 %update.1 = (f32[512,2048]{1,0:T(8,128)}, f32[1,64]{1,0:T(1,128)}) custom-call(f32[2,512,512]{2,1,0:T(8,128)S(1)} %fetch.2.early_ref, f32[512,2048]{1,0:T(8,128)} %cov_ref.7, f32[8,32,128]{2,1,0:T(8,128)S(1)} %get-tuple-element.20.line_refs_0_, f32[8,32,128]{2,1,0:T(8,128)S(1)} %collective-permute-done.5.line_refs_1_, ...), custom_call_target="tpu_custom_call" | custom-call | tf_op jit(solution)/shard_map/update/pallas_call | solution.py:365
  (13 shorter events, 1.1 us)
Async XLA Ops:
  2.8 9.6 %all-to-all-start = ((bf16[8,32,128]{2,1,0:T(8,128)(2,1)}), bf16[8,32,128]{2,1,0:T(8,128)(2,1)S(1)}, u32[]{:S(2)}, u32[]{:S(2)}) async-start(bf16[8,32,128]{2,1,0:T(8,128)(2,1)} %pad_maximum_fusion), calls=%async_computation | async-start | bytes 131072 | tf_op jit(solution)/shard_map/all_to_all | solution.py:385
  14.6 7.2 %collective-permute-start = (f32[8,32,128]{2,1,0:T(8,128)S(1)}, f32[8,32,128]{2,1,0:T(8,128)S(1)}, u32[]{:S(2)}, u32[]{:S(2)}) collective-permute-start(f32[8,32,128]{2,1,0:T(8,128)S(1)} %get-tuple-element.14), channel_id=1, source_target_pairs={{0,64},{8,72},{16,80},{24,88},{32,96},{40,104},{48,112},{56,120},{... | collective-permute-start | bytes 393224 | tf_op jit(solution)/shard_map/ppermute | solution.py:397
  15.6 8.7 %collective-permute-start.1 = (f32[8,32,128]{2,1,0:T(8,128)S(1)}, f32[8,32,128]{2,1,0:T(8,128)S(1)}, u32[]{:S(2)}, u32[]{:S(2)}) collective-permute-start(f32[8,32,128]{2,1,0:T(8,128)S(1)} %get-tuple-element.15), channel_id=1, source_target_pairs={{0,128},{8,136},{16,144},{24,152},{32,160},{40,168},{48,176},{56,1... | collective-permute-start | bytes 393224 | tf_op jit(solution)/shard_map/ppermute | solution.py:397
  18.3 6.0 %collective-permute-start.2 = (f32[8,32,128]{2,1,0:T(8,128)S(1)}, f32[8,32,128]{2,1,0:T(8,128)S(1)}, u32[]{:S(2)}, u32[]{:S(2)}) collective-permute-start(f32[8,32,128]{2,1,0:T(8,128)S(1)} %get-tuple-element.16), channel_id=1, source_target_pairs={{0,192},{8,200},{16,208},{24,216},{32,224},{40,232},{48,240},{56,2... | collective-permute-start | bytes 393224 | tf_op jit(solution)/shard_map/ppermute | solution.py:397
  25.1 53.6 %copy-start = (f32[32]{0:T(128)S(1)}, f32[32]{0:T(128)}, u32[]{:S(2)}) copy-start(f32[32]{0:T(128)} %param.8) | copy-start | bytes 388
  25.1 53.6 %copy-start.1 = (f32[32]{0:T(128)S(1)}, f32[32]{0:T(128)}, u32[]{:S(2)}) copy-start(f32[32]{0:T(128)} %param.9) | copy-start | bytes 388
  25.1 17.6 %all-to-all-start.1 = ((f32[8,32,128]{2,1,0:T(8,128)}), f32[8,32,128]{2,1,0:T(8,128)S(1)}, u32[]{:S(2)}, u32[]{:S(2)}) async-start(f32[8,32,128]{2,1,0:T(8,128)} %add.1), calls=%async_computation.1 | async-start | bytes 262144 | tf_op jit(solution)/shard_map/all_to_all | solution.py:385
  33.5 8.3 %collective-permute-start.3 = (bf16[64,128]{1,0:T(8,128)(2,1)S(1)}, bf16[64,128]{1,0:T(8,128)(2,1)S(1)}, u32[]{:S(2)}, u32[]{:S(2)}) collective-permute-start(bf16[64,128]{1,0:T(8,128)(2,1)S(1)} %get-tuple-element.17), channel_id=1, source_target_pairs={{12,0},{60,1},{13,8},{61,9},{20,16},{36,17},{21,24},{37,25},{28,32... | collective-permute-start | bytes 49160 | tf_op jit(solution)/shard_map/ppermute | solution.py:413
  43.5 16.4 %all-to-all-start.2 = ((f32[8,48,128]{2,1,0:T(8,128)}), f32[8,48,128]{2,1,0:T(8,128)S(1)}, u32[]{:S(2)}, u32[]{:S(2)}) async-start(f32[8,48,128]{2,1,0:T(8,128)} %get-tuple-element.18), calls=%async_computation.2 | async-start | bytes 393216 | tf_op jit(solution)/shard_map/all_to_all | solution.py:385
  48.4 11.6 %collective-permute-start.4 = (f32[32,128]{1,0:T(8,128)S(1)}, f32[32,128]{1,0:T(8,128)S(1)}, u32[]{:S(2)}, u32[]{:S(2)}) collective-permute-start(f32[32,128]{1,0:T(8,128)S(1)} %get-tuple-element.19), channel_id=1, source_target_pairs={{0,12},{1,60},{8,13},{9,61},{16,20},{17,36},{24,21},{25,37},{32,28... | collective-permute-start | bytes 49160 | tf_op jit(solution)/shard_map/ppermute | solution.py:416
  60.7 9.9 %all-to-all-start.3 = ((f32[8,64,128]{2,1,0:T(8,128)}), f32[8,64,128]{2,1,0:T(8,128)S(1)}, u32[]{:S(2)}, u32[]{:S(2)}) async-start(f32[8,64,128]{2,1,0:T(8,128)} %get-tuple-element.21), calls=%async_computation.3 | async-start | bytes 524288 | tf_op jit(solution)/shard_map/all_to_all | solution.py:385
  64.5 10.4 %collective-permute-start.7 = (f32[8,32,128]{2,1,0:T(8,128)S(1)}, f32[8,32,128]{2,1,0:T(8,128)S(1)}, u32[]{:S(2)}, u32[]{:S(2)}) collective-permute-start(f32[8,32,128]{2,1,0:T(8,128)S(1)} %get-tuple-element.20.line_refs_0_), channel_id=1, source_target_pairs={{0,64},{8,72},{16,80},{24,88},{32,96},{40,104},{48,112},{56,120},{... | collective-permute-start | bytes 393224 | tf_op jit(solution)/shard_map/ppermute | solution.py:397
  66.4 11.1 %collective-permute-start.6 = (f32[8,32,128]{2,1,0:T(8,128)S(1)}, f32[8,32,128]{2,1,0:T(8,128)S(1)}, u32[]{:S(2)}, u32[]{:S(2)}) collective-permute-start(f32[8,32,128]{2,1,0:T(8,128)S(1)} %get-tuple-element.20.line_refs_0_), channel_id=1, source_target_pairs={{0,128},{8,136},{16,144},{24,152},{32,160},{40,168},{48,176},{56,1... | collective-permute-start | bytes 393224 | tf_op jit(solution)/shard_map/ppermute | solution.py:397
  68.8 8.8 %collective-permute-start.5 = (f32[8,32,128]{2,1,0:T(8,128)S(1)}, f32[8,32,128]{2,1,0:T(8,128)S(1)}, u32[]{:S(2)}, u32[]{:S(2)}) collective-permute-start(f32[8,32,128]{2,1,0:T(8,128)S(1)} %get-tuple-element.20.line_refs_0_), channel_id=1, source_target_pairs={{0,192},{8,200},{16,208},{24,216},{32,224},{40,232},{48,240},{56,2... | collective-permute-start | bytes 393224 | tf_op jit(solution)/shard_map/ppermute | solution.py:397
  70.6 7.0 %collective-permute-start.10 = (f32[32,128]{1,0:T(8,128)S(1)}, f32[32,128]{1,0:T(8,128)S(1)}, u32[]{:S(2)}, u32[]{:S(2)}) collective-permute-start(f32[32,128]{1,0:T(8,128)S(1)} %gather.1.gram_refs_0_), channel_id=1, source_target_pairs={{0,64},{8,72},{16,80},{24,88},{32,96},{40,104},{48,112},{56,120},{... | collective-permute-start | bytes 49160 | tf_op jit(solution)/shard_map/ppermute | solution.py:397
  72.6 5.2 %collective-permute-start.9 = (f32[32,128]{1,0:T(8,128)S(1)}, f32[32,128]{1,0:T(8,128)S(1)}, u32[]{:S(2)}, u32[]{:S(2)}) collective-permute-start(f32[32,128]{1,0:T(8,128)S(1)} %gather.1.gram_refs_0_), channel_id=1, source_target_pairs={{0,128},{8,136},{16,144},{24,152},{32,160},{40,168},{48,176},{56,1... | collective-permute-start | bytes 49160 | tf_op jit(solution)/shard_map/ppermute | solution.py:397
  74.9 3.7 %collective-permute-start.8 = (f32[32,128]{1,0:T(8,128)S(1)}, f32[32,128]{1,0:T(8,128)S(1)}, u32[]{:S(2)}, u32[]{:S(2)}) collective-permute-start(f32[32,128]{1,0:T(8,128)S(1)} %gather.1.gram_refs_0_), channel_id=1, source_target_pairs={{0,192},{8,200},{16,208},{24,216},{32,224},{40,232},{48,240},{56,2... | collective-permute-start | bytes 49160 | tf_op jit(solution)/shard_map/ppermute | solution.py:397

commit v9 on v7

--- a/solution.py
+++ b/solution.py
@@ -202,8 +202,22 @@
     )(parts, jac)
 
 
-def spread_kernel(parts_ref, natural_ref, line_ref, out_ref):
-    line_ref[...] = parts_ref[:, :32]
+def line_kernel(parts_ref, out_ref):
+    out_ref[...] = parts_ref[:, :32]
+
+
+def line_of(parts):
+    return pl.pallas_call(
+        line_kernel,
+        in_specs=[VMEM],
+        out_specs=VMEM,
+        out_shape=jax.ShapeDtypeStruct((8, 32, 128), f32),
+        compiler_params=params(4),
+        name="line",
+    )(parts)
+
+
+def spread_kernel(parts_ref, natural_ref, out_ref):
     out_ref[:, :32] = jnp.broadcast_to(natural_ref[...][None], (8, 32, 128))
     for h in range(2):
         total = parts_ref[h, 32:]
@@ -216,11 +230,8 @@
     return pl.pallas_call(
         spread_kernel,
         in_specs=[VMEM] * 2,
-        out_specs=[VMEM] * 2,
-        out_shape=[
-            jax.ShapeDtypeStruct((8, 32, 128), f32),
-            jax.ShapeDtypeStruct((8, 64, 128), f32),
-        ],
+        out_specs=VMEM,
+        out_shape=jax.ShapeDtypeStruct((8, 64, 128), f32),
         compiler_params=params(4),
         name="spread",
     )(parts, natural)
@@ -410,7 +421,8 @@
     own, line = reduce(parts, jac_piece)
     line = exchange(line, "row", Z_LINES)
     natural = lax.ppermute(own, both, to_row_block())
-    line, rows = spread(line, natural)
+    rows = spread(line, natural)
+    line = line_of(line)
     rows = exchange(rows, "col")
     lines = along_x(line)
     held = load(covariance, AGAIN)

time: 84.4 us -> 84.2 us (level)
  no operation moved by 1% of the time
where the time goes in v9:
time: 84.2 us; the launch traced here: 83.2 us
  starting transfers between devices  47.8 us (57%)
  waiting for transfers between devices  19.9 us (24%)
  Pallas kernels  13.3 us (16%)
    all_to_all x4, starting transfers between devices, exchange(): lax.all_to_all(array, axis, 0, 0, axis_index_groups=groups, tiled=True)  22.4 us
    ppermute x9, starting transfers between devices, moved(): lax.ppermute(array, 'row', [(r, (r + 8 * turn) % 32) for r in range(32)])  15.9 us
    ppermute x1, waiting for transfers between devices, body(): natural = lax.ppermute(own, both, to_row_block())  8.94 us
    ppermute x1, starting transfers between devices, body(): jac_piece = lax.ppermute(jac_own, both, reversed_pairs(to_row_block()))  6.83 us
    ppermute x9, waiting for transfers between devices, moved(): lax.ppermute(array, 'row', [(r, (r + 8 * turn) % 32) for r in range(32)])  5.73 us
    pallas_call x1, Pallas kernels, update(): pl.pallas_call(update_kernel, in_specs=[VMEM, HBM, [VMEM] * 4, [VMEM] * 4...  5.34 us
    all_to_all x4, waiting for transfers between devices, exchange(): lax.all_to_all(array, axis, 0, 0, axis_index_groups=groups, tiled=True)  3.78 us
    pallas_call x2, Pallas kernels, load(): pl.pallas_call(load_kernel, in_specs=[HBM], out_specs=VMEM, out_shape=jax...  3.45 us
  transfers between devices with their start and end apart: 15, of which 10 were waited for; matrix products, arithmetic and copies ran while one was open for 0% of the time, Pallas kernels for 4%

profile of v9, /device:TPU:8, one launch (start us, length us, event | category | flops | bytes accessed | tf_op | source)
XLA Modules:
  0.0 83.2 jit_solution(2572978871818611548)
XLA Ops:
  0.6 0.8 pad_maximum_fusion
  1.4 0.6 broadcast_in_dim.12
  2.1 5.4 %all-to-all-start = ((bf16[8,32,128]{2,1,0:T(8,128)(2,1)}), bf16[8,32,128]{2,1,0:T(8,128)(2,1)S(1)}, u32[]{:S(2)}, u32[]{:S(2)}) async-start(bf16[8,32,128]{2,1,0:T(8,128)(2,1)} %broadcast_in_dim.12), calls=%async_computation | async-start | bytes 131072 | tf_op jit(solution)/shard_map/all_to_all | solution.py:396
  7.5 1.9 %fetch.3.early_ref = f32[3,512,512]{2,1,0:T(8,128)S(1)} custom-call(f32[512,2048]{1,0:T(8,128)} %cov_ref.7), custom_call_target="tpu_custom_call" | custom-call | tf_op jit(solution)/shard_map/fetch/pallas_call | solution.py:100
  9.4 2.3 %all-to-all-done.jac_ref = bf16[8,32,128]{2,1,0:T(8,128)(2,1)S(1)} async-done(((bf16[8,32,128]{2,1,0:T(8,128)(2,1)}), bf16[8,32,128]{2,1,0:T(8,128)(2,1)S(1)}, u32[]{:S(2)}, u32[]{:S(2)}) %all-to-all-start) | async-done | bytes 65568 | tf_op jit(solution)/shard_map/all_to_all | solution.py:396
  11.7 2.2 %product.1 = (f32[8,32,128]{2,1,0:T(8,128)S(1)}, f32[8,32,128]{2,1,0:T(8,128)S(1)}, f32[8,32,128]{2,1,0:T(8,128)S(1)}, f32[8,32,128]{2,1,0:T(8,128)S(1)}, bf16[64,128]{1,0:T(8,128)(2,1)S(1)}) custom-call(bf16[8,32,128]{2,1,0:T(8,128)(2,1)S(1)} %all-to-all-done.jac_ref, f32[3,512,512]{2,1,0:T(8,128)S(1)} %fetch.3.early_ref, f32[512,2048]{1,0:T(8,128)} %cov_ref.7), custom_call_target="tpu_custom_call" | custom-call | tf_op jit(solution)/shard_map/product/pallas_call | solution.py:146
  13.9 1.1 %collective-permute-start = (f32[8,32,128]{2,1,0:T(8,128)S(1)}, f32[8,32,128]{2,1,0:T(8,128)S(1)}, u32[]{:S(2)}, u32[]{:S(2)}) collective-permute-start(f32[8,32,128]{2,1,0:T(8,128)S(1)} %get-tuple-element.12), channel_id=1, source_target_pairs={{0,64},{8,72},{16,80},{24,88},{32,96},{40,104},{48,112},{56,120},{... | collective-permute-start | bytes 393224 | tf_op jit(solution)/shard_map/ppermute | solution.py:403
  14.9 2.7 %collective-permute-start.1 = (f32[8,32,128]{2,1,0:T(8,128)S(1)}, f32[8,32,128]{2,1,0:T(8,128)S(1)}, u32[]{:S(2)}, u32[]{:S(2)}) collective-permute-start(f32[8,32,128]{2,1,0:T(8,128)S(1)} %get-tuple-element.13), channel_id=1, source_target_pairs={{0,128},{8,136},{16,144},{24,152},{32,160},{40,168},{48,176},{56,1... | collective-permute-start | bytes 393224 | tf_op jit(solution)/shard_map/ppermute | solution.py:403
  17.6 1.4 %collective-permute-start.2 = (f32[8,32,128]{2,1,0:T(8,128)S(1)}, f32[8,32,128]{2,1,0:T(8,128)S(1)}, u32[]{:S(2)}, u32[]{:S(2)}) collective-permute-start(f32[8,32,128]{2,1,0:T(8,128)S(1)} %get-tuple-element.14), channel_id=1, source_target_pairs={{0,192},{8,200},{16,208},{24,216},{32,224},{40,232},{48,240},{56,2... | collective-permute-start | bytes 393224 | tf_op jit(solution)/shard_map/ppermute | solution.py:403
  19.1 2.0 %collective-permute-done.second_ref = f32[8,32,128]{2,1,0:T(8,128)S(1)} collective-permute-done((f32[8,32,128]{2,1,0:T(8,128)S(1)}, f32[8,32,128]{2,1,0:T(8,128)S(1)}, u32[]{:S(2)}, u32[]{:S(2)}) %collective-permute-start) | collective-permute-done | bytes 131104 | tf_op jit(solution)/shard_map/ppermute | solution.py:403
  21.1 2.5 %collective-permute-done.1.third_ref = f32[8,32,128]{2,1,0:T(8,128)S(1)} collective-permute-done((f32[8,32,128]{2,1,0:T(8,128)S(1)}, f32[8,32,128]{2,1,0:T(8,128)S(1)}, u32[]{:S(2)}, u32[]{:S(2)}) %collective-permute-start.1) | collective-permute-done | bytes 131104 | tf_op jit(solution)/shard_map/ppermute | solution.py:403
  23.7 0.7 add.1
  24.4 8.3 %all-to-all-start.1 = ((f32[8,32,128]{2,1,0:T(8,128)}), f32[8,32,128]{2,1,0:T(8,128)S(1)}, u32[]{:S(2)}, u32[]{:S(2)}) async-start(f32[8,32,128]{2,1,0:T(8,128)} %add.1), calls=%async_computation.1 | async-start | bytes 262144 | tf_op jit(solution)/shard_map/all_to_all | solution.py:396
  32.7 6.8 %collective-permute-start.3 = (bf16[64,128]{1,0:T(8,128)(2,1)S(1)}, bf16[64,128]{1,0:T(8,128)(2,1)S(1)}, u32[]{:S(2)}, u32[]{:S(2)}) collective-permute-start(bf16[64,128]{1,0:T(8,128)(2,1)S(1)} %get-tuple-element.15), channel_id=1, source_target_pairs={{12,0},{60,1},{13,8},{61,9},{20,16},{36,17},{21,24},{37,25},{28,32... | collective-permute-start | bytes 49160 | tf_op jit(solution)/shard_map/ppermute | solution.py:420
  39.6 1.4 %collective-permute-done.3.jac_ref = bf16[64,128]{1,0:T(8,128)(2,1)S(1)} collective-permute-done((bf16[64,128]{1,0:T(8,128)(2,1)S(1)}, bf16[64,128]{1,0:T(8,128)(2,1)S(1)}, u32[]{:S(2)}, u32[]{:S(2)}) %collective-permute-start.3) | collective-permute-done | bytes 16416 | tf_op jit(solution)/shard_map/ppermute | solution.py:420
  41.0 0.8 all-to-all-done.1.parts_ref
  41.8 0.9 %reduce.1 = (f32[32,128]{1,0:T(8,128)S(1)}, f32[8,48,128]{2,1,0:T(8,128)}) custom-call(f32[8,32,128]{2,1,0:T(8,128)S(1)} %all-to-all-done.1.parts_ref, bf16[64,128]{1,0:T(8,128)(2,1)S(1)} %collective-permute-done.3.jac_ref), custom_call_target="tpu_custom_call" | custom-call | tf_op jit(solution)/shard_map/reduce/pallas_call | solution.py:192
  42.7 4.9 %all-to-all-start.2 = ((f32[8,48,128]{2,1,0:T(8,128)}), f32[8,48,128]{2,1,0:T(8,128)S(1)}, u32[]{:S(2)}, u32[]{:S(2)}) async-start(f32[8,48,128]{2,1,0:T(8,128)} %get-tuple-element.16), calls=%async_computation.2 | async-start | bytes 393216 | tf_op jit(solution)/shard_map/all_to_all | solution.py:396
  47.6 2.6 %collective-permute-start.7 = (f32[32,128]{1,0:T(8,128)S(1)}, f32[32,128]{1,0:T(8,128)S(1)}, u32[]{:S(2)}, u32[]{:S(2)}) collective-permute-start(f32[32,128]{1,0:T(8,128)S(1)} %get-tuple-element.17), channel_id=1, source_target_pairs={{0,12},{1,60},{8,13},{9,61},{16,20},{17,36},{24,21},{25,37},{32,28... | collective-permute-start | bytes 49160 | tf_op jit(solution)/shard_map/ppermute | solution.py:423
  50.2 8.9 %collective-permute-done.7.natural_ref = f32[32,128]{1,0:T(8,128)S(1)} collective-permute-done((f32[32,128]{1,0:T(8,128)S(1)}, f32[32,128]{1,0:T(8,128)S(1)}, u32[]{:S(2)}, u32[]{:S(2)}) %collective-permute-start.7) | collective-permute-done | bytes 16416 | tf_op jit(solution)/shard_map/ppermute | solution.py:423
  59.1 0.7 spread.1
  59.8 3.8 %all-to-all-start.3 = ((f32[8,64,128]{2,1,0:T(8,128)}), f32[8,64,128]{2,1,0:T(8,128)S(1)}, u32[]{:S(2)}, u32[]{:S(2)}) async-start(f32[8,64,128]{2,1,0:T(8,128)} %spread.1), calls=%async_computation.3 | async-start | bytes 524288 | tf_op jit(solution)/shard_map/all_to_all | solution.py:396
  63.7 2.0 %collective-permute-start.6 = (f32[8,32,128]{2,1,0:T(8,128)S(1)}, f32[8,32,128]{2,1,0:T(8,128)S(1)}, u32[]{:S(2)}, u32[]{:S(2)}) collective-permute-start(f32[8,32,128]{2,1,0:T(8,128)S(1)} %line.1.line_refs_0_), channel_id=1, source_target_pairs={{0,64},{8,72},{16,80},{24,88},{32,96},{40,104},{48,112},{56,120},{... | collective-permute-start | bytes 393224 | tf_op jit(solution)/shard_map/ppermute | solution.py:403
  65.7 2.3 %collective-permute-start.5 = (f32[8,32,128]{2,1,0:T(8,128)S(1)}, f32[8,32,128]{2,1,0:T(8,128)S(1)}, u32[]{:S(2)}, u32[]{:S(2)}) collective-permute-start(f32[8,32,128]{2,1,0:T(8,128)S(1)} %line.1.line_refs_0_), channel_id=1, source_target_pairs={{0,128},{8,136},{16,144},{24,152},{32,160},{40,168},{48,176},{56,1... | collective-permute-start | bytes 393224 | tf_op jit(solution)/shard_map/ppermute | solution.py:403
  68.0 1.0 %collective-permute-start.4 = (f32[8,32,128]{2,1,0:T(8,128)S(1)}, f32[8,32,128]{2,1,0:T(8,128)S(1)}, u32[]{:S(2)}, u32[]{:S(2)}) collective-permute-start(f32[8,32,128]{2,1,0:T(8,128)S(1)} %line.1.line_refs_0_), channel_id=1, source_target_pairs={{0,192},{8,200},{16,208},{24,216},{32,224},{40,232},{48,240},{56,2... | collective-permute-start | bytes 393224 | tf_op jit(solution)/shard_map/ppermute | solution.py:403
  69.0 0.7 all-to-all-done.3.rows_ref
  69.7 2.0 %collective-permute-start.10 = (f32[32,128]{1,0:T(8,128)S(1)}, f32[32,128]{1,0:T(8,128)S(1)}, u32[]{:S(2)}, u32[]{:S(2)}) collective-permute-start(f32[32,128]{1,0:T(8,128)S(1)} %gather.1.gram_refs_0_), channel_id=1, source_target_pairs={{0,64},{8,72},{16,80},{24,88},{32,96},{40,104},{48,112},{56,120},{... | collective-permute-start | bytes 49160 | tf_op jit(solution)/shard_map/ppermute | solution.py:403
  71.7 2.3 %collective-permute-start.9 = (f32[32,128]{1,0:T(8,128)S(1)}, f32[32,128]{1,0:T(8,128)S(1)}, u32[]{:S(2)}, u32[]{:S(2)}) collective-permute-start(f32[32,128]{1,0:T(8,128)S(1)} %gather.1.gram_refs_0_), channel_id=1, source_target_pairs={{0,128},{8,136},{16,144},{24,152},{32,160},{40,168},{48,176},{56,1... | collective-permute-start | bytes 49160 | tf_op jit(solution)/shard_map/ppermute | solution.py:403
  74.1 1.0 %collective-permute-start.8 = (f32[32,128]{1,0:T(8,128)S(1)}, f32[32,128]{1,0:T(8,128)S(1)}, u32[]{:S(2)}, u32[]{:S(2)}) collective-permute-start(f32[32,128]{1,0:T(8,128)S(1)} %gather.1.gram_refs_0_), channel_id=1, source_target_pairs={{0,192},{8,200},{16,208},{24,216},{32,224},{40,232},{48,240},{56,2... | collective-permute-start | bytes 49160 | tf_op jit(solution)/shard_map/ppermute | solution.py:403
  75.1 1.6 %fetch.2.early_ref = f32[2,512,512]{2,1,0:T(8,128)S(1)} custom-call(f32[512,2048]{1,0:T(8,128)} %cov_ref.7), custom_call_target="tpu_custom_call" | custom-call | tf_op jit(solution)/shard_map/fetch/pallas_call | solution.py:100
  77.0 0.8 collective-permute-done.8.gram_refs_1_
  77.8 5.3 %update.1 = (f32[512,2048]{1,0:T(8,128)}, f32[1,64]{1,0:T(1,128)}) custom-call(f32[2,512,512]{2,1,0:T(8,128)S(1)} %fetch.2.early_ref, f32[512,2048]{1,0:T(8,128)} %cov_ref.7, f32[8,32,128]{2,1,0:T(8,128)S(1)} %line.1.line_refs_0_, f32[8,32,128]{2,1,0:T(8,128)S(1)} %collective-permute-done.4.line_refs_1_, ...), custom_call_target="tpu_custom_call" | custom-call | tf_op jit(solution)/shard_map/update/pallas_call | solution.py:376
  (13 shorter events, 0.5 us)
Async XLA Ops:
  2.1 9.6 %all-to-all-start = ((bf16[8,32,128]{2,1,0:T(8,128)(2,1)}), bf16[8,32,128]{2,1,0:T(8,128)(2,1)S(1)}, u32[]{:S(2)}, u32[]{:S(2)}) async-start(bf16[8,32,128]{2,1,0:T(8,128)(2,1)} %broadcast_in_dim.12), calls=%async_computation | async-start | bytes 131072 | tf_op jit(solution)/shard_map/all_to_all | solution.py:396
  13.9 7.2 %collective-permute-start = (f32[8,32,128]{2,1,0:T(8,128)S(1)}, f32[8,32,128]{2,1,0:T(8,128)S(1)}, u32[]{:S(2)}, u32[]{:S(2)}) collective-permute-start(f32[8,32,128]{2,1,0:T(8,128)S(1)} %get-tuple-element.12), channel_id=1, source_target_pairs={{0,64},{8,72},{16,80},{24,88},{32,96},{40,104},{48,112},{56,120},{... | collective-permute-start | bytes 393224 | tf_op jit(solution)/shard_map/ppermute | solution.py:403
  14.9 8.6 %collective-permute-start.1 = (f32[8,32,128]{2,1,0:T(8,128)S(1)}, f32[8,32,128]{2,1,0:T(8,128)S(1)}, u32[]{:S(2)}, u32[]{:S(2)}) collective-permute-start(f32[8,32,128]{2,1,0:T(8,128)S(1)} %get-tuple-element.13), channel_id=1, source_target_pairs={{0,128},{8,136},{16,144},{24,152},{32,160},{40,168},{48,176},{56,1... | collective-permute-start | bytes 393224 | tf_op jit(solution)/shard_map/ppermute | solution.py:403
  17.6 6.0 %collective-permute-start.2 = (f32[8,32,128]{2,1,0:T(8,128)S(1)}, f32[8,32,128]{2,1,0:T(8,128)S(1)}, u32[]{:S(2)}, u32[]{:S(2)}) collective-permute-start(f32[8,32,128]{2,1,0:T(8,128)S(1)} %get-tuple-element.14), channel_id=1, source_target_pairs={{0,192},{8,200},{16,208},{24,216},{32,224},{40,232},{48,240},{56,2... | collective-permute-start | bytes 393224 | tf_op jit(solution)/shard_map/ppermute | solution.py:403
  24.4 17.4 %all-to-all-start.1 = ((f32[8,32,128]{2,1,0:T(8,128)}), f32[8,32,128]{2,1,0:T(8,128)S(1)}, u32[]{:S(2)}, u32[]{:S(2)}) async-start(f32[8,32,128]{2,1,0:T(8,128)} %add.1), calls=%async_computation.1 | async-start | bytes 262144 | tf_op jit(solution)/shard_map/all_to_all | solution.py:396
  32.7 45.1 %copy-start = (f32[32]{0:T(128)S(1)}, f32[32]{0:T(128)}, u32[]{:S(2)}) copy-start(f32[32]{0:T(128)} %param.8) | copy-start | bytes 388
  32.7 45.1 %copy-start.1 = (f32[32]{0:T(128)S(1)}, f32[32]{0:T(128)}, u32[]{:S(2)}) copy-start(f32[32]{0:T(128)} %param.9) | copy-start | bytes 388
  32.7 8.3 %collective-permute-start.3 = (bf16[64,128]{1,0:T(8,128)(2,1)S(1)}, bf16[64,128]{1,0:T(8,128)(2,1)S(1)}, u32[]{:S(2)}, u32[]{:S(2)}) collective-permute-start(bf16[64,128]{1,0:T(8,128)(2,1)S(1)} %get-tuple-element.15), channel_id=1, source_target_pairs={{12,0},{60,1},{13,8},{61,9},{20,16},{36,17},{21,24},{37,25},{28,32... | collective-permute-start | bytes 49160 | tf_op jit(solution)/shard_map/ppermute | solution.py:420
  42.7 16.4 %all-to-all-start.2 = ((f32[8,48,128]{2,1,0:T(8,128)}), f32[8,48,128]{2,1,0:T(8,128)S(1)}, u32[]{:S(2)}, u32[]{:S(2)}) async-start(f32[8,48,128]{2,1,0:T(8,128)} %get-tuple-element.16), calls=%async_computation.2 | async-start | bytes 393216 | tf_op jit(solution)/shard_map/all_to_all | solution.py:396
  47.6 11.6 %collective-permute-start.7 = (f32[32,128]{1,0:T(8,128)S(1)}, f32[32,128]{1,0:T(8,128)S(1)}, u32[]{:S(2)}, u32[]{:S(2)}) collective-permute-start(f32[32,128]{1,0:T(8,128)S(1)} %get-tuple-element.17), channel_id=1, source_target_pairs={{0,12},{1,60},{8,13},{9,61},{16,20},{17,36},{24,21},{25,37},{32,28... | collective-permute-start | bytes 49160 | tf_op jit(solution)/shard_map/ppermute | solution.py:423
  59.8 9.9 %all-to-all-start.3 = ((f32[8,64,128]{2,1,0:T(8,128)}), f32[8,64,128]{2,1,0:T(8,128)S(1)}, u32[]{:S(2)}, u32[]{:S(2)}) async-start(f32[8,64,128]{2,1,0:T(8,128)} %spread.1), calls=%async_computation.3 | async-start | bytes 524288 | tf_op jit(solution)/shard_map/all_to_all | solution.py:396
  63.7 10.4 %collective-permute-start.6 = (f32[8,32,128]{2,1,0:T(8,128)S(1)}, f32[8,32,128]{2,1,0:T(8,128)S(1)}, u32[]{:S(2)}, u32[]{:S(2)}) collective-permute-start(f32[8,32,128]{2,1,0:T(8,128)S(1)} %line.1.line_refs_0_), channel_id=1, source_target_pairs={{0,64},{8,72},{16,80},{24,88},{32,96},{40,104},{48,112},{56,120},{... | collective-permute-start | bytes 393224 | tf_op jit(solution)/shard_map/ppermute | solution.py:403
  65.7 11.0 %collective-permute-start.5 = (f32[8,32,128]{2,1,0:T(8,128)S(1)}, f32[8,32,128]{2,1,0:T(8,128)S(1)}, u32[]{:S(2)}, u32[]{:S(2)}) collective-permute-start(f32[8,32,128]{2,1,0:T(8,128)S(1)} %line.1.line_refs_0_), channel_id=1, source_target_pairs={{0,128},{8,136},{16,144},{24,152},{32,160},{40,168},{48,176},{56,1... | collective-permute-start | bytes 393224 | tf_op jit(solution)/shard_map/ppermute | solution.py:403
  68.0 8.7 %collective-permute-start.4 = (f32[8,32,128]{2,1,0:T(8,128)S(1)}, f32[8,32,128]{2,1,0:T(8,128)S(1)}, u32[]{:S(2)}, u32[]{:S(2)}) collective-permute-start(f32[8,32,128]{2,1,0:T(8,128)S(1)} %line.1.line_refs_0_), channel_id=1, source_target_pairs={{0,192},{8,200},{16,208},{24,216},{32,224},{40,232},{48,240},{56,2... | collective-permute-start | bytes 393224 | tf_op jit(solution)/shard_map/ppermute | solution.py:403
  69.7 7.0 %collective-permute-start.10 = (f32[32,128]{1,0:T(8,128)S(1)}, f32[32,128]{1,0:T(8,128)S(1)}, u32[]{:S(2)}, u32[]{:S(2)}) collective-permute-start(f32[32,128]{1,0:T(8,128)S(1)} %gather.1.gram_refs_0_), channel_id=1, source_target_pairs={{0,64},{8,72},{16,80},{24,88},{32,96},{40,104},{48,112},{56,120},{... | collective-permute-start | bytes 49160 | tf_op jit(solution)/shard_map/ppermute | solution.py:403
  71.7 5.2 %collective-permute-start.9 = (f32[32,128]{1,0:T(8,128)S(1)}, f32[32,128]{1,0:T(8,128)S(1)}, u32[]{:S(2)}, u32[]{:S(2)}) collective-permute-start(f32[32,128]{1,0:T(8,128)S(1)} %gather.1.gram_refs_0_), channel_id=1, source_target_pairs={{0,128},{8,136},{16,144},{24,152},{32,160},{40,168},{48,176},{56,1... | collective-permute-start | bytes 49160 | tf_op jit(solution)/shard_map/ppermute | solution.py:403
  74.1 3.7 %collective-permute-start.8 = (f32[32,128]{1,0:T(8,128)S(1)}, f32[32,128]{1,0:T(8,128)S(1)}, u32[]{:S(2)}, u32[]{:S(2)}) collective-permute-start(f32[32,128]{1,0:T(8,128)S(1)} %gather.1.gram_refs_0_), channel_id=1, source_target_pairs={{0,192},{8,200},{16,208},{24,216},{32,224},{40,232},{48,240},{56,2... | collective-permute-start | bytes 49160 | tf_op jit(solution)/shard_map/ppermute | solution.py:403
